TPU v7x, 256 devices: a whole 4x4x8 slice. The times are simulated.
256 devices in a mesh: frames: 16 (over y_lo, x, core), rows: 16 (over y_hi, z).
Axes of the slice: x: 4, y: 4 (y_hi: 2, y_lo: 2; y = y_hi * 2 + y_lo), z: 8, core: 2. Of those that a mesh axis runs over, the one named last changes fastest.
Arguments:
- video: bfloat16 [16, 64, 320, 192], P('frames', 'rows'), may hold values from -6 to 6
- spatial_weights: bfloat16 [4, 3, 3, 192, 192], replicated, may hold values from -0.15625 to 0.15625
- norm_gains: float32 [4, 192], replicated, may hold values from 0.5 to 1.5
- temporal_weights: bfloat16 [2, 3, 192, 192], replicated, may hold values from -0.25 to 0.25
Outputs:
- decoded: bfloat16 [16, 64, 320, 192], P('frames', 'rows')
All inputs are finite; a program needn't handle non-finite values.
Results may differ from a plain program's by a relative error of at most 0.013.
Values may be sent and summed in bfloat16 or wider, within the bound.
No kernel may reach another device: no remote copies, remote signals or barrier semaphores. Data moves between devices by JAX's collectives and lax.ppermute only.
A program may use at most 64 MiB of HBM per device.

v0:
```python
import jax
import jax.numpy as jnp
from jax import lax
from jax.sharding import PartitionSpec as P

epsilon = 1e-06


def shifted(block, axis, distance):
    devices = range(lax.axis_size(axis))
    route = [(i - distance, i) for i in devices if i - distance in devices]
    return lax.ppermute(block, axis, route)


def extended_2(cells, sides, width):
    for axis, dim in sides:
        count = lax.axis_size(axis)
        ends = count - 1
        head = lax.slice_in_dim(cells, 0, width, axis=dim)
        tail = lax.slice_in_dim(cells, cells.shape[dim] - width, cells.shape[dim], axis=dim)
        cells = jnp.concatenate(
            [
                lax.ppermute(tail, axis, [(i, (i + 1) % count) for i in range(ends)]),
                cells,
                lax.ppermute(head, axis, [((i + 1) % count, i) for i in range(ends)]),
            ],
            axis=dim,
        )
    return cells


def activate(values, gain):
    values = values.astype(jnp.float32)
    mean_sq = jnp.mean(values * values, axis=-1, keepdims=True)
    scaled = values * lax.rsqrt(mean_sq + epsilon) * gain
    return jax.nn.silu(scaled).astype(jnp.bfloat16)


def convolve(active, kernel):
    out_rows = active.shape[1] - 2
    width = active.shape[2]
    padded = jnp.pad(active, ((0, 0), (0, 0), (1, 1), (0, 0)))
    total = None
    for row_step in range(3):
        for col_step in range(3):
            window = padded[:, row_step : row_step + out_rows, col_step : col_step + width]
            term = jnp.einsum(
                "frwc,cd->frwd",
                window,
                kernel[row_step, col_step],
                preferred_element_type=jnp.float32,
            )
            total = term if total is None else total + term
    return total


def past_frames(inner):
    frame_count = inner.shape[0]
    hops = (frame_count + 1) // frame_count
    pieces = []
    for offset in range(1, hops + 1):
        pieces.append(shifted(inner, "frames", offset))
    joined = jnp.concatenate(pieces[::-1], axis=0)
    return joined


def on_device(video, spatial_weights, norm_gains, temporal_weights):
    current = video
    frame_count = video.shape[0]
    rows_dev = video.shape[1]
    first_row = lax.axis_index("rows") * rows_dev
    all_rows = rows_dev * lax.axis_size("rows")
    for block in range(spatial_weights.shape[0] // 2):
        widened = extended_2(current, (("rows", 1),), 2)
        first = convolve(activate(widened, norm_gains[2 * block]), spatial_weights[2 * block])
        row_index = first_row - 1 + jnp.arange(rows_dev + 2, dtype=jnp.int32)
        inside = (row_index >= 0) & (row_index < all_rows)
        first = jnp.where(inside[None, :, None, None], first, 0.0).astype(jnp.bfloat16)
        second = convolve(
            activate(first, norm_gains[2 * block + 1]), spatial_weights[2 * block + 1]
        )
        inner = (current.astype(jnp.float32) + second).astype(jnp.bfloat16)
        history = past_frames(inner)
        extended = jnp.concatenate([history, inner], axis=0)
        total = inner.astype(jnp.float32)
        for offset in range(3):
            frames_in = extended[2 - offset : 2 - offset + frame_count]
            total = total + jnp.einsum(
                "frwc,cd->frwd",
                frames_in,
                temporal_weights[block, offset],
                preferred_element_type=jnp.float32,
            )
        current = total.astype(jnp.bfloat16)
    return current


def solution(mesh):
    placed = (P("frames", "rows", None, None), P(), P(), P())
    return jax.shard_map(
        on_device,
        mesh=mesh,
        in_specs=placed,
        out_specs=P("frames", "rows", None, None),
        check_vma=False,
    )
```

profile of v0, /device:TPU:25, one launch (start us, length us, event | category | flops | bytes accessed | tf_op | source)
XLA Modules:
  0.0 104.8 jit_solution(11397811055797997091)
XLA Ops:
  0.0 1.9 %fusion.182 = (bf16[1,2,320,192]{2,3,1,0:T(8,128)(2,1)}, bf16[1,2,320,192]{2,3,1,0:T(8,128)(2,1)}) fusion(bf16[1,4,320,192]{2,3,1,0:T(8,128)(2,1)} %param.4), kind=kLoop, calls=%fused_computation.268 | loop fusion | bytes 983040 | tf_op jit(solution)/shard_map/slice | solution.py:20
  1.9 3.5 %collective-permute-start = (bf16[1,2,320,192]{2,3,1,0:T(8,128)(2,1)}, bf16[1,2,320,192]{2,3,1,0:T(8,128)(2,1)S(1)}, u32[]{:S(2)}, u32[]{:S(2)}) collective-permute-start(bf16[1,2,320,192]{2,3,1,0:T(8,128)(2,1)} %get-tuple-element.11), channel_id=1, source_target_pairs={{0,1},{1,2},{2,3},{3,4},{4,5},{5,6},{6,7},{7,8},{8,9},{9,10},{10,1... | collective-permute-start | bytes 737288 | tf_op jit(solution)/shard_map/ppermute | solution.py:23
  5.5 6.5 %collective-permute-start.1 = (bf16[1,2,320,192]{2,3,1,0:T(8,128)(2,1)}, bf16[1,2,320,192]{2,3,1,0:T(8,128)(2,1)}, u32[]{:S(2)}, u32[]{:S(2)}) collective-permute-start(bf16[1,2,320,192]{2,3,1,0:T(8,128)(2,1)} %get-tuple-element.12), channel_id=1, source_target_pairs={{1,0},{2,1},{3,2},{4,3},{5,4},{6,5},{7,6},{8,7},{9,8},{10,9},{11,1... | collective-permute-start | bytes 737288 | tf_op jit(solution)/shard_map/ppermute | solution.py:25
  12.0 3.6 %fusion.180 = (bf16[1,3,3,192,192]{4,3,2,1,0:T(8,128)(2,1)}, bf16[1,3,3,192,192]{4,3,2,1,0:T(8,128)(2,1)S(1)}, bf16[1,3,3,192,192]{4,3,2,1,0:T(8,128)(2,1)}, bf16[1,3,3,192,192]{4,3,2,1,0:T(8,128)(2,1)S(1)}) fusion(bf16[4,3,3,192,192]{4,3,2,1,0:T(8,128)(2,1)} %param.5), kind=kLoop, calls=%fused_computation.266 | loop fusion | bytes 5308416 | tf_op jit(solution)/shard_map/slice | solution.py:80
  15.6 0.8 copy.16
  16.3 1.7 %copy.15 = bf16[1,3,3,192,192]{3,4,2,1,0:T(8,128)(2,1)S(1)} copy(bf16[1,3,3,192,192]{4,3,2,1,0:T(8,128)(2,1)} %get-tuple-element.7) | data formatting | bytes 1327104
  18.1 1.3 %fusion = f32[8,320]{1,0:T(8,128)S(1)} fusion(bf16[1,2,320,192]{2,3,1,0:T(8,128)(2,1)} %collective-permute-done.1, bf16[1,4,320,192]{2,3,1,0:T(8,128)(2,1)S(1)} %copy-done, bf16[1,2,320,192]{2,3,1,0:T(8,128)(2,1)S(1)} %collective-permute-done), kind=kLoop, calls=%fused_computation.4 | loop fusion | flops 2455040 | bytes 993280 | tf_op jit(solution)/shard_map/reduce_sum | solution.py:34
  19.4 1.8 %fusion.7 = bf16[1,8,320,192]{2,3,1,0:T(8,128)(2,1)S(1)} fusion(f32[192]{0:T(256)S(1)} %bitcast.441, f32[8,320]{1,0:T(8,128)S(1)} %add_rsqrt_fusion.3, bf16[1,2,320,192]{2,3,1,0:T(8,128)(2,1)} %collective-permute-done.1, bf16[1,4,320,192]{2,3,1,0:T(8,128)(2,1)S(1)} %copy-done, bf16[1,2,320,192]{2,3,1,0:T(8,128)(2,1)S(1)} %collective-permute-done), kind=kLoop, calls=%fused_computation.11 | loop fusion | flops 4915200 | bytes 1977088 | tf_op jit(solution)/shard_map/convert_element_type | solution.py:36
  21.6 0.5 fusion.64
  22.1 0.5 fusion.66
  23.0 0.5 fusion.68
  23.5 0.5 fusion.70
  24.4 0.5 fusion.72
  24.9 1.2 %fusion.16 = (f32[6,320]{1,0:T(8,128)S(1)}, bf16[6,320,192]{1,2,0:T(8,128)(2,1)S(1)}) fusion(bf16[1,8,320,192]{2,3,1,0:T(8,128)(2,1)S(1)} %fusion.7, bf16[3,3,192,192]{2,3,1,0:T(8,128)(2,1)S(1)} %bitcast.410, f32[6,320,192]{1,2,0:T(8,128)S(1)} %fusion.49, f32[6,320,192]{1,2,0:T(8,128)S(1)} %fusion.64, f32[6,320,192]{1,2,0:T(8,128)S(1)} %fusion.66, ...), kind=kOutput, calls=%fused_computation.24 | convolution fusion | flops 146348160 | bytes 16179200 | tf_op jit(solution)/shard_map/frwc,cd->frwd/dot_general | solution.py:47
  26.1 0.6 fusion.45
  26.8 0.4 fusion.106
  27.5 0.4 convolution_add_fusion.14
  27.9 0.4 convolution_add_fusion.13
  29.1 0.4 convolution_add_fusion.10
  29.8 0.4 fusion.41
  30.3 3.1 %collective-permute-start.3 = (bf16[1,4,320,192]{2,3,1,0:T(8,128)(2,1)S(1)}, bf16[1,4,320,192]{2,3,1,0:T(8,128)(2,1)S(1)}, u32[]{:S(2)}, u32[]{:S(2)}) collective-permute-start(bf16[1,4,320,192]{2,3,1,0:T(8,128)(2,1)S(1)} %fusion.41), channel_id=1, source_target_pairs={{0,32},{16,48},{32,64},{48,80},{64,96},{80,112},{96,128},{112,144}... | collective-permute-start | bytes 1474568 | tf_op jit(solution)/shard_map/ppermute | solution.py:12
  33.4 4.7 %collective-permute-start.2 = (bf16[1,4,320,192]{2,3,1,0:T(8,128)(2,1)S(1)}, bf16[1,4,320,192]{2,3,1,0:T(8,128)(2,1)S(1)}, u32[]{:S(2)}, u32[]{:S(2)}) collective-permute-start(bf16[1,4,320,192]{2,3,1,0:T(8,128)(2,1)S(1)} %fusion.41), channel_id=1, source_target_pairs={{0,16},{16,32},{32,48},{48,64},{64,80},{80,96},{96,112},{112,128},... | collective-permute-start | bytes 1474568 | tf_op jit(solution)/shard_map/ppermute | solution.py:12
  38.5 9.2 %collective-permute-done.3 = bf16[1,4,320,192]{2,3,1,0:T(8,128)(2,1)S(1)} collective-permute-done((bf16[1,4,320,192]{2,3,1,0:T(8,128)(2,1)S(1)}, bf16[1,4,320,192]{2,3,1,0:T(8,128)(2,1)S(1)}, u32[]{:S(2)}, u32[]{:S(2)}) %collective-permute-start.3) | collective-permute-done | bytes 491552 | tf_op jit(solution)/shard_map/ppermute | solution.py:12
  48.0 4.8 %collective-permute-done.2 = bf16[1,4,320,192]{2,3,1,0:T(8,128)(2,1)S(1)} collective-permute-done((bf16[1,4,320,192]{2,3,1,0:T(8,128)(2,1)S(1)}, bf16[1,4,320,192]{2,3,1,0:T(8,128)(2,1)S(1)}, u32[]{:S(2)}, u32[]{:S(2)}) %collective-permute-start.2) | collective-permute-done | bytes 491552 | tf_op jit(solution)/shard_map/ppermute | solution.py:12
  53.2 0.9 fusion.181
  54.1 1.9 %collective-permute-start.4 = (bf16[1,2,320,192]{2,3,1,0:T(8,128)(2,1)}, bf16[1,2,320,192]{2,3,1,0:T(8,128)(2,1)S(1)}, u32[]{:S(2)}, u32[]{:S(2)}) collective-permute-start(bf16[1,2,320,192]{2,3,1,0:T(8,128)(2,1)} %get-tuple-element.9), channel_id=1, source_target_pairs={{0,1},{1,2},{2,3},{3,4},{4,5},{5,6},{6,7},{7,8},{8,9},{9,10},{10,1... | collective-permute-start | bytes 737288 | tf_op jit(solution)/shard_map/ppermute | solution.py:23
  56.0 7.8 %collective-permute-start.5 = (bf16[1,2,320,192]{2,3,1,0:T(8,128)(2,1)}, bf16[1,2,320,192]{2,3,1,0:T(8,128)(2,1)}, u32[]{:S(2)}, u32[]{:S(2)}) collective-permute-start(bf16[1,2,320,192]{2,3,1,0:T(8,128)(2,1)} %get-tuple-element.10), channel_id=1, source_target_pairs={{1,0},{2,1},{3,2},{4,3},{5,4},{6,5},{7,6},{8,7},{9,8},{10,9},{11,1... | collective-permute-start | bytes 737288 | tf_op jit(solution)/shard_map/ppermute | solution.py:25
  63.8 0.8 copy.20
  64.6 0.8 copy.21
  65.4 0.7 collective-permute-done.4
  66.0 1.6 %collective-permute-done.5 = bf16[1,2,320,192]{2,3,1,0:T(8,128)(2,1)} collective-permute-done((bf16[1,2,320,192]{2,3,1,0:T(8,128)(2,1)}, bf16[1,2,320,192]{2,3,1,0:T(8,128)(2,1)}, u32[]{:S(2)}, u32[]{:S(2)}) %collective-permute-start.5) | collective-permute-done | bytes 245792 | tf_op jit(solution)/shard_map/ppermute | solution.py:25
  67.6 1.3 %fusion.8 = f32[8,320]{1,0:T(8,128)S(1)} fusion(bf16[1,2,320,192]{2,3,1,0:T(8,128)(2,1)} %collective-permute-done.5, bf16[1,4,320,192]{2,3,1,0:T(8,128)(2,1)S(1)} %fusion.43, bf16[1,2,320,192]{2,3,1,0:T(8,128)(2,1)S(1)} %collective-permute-done.4), kind=kLoop, calls=%fused_computation.12 | loop fusion | flops 2455040 | bytes 993280 | tf_op jit(solution)/shard_map/reduce_sum | solution.py:34
  68.9 1.8 %fusion.15 = bf16[1,8,320,192]{2,3,1,0:T(8,128)(2,1)S(1)} fusion(f32[192]{0:T(256)S(1)} %bitcast.439, f32[8,320]{1,0:T(8,128)S(1)} %add_rsqrt_fusion.1, bf16[1,2,320,192]{2,3,1,0:T(8,128)(2,1)} %collective-permute-done.5, bf16[1,4,320,192]{2,3,1,0:T(8,128)(2,1)S(1)} %fusion.43, bf16[1,2,320,192]{2,3,1,0:T(8,128)(2,1)S(1)} %collective-permute-done.4), kind=kLoop, calls=%fused_computation.19 | loop fusion | flops 4915200 | bytes 1977088 | tf_op jit(solution)/shard_map/convert_element_type | solution.py:36
  70.7 0.5 fusion.59
  71.2 0.5 fusion.57
  71.7 0.5 fusion.55
  72.2 0.5 fusion.53
  73.9 0.5 fusion.61
  74.5 1.2 %fusion.24 = (f32[6,320]{1,0:T(8,128)S(1)}, bf16[6,320,192]{1,2,0:T(8,128)(2,1)S(1)}) fusion(bf16[1,8,320,192]{2,3,1,0:T(8,128)(2,1)S(1)} %fusion.15, bf16[3,3,192,192]{2,3,1,0:T(8,128)(2,1)S(1)} %bitcast.419, f32[6,320,192]{1,2,0:T(8,128)S(1)} %fusion.46, f32[6,320,192]{1,2,0:T(8,128)S(1)} %fusion.53, f32[6,320,192]{1,2,0:T(8,128)S(1)} %fusion.55, ...), kind=kOutput, calls=%fused_computation.32 | convolution fusion | flops 146348160 | bytes 16179200 | tf_op jit(solution)/shard_map/frwc,cd->frwd/dot_general | solution.py:47
  75.7 0.6 fusion.44
  76.3 0.4 fusion.96
  77.0 0.4 convolution_add_fusion.6
  79.4 0.4 add_convert_fusion
  79.8 4.3 %collective-permute-start.7 = (bf16[1,4,320,192]{2,3,1,0:T(8,128)(2,1)S(1)}, bf16[1,4,320,192]{2,3,1,0:T(8,128)(2,1)S(1)}, u32[]{:S(2)}, u32[]{:S(2)}) collective-permute-start(bf16[1,4,320,192]{2,3,1,0:T(8,128)(2,1)S(1)} %add_convert_fusion), channel_id=1, source_target_pairs={{0,32},{16,48},{32,64},{48,80},{64,96},{80,112},{96,128},{112,144}... | collective-permute-start | bytes 1474568 | tf_op jit(solution)/shard_map/ppermute | solution.py:12
  84.2 5.3 %collective-permute-start.6 = (bf16[1,4,320,192]{2,3,1,0:T(8,128)(2,1)S(1)}, bf16[1,4,320,192]{2,3,1,0:T(8,128)(2,1)S(1)}, u32[]{:S(2)}, u32[]{:S(2)}) collective-permute-start(bf16[1,4,320,192]{2,3,1,0:T(8,128)(2,1)S(1)} %add_convert_fusion), channel_id=1, source_target_pairs={{0,16},{16,32},{32,48},{48,64},{64,80},{80,96},{96,112},{112,128},... | collective-permute-start | bytes 1474568 | tf_op jit(solution)/shard_map/ppermute | solution.py:12
  89.8 4.6 %collective-permute-done.7 = bf16[1,4,320,192]{2,3,1,0:T(8,128)(2,1)S(1)} collective-permute-done((bf16[1,4,320,192]{2,3,1,0:T(8,128)(2,1)S(1)}, bf16[1,4,320,192]{2,3,1,0:T(8,128)(2,1)S(1)}, u32[]{:S(2)}, u32[]{:S(2)}) %collective-permute-start.7) | collective-permute-done | bytes 491552 | tf_op jit(solution)/shard_map/ppermute | solution.py:12
  94.8 8.8 %collective-permute-done.6 = bf16[1,4,320,192]{2,3,1,0:T(8,128)(2,1)S(1)} collective-permute-done((bf16[1,4,320,192]{2,3,1,0:T(8,128)(2,1)S(1)}, bf16[1,4,320,192]{2,3,1,0:T(8,128)(2,1)S(1)}, u32[]{:S(2)}, u32[]{:S(2)}) %collective-permute-start.6) | collective-permute-done | bytes 491552 | tf_op jit(solution)/shard_map/ppermute | solution.py:12
  103.6 1.2 %fusion.42 = bf16[1,4,320,192]{2,3,1,0:T(8,128)(2,1)} fusion(f32[1,4,320,192]{2,3,1,0:T(8,128)S(1)} %convolution_bitcast_fusion, f32[1,4,320,192]{2,3,1,0:T(8,128)S(1)} %fusion.37, bf16[1,4,320,192]{2,3,1,0:T(8,128)(2,1)S(1)} %collective-permute-done.6, bf16[2,3,192,192]{3,2,1,0:T(8,128)(2,1)S(1)} %copy-done.3), kind=kOutput, calls=%fused_computation.74 | convolution fusion | flops 95109120 | bytes 3538944 | tf_op jit(solution)/shard_map/frwc,cd->frwd/dot_general | solution.py:88
  (39 shorter events, 7.6 us)
Async XLA Ops:
  1.9 16.1 %collective-permute-start = (bf16[1,2,320,192]{2,3,1,0:T(8,128)(2,1)}, bf16[1,2,320,192]{2,3,1,0:T(8,128)(2,1)S(1)}, u32[]{:S(2)}, u32[]{:S(2)}) collective-permute-start(bf16[1,2,320,192]{2,3,1,0:T(8,128)(2,1)} %get-tuple-element.11), channel_id=1, source_target_pairs={{0,1},{1,2},{2,3},{3,4},{4,5},{5,6},{6,7},{7,8},{8,9},{9,10},{10,1... | collective-permute-start | bytes 737288 | tf_op jit(solution)/shard_map/ppermute | solution.py:23
  5.5 12.6 %collective-permute-start.1 = (bf16[1,2,320,192]{2,3,1,0:T(8,128)(2,1)}, bf16[1,2,320,192]{2,3,1,0:T(8,128)(2,1)}, u32[]{:S(2)}, u32[]{:S(2)}) collective-permute-start(bf16[1,2,320,192]{2,3,1,0:T(8,128)(2,1)} %get-tuple-element.12), channel_id=1, source_target_pairs={{1,0},{2,1},{3,2},{4,3},{5,4},{6,5},{7,6},{8,7},{9,8},{10,9},{11,1... | collective-permute-start | bytes 737288 | tf_op jit(solution)/shard_map/ppermute | solution.py:25
  16.3 1.7 %copy-start.4 = (f32[4,192]{1,0:T(4,128)S(1)}, f32[4,192]{1,0:T(4,128)}, u32[]{:S(2)}) copy-start(f32[4,192]{1,0:T(4,128)} %param.6) | copy-start | bytes 9220
  16.3 1.7 %copy-start = (bf16[1,4,320,192]{2,3,1,0:T(8,128)(2,1)S(1)}, bf16[1,4,320,192]{2,3,1,0:T(8,128)(2,1)}, u32[]{:S(2)}) copy-start(bf16[1,4,320,192]{2,3,1,0:T(8,128)(2,1)} %param.4) | copy-start | bytes 1474564
  29.8 8.3 %copy-start.2 = (bf16[2,3,192,192]{3,2,1,0:T(8,128)(2,1)S(1)}, bf16[2,3,192,192]{3,2,1,0:T(8,128)(2,1)}, u32[]{:S(2)}) copy-start(bf16[2,3,192,192]{3,2,1,0:T(8,128)(2,1)} %param.7) | copy-start | bytes 1327108
  30.3 17.4 %collective-permute-start.3 = (bf16[1,4,320,192]{2,3,1,0:T(8,128)(2,1)S(1)}, bf16[1,4,320,192]{2,3,1,0:T(8,128)(2,1)S(1)}, u32[]{:S(2)}, u32[]{:S(2)}) collective-permute-start(bf16[1,4,320,192]{2,3,1,0:T(8,128)(2,1)S(1)} %fusion.41), channel_id=1, source_target_pairs={{0,32},{16,48},{32,64},{48,80},{64,96},{80,112},{96,128},{112,144}... | collective-permute-start | bytes 1474568 | tf_op jit(solution)/shard_map/ppermute | solution.py:12
  33.4 19.4 %collective-permute-start.2 = (bf16[1,4,320,192]{2,3,1,0:T(8,128)(2,1)S(1)}, bf16[1,4,320,192]{2,3,1,0:T(8,128)(2,1)S(1)}, u32[]{:S(2)}, u32[]{:S(2)}) collective-permute-start(bf16[1,4,320,192]{2,3,1,0:T(8,128)(2,1)S(1)} %fusion.41), channel_id=1, source_target_pairs={{0,16},{16,32},{32,48},{48,64},{64,80},{80,96},{96,112},{112,128},... | collective-permute-start | bytes 1474568 | tf_op jit(solution)/shard_map/ppermute | solution.py:12
  53.2 10.6 %copy-start.1 = (bf16[1,3,3,192,192]{4,3,2,1,0:T(8,128)(2,1)S(1)}, bf16[1,3,3,192,192]{4,3,2,1,0:T(8,128)(2,1)}, u32[]{:S(2)}) copy-start(bf16[1,3,3,192,192]{4,3,2,1,0:T(8,128)(2,1)} %get-tuple-element.5) | copy-start | bytes 1990660
  54.1 11.9 %collective-permute-start.4 = (bf16[1,2,320,192]{2,3,1,0:T(8,128)(2,1)}, bf16[1,2,320,192]{2,3,1,0:T(8,128)(2,1)S(1)}, u32[]{:S(2)}, u32[]{:S(2)}) collective-permute-start(bf16[1,2,320,192]{2,3,1,0:T(8,128)(2,1)} %get-tuple-element.9), channel_id=1, source_target_pairs={{0,1},{1,2},{2,3},{3,4},{4,5},{5,6},{6,7},{7,8},{8,9},{9,10},{10,1... | collective-permute-start | bytes 737288 | tf_op jit(solution)/shard_map/ppermute | solution.py:23
  56.0 11.6 %collective-permute-start.5 = (bf16[1,2,320,192]{2,3,1,0:T(8,128)(2,1)}, bf16[1,2,320,192]{2,3,1,0:T(8,128)(2,1)}, u32[]{:S(2)}, u32[]{:S(2)}) collective-permute-start(bf16[1,2,320,192]{2,3,1,0:T(8,128)(2,1)} %get-tuple-element.10), channel_id=1, source_target_pairs={{1,0},{2,1},{3,2},{4,3},{5,4},{6,5},{7,6},{8,7},{9,8},{10,9},{11,1... | collective-permute-start | bytes 737288 | tf_op jit(solution)/shard_map/ppermute | solution.py:25
  79.4 10.1 %copy-start.3 = (bf16[2,3,192,192]{3,2,1,0:T(8,128)(2,1)S(1)}, bf16[2,3,192,192]{3,2,1,0:T(8,128)(2,1)}, u32[]{:S(2)}) copy-start(bf16[2,3,192,192]{3,2,1,0:T(8,128)(2,1)} %param.7) | copy-start | bytes 1327108
  79.8 14.6 %collective-permute-start.7 = (bf16[1,4,320,192]{2,3,1,0:T(8,128)(2,1)S(1)}, bf16[1,4,320,192]{2,3,1,0:T(8,128)(2,1)S(1)}, u32[]{:S(2)}, u32[]{:S(2)}) collective-permute-start(bf16[1,4,320,192]{2,3,1,0:T(8,128)(2,1)S(1)} %add_convert_fusion), channel_id=1, source_target_pairs={{0,32},{16,48},{32,64},{48,80},{64,96},{80,112},{96,128},{112,144}... | collective-permute-start | bytes 1474568 | tf_op jit(solution)/shard_map/ppermute | solution.py:12
  84.2 19.4 %collective-permute-start.6 = (bf16[1,4,320,192]{2,3,1,0:T(8,128)(2,1)S(1)}, bf16[1,4,320,192]{2,3,1,0:T(8,128)(2,1)S(1)}, u32[]{:S(2)}, u32[]{:S(2)}) collective-permute-start(bf16[1,4,320,192]{2,3,1,0:T(8,128)(2,1)S(1)} %add_convert_fusion), channel_id=1, source_target_pairs={{0,16},{16,32},{32,48},{48,64},{64,80},{80,96},{96,112},{112,128},... | collective-permute-start | bytes 1474568 | tf_op jit(solution)/shard_map/ppermute | solution.py:12
where the time goes:
time: 107 us; the launch traced here: 105 us
  starting transfers between devices  37.3 us (35%)
  waiting for transfers between devices  29.7 us (28%)
  matrix products  19.5 us (18%)
  local copies, waits for them, and re-layouts  10.3 us (10%)
  other arithmetic  7.46 us (7%)
    ppermute x4, waiting for transfers between devices, shifted(): return lax.ppermute(block, axis, route)  27.5 us
    ppermute x4, starting transfers between devices, shifted(): return lax.ppermute(block, axis, route)  17.5 us
    dot_general x36, matrix products, convolve(): jnp.einsum('frwc,cd->frwd', window, kernel[row_step, col_step], preferred...  16.7 us
    ppermute x2, starting transfers between devices, extended_2(): lax.ppermute(head, axis, [((i + 1) % count, i) for i in range(ends)])  14.3 us
    ppermute x2, starting transfers between devices, extended_2(): lax.ppermute(tail, axis, [(i, (i + 1) % count) for i in range(ends)])  5.44 us
    convert_element_type x4, other arithmetic, activate(): return jax.nn.silu(scaled).astype(jnp.bfloat16)  4.89 us
    unnamed x14, local copies, waits for them, and re-layouts  3.96 us
    slice x1, local copies, waits for them, and re-layouts, on_device(): spatial_weights[2 * block + 1]  3.56 us
  transfers between devices with their start and end apart: 8, of which 6 were waited for; matrix products, arithmetic and copies ran while one was open for 8% of the time, Pallas kernels for 0%

commit v1 on v0

v1 whole, which is shorter than its diff:
```python
import functools

import jax
import jax.numpy as jnp
from jax import lax
from jax.experimental import pallas as pl
from jax.experimental.pallas import tpu as pltpu
from jax.sharding import PartitionSpec as P

C = 192
W = 320
PAIR = 2 * W
LANES = 128
EPS = 1e-06
F32 = jnp.float32
BF16 = jnp.bfloat16
VMEM = pl.BlockSpec(memory_space=pltpu.VMEM)
SMEM = pl.BlockSpec(memory_space=pltpu.SMEM)
LIMIT = 28 << 20


def call(kernel, outs, n_in, name, scratch=(), scalars=True, flops=0, moved=0):
    specs = ([SMEM] if scalars else []) + [VMEM] * n_in
    many = isinstance(outs, (list, tuple))
    return pl.pallas_call(
        kernel,
        out_shape=outs,
        in_specs=specs,
        out_specs=[VMEM] * len(outs) if many else VMEM,
        scratch_shapes=list(scratch),
        compiler_params=pltpu.CompilerParams(vmem_limit_bytes=LIMIT),
        cost_estimate=pl.CostEstimate(flops=flops, bytes_accessed=moved, transcendentals=0),
        name=name,
    )


def pair_shape():
    return jax.ShapeDtypeStruct((C, PAIR), BF16)


def weights_kernel(sw, g, wt, gt):
    for tap in range(9):
        wt[:, tap * C : (tap + 1) * C] = sw[tap // 3, tap % 3].T
    gt[...] = jnp.broadcast_to(g[...] * 0.5, (LANES, C)).T


def prepare(weight, gain):
    return call(
        weights_kernel,
        [jax.ShapeDtypeStruct((C, 9 * C), BF16), jax.ShapeDtypeStruct((C, LANES), F32)],
        2,
        "weights",
        scalars=False,
        moved=1500000,
    )(weight, gain.reshape(1, C))


def taps_kernel(tw, wt):
    for tap in range(3):
        wt[:, tap * C : (tap + 1) * C] = tw[tap].T


def prepare_taps(weight):
    return call(
        taps_kernel, jax.ShapeDtypeStruct((C, 3 * C), BF16), 1, "taps", scalars=False, moved=500000
    )(weight)


def pack_kernel(sc, v, own, sib):
    core = sc[0]
    for dst, pair in ((own, core), (sib, 1 - core)):
        dst[:, :W] = v[2 * pair]
        dst[:, W:] = v[2 * pair + 1]


def unpack_kernel(sc, keep, got, out):
    core = sc[0]
    for src, pair in ((keep, core), (got, 1 - core)):
        out[2 * pair] = src[:, :W]
        out[2 * pair + 1] = src[:, W:]


def activate(x, gain, valid):
    x = x.astype(F32)
    scale = lax.rsqrt(jnp.sum(x * x, axis=0, keepdims=True) * (1.0 / C) + EPS)
    if valid is not None:
        scale = scale * valid
    h = x * scale * gain
    return (h + h * jnp.tanh(h)).astype(BF16)


def column_taps(a):
    col = lax.broadcasted_iota(jnp.int32, (1, PAIR), 1)
    zero = jnp.zeros_like(a)
    left = jnp.where((col == 0) | (col == W), zero, pltpu.roll(a, 1, 1))
    right = jnp.where((col == W - 1) | (col == PAIR - 1), zero, pltpu.roll(a, PAIR - 1, 1))
    return left, a, right


def fill(stack, act, blocks):
    col = lax.broadcasted_iota(jnp.int32, (1, PAIR), 1)
    before = None
    for p in range(blocks):
        taps = column_taps(act[p])
        turned = [pltpu.roll(t, W, 1) for t in taps]
        for dj in range(3):
            if p < blocks - 1:
                stack[dj * C : (dj + 1) * C, p * PAIR : (p + 1) * PAIR] = taps[dj]
            if p > 0:
                q = slice((p - 1) * PAIR, p * PAIR)
                stack[(6 + dj) * C : (7 + dj) * C, q] = taps[dj]
                stack[(3 + dj) * C : (4 + dj) * C, q] = jnp.where(col < W, before[dj], turned[dj])
        before = turned


def spatial_body(sc, load, w1, g1, w2, g2, out, act1, s1, first, act2, s2):
    core, top, bottom = sc[0], sc[1], sc[2]
    for which, block in ((0, 2 * core), (1, 1), (2, 2 - 2 * core)):
        for t in range(PAIR // LANES):
            lanes = slice(t * LANES, (t + 1) * LANES)
            act1[block, :, lanes] = activate(load(which, lanes), g1[...], None)
    fill(s1, act1, 3)
    first[...] = jnp.dot(w1[...], s1[...], preferred_element_type=F32).astype(BF16)
    lane = lax.broadcasted_iota(jnp.int32, (1, LANES), 1)
    for p in range(2):
        for t in range(PAIR // LANES):
            at = p * PAIR + t * LANES
            pixel = lane + at
            outside = ((pixel < W) & (top > 0)) | ((pixel >= 3 * W) & (bottom > 0))
            valid = jnp.where(outside, 0.0, 1.0).astype(F32)
            act2[p, :, t * LANES : (t + 1) * LANES] = activate(
                first[:, at : at + LANES], g2[...], valid
            )
    fill(s2, act2, 2)
    second = jnp.dot(w2[...], s2[...], preferred_element_type=F32)
    out[...] = (load(1, slice(0, PAIR)).astype(F32) + second).astype(BF16)


def spatial_kernel(sc, z, own, sib, w1, g1, w2, g2, out, *scratch):
    refs = (z, own, sib)
    spatial_body(sc, lambda k, lanes: refs[k][:, lanes], w1, g1, w2, g2, out, *scratch)


def spatial_pick_kernel(pick, sc, z0, own0, sib0, z1, own1, sib1, w1, g1, w2, g2, out, *scratch):
    ones, others = (z0, own0, sib0), (z1, own1, sib1)
    mine = sc[0] == pick

    def load(k, lanes):
        return jnp.where(mine, ones[k][:, lanes], others[k][:, lanes])

    spatial_body(sc, load, w1, g1, w2, g2, out, *scratch)


def spatial(kernel, n_in, name):
    return call(
        kernel,
        pair_shape(),
        n_in,
        name,
        scratch=[
            pltpu.VMEM((3, C, PAIR), BF16),
            pltpu.VMEM((9 * C, 2 * PAIR), BF16),
            pltpu.VMEM((C, 2 * PAIR), BF16),
            pltpu.VMEM((2, C, PAIR), BF16),
            pltpu.VMEM((9 * C, PAIR), BF16),
        ],
        flops=2 * C * C * 9 * 3 * PAIR,
        moved=4000000,
    )


def mixed(wt, x0, x1, x2):
    total = x0[...].astype(F32)
    for tap, x in enumerate((x0, x1, x2)):
        total = total + jnp.dot(
            wt[:, tap * C : (tap + 1) * C], x[...], preferred_element_type=F32
        )
    return total.astype(BF16)


def temporal_kernel(wt, x0, x1, x2, out):
    out[...] = mixed(wt, x0, x1, x2)


def temporal(wt, x0, x1, x2):
    return call(
        temporal_kernel,
        pair_shape(),
        4,
        "temporal",
        scalars=False,
        flops=2 * C * C * 3 * PAIR,
        moved=1300000,
    )(wt, x0, x1, x2)


def temporal_last_kernel(sc, wt, x0, x1, x2, late, keep, send):
    early = mixed(wt, x0, x1, x2)
    is0 = sc[0] == 0
    other = late[...]
    keep[...] = jnp.where(is0, early, other)
    send[...] = jnp.where(is0, other, early)


def on_device(video, spatial_weights, norm_gains, temporal_weights):
    frames, rows = lax.axis_size("frames"), lax.axis_size("rows")
    core = lax.axis_index("frames") % 2
    row = lax.axis_index("rows")
    top = (core == 0) & (row == 0)
    bottom = (core == 1) & (row == rows - 1)
    sc = jnp.stack([core, top, bottom]).astype(jnp.int32)

    swaps = [(i, i ^ 1) for i in range(frames)]
    across = []
    for f in range(frames):
        for r in range(rows):
            to = r + 1 if f % 2 else r - 1
            if 0 <= to < rows:
                across.append((f * rows + r, (f ^ 1) * rows + to))
    later = [(i, i + 2) for i in range(frames - 2)]

    def swap(x):
        return lax.ppermute(x, "frames", swaps)

    def halo(x):
        return lax.ppermute(x, ("frames", "rows"), across)

    def onward(x):
        return lax.ppermute(x, "frames", later)

    view = jnp.transpose(video[0], (0, 2, 1))
    own_m, sib_m = call(pack_kernel, [pair_shape()] * 2, 1, "pack", moved=1000000)(sc, view)
    own_o = swap(sib_m)
    sib_o = swap(own_m)
    z_o = halo(own_m)
    z_m = halo(own_o)
    ws = [prepare(spatial_weights[k], norm_gains[k]) for k in range(4)]
    ts = [prepare_taps(temporal_weights[k]) for k in range(2)]

    weights = (*ws[0], *ws[1])
    arrays = (z_m, own_m, sib_m, z_o, own_o, sib_o)
    inner_b = spatial(functools.partial(spatial_pick_kernel, 1), 10, "spatial_b")(sc, *arrays, *weights)
    before_b = onward(inner_b)
    inner_a = spatial(functools.partial(spatial_pick_kernel, 0), 10, "spatial_a")(sc, *arrays, *weights)
    before_a = onward(inner_a)
    own_b = temporal(ts[0], inner_b, inner_a, before_b)
    sib_b, z_b = swap(own_b), halo(own_b)
    own_a = temporal(ts[0], inner_a, before_b, before_a)
    sib_a, z_a = swap(own_a), halo(own_a)

    weights = (*ws[2], *ws[3])
    inner_b = spatial(spatial_kernel, 7, "spatial_b2")(sc, z_b, own_b, sib_b, *weights)
    before_b = onward(inner_b)
    inner_a = spatial(spatial_kernel, 7, "spatial_a2")(sc, z_a, own_a, sib_a, *weights)
    before_a = onward(inner_a)
    late = temporal(ts[1], inner_b, inner_a, before_b)
    keep, send = call(
        temporal_last_kernel, [pair_shape()] * 2, 5, "temporal_last", moved=1500000
    )(sc, ts[1], inner_a, before_b, before_a, late)
    got = swap(send)
    out = call(
        unpack_kernel, jax.ShapeDtypeStruct((4, C, W), BF16), 2, "unpack", moved=1000000
    )(sc, keep, got)
    return jnp.transpose(out, (0, 2, 1))[None]


def solution(mesh):
    placed = (P("frames", "rows", None, None), P(), P(), P())
    return jax.shard_map(
        on_device,
        mesh=mesh,
        in_specs=placed,
        out_specs=P("frames", "rows", None, None),
        check_vma=False,
    )
```

time: 107 us -> 77.6 us (0.73); the launches traced: 105 us -> 77.3 us
  Pallas kernels: 0 us -> 24 us
  matrix products: 19.5 us -> 0 us
  waiting for transfers between devices: 29.7 us -> 12 us
  other arithmetic: 7.46 us -> 0.08 us
  local copies, waits for them, and re-layouts: 10.3 us -> 3.39 us
    pallas_call x0 -> x16, Pallas kernels: none -> 24 us  [the longest x1 4.39 us: on_device(): spatial(functools.partial(spatial_pick_kernel, 0), 10, 'spatial_a')]
    dot_general x42 -> x0, matrix products: 19.5 us -> none  [the longest x36 16.7 us: convolve(): jnp.einsum('frwc,cd->frwd', window, kernel[row_step, col_step], preferred...]
    ppermute x8 -> x13, waiting for transfers between devices: 29.7 us -> 12 us  [the longest x4 8.53 us: onward(): return lax.ppermute(x, 'frames', later)]
    slice x4 -> x1, local copies, waits for them, and re-layouts: 6.36 us -> 0.01 us  [on_device(): ws = [prepare(spatial_weights[k], norm_gains[k]) for k in range(4)]]
    convert_element_type x4 -> x0, other arithmetic: 4.89 us -> none  [activate(): return jax.nn.silu(scaled).astype(jnp.bfloat16)]
    unnamed x14 -> x6, local copies, waits for them, and re-layouts: 3.96 us -> 1.07 us
    reduce_sum x2 -> x0, other arithmetic: 2.53 us -> none  [activate(): mean_sq = jnp.mean(values * values, axis=-1, keepdims=True)]
    squeeze x0 -> x2, local copies, waits for them, and re-layouts: none -> 2.31 us  [the longest x1 2.27 us: on_device(): ws = [prepare(spatial_weights[k], norm_gains[k]) for k in range(4)]]
  transfers between devices with their start and end apart: 8 -> 13, of which waited for: 6 -> 4; matrix products, arithmetic and copies ran while one was open for 8% -> 3% of each run, Pallas kernels for 0% -> 21%
where the time goes in v1:
time: 77.6 us; the launch traced here: 77.3 us
  starting transfers between devices  37.6 us (48%)
  Pallas kernels  24 us (31%)
  waiting for transfers between devices  12 us (15%)
  local copies, waits for them, and re-layouts  3.39 us (4%)
    ppermute x5, starting transfers between devices, swap(): return lax.ppermute(x, 'frames', swaps)  16.8 us
    ppermute x4, starting transfers between devices, onward(): return lax.ppermute(x, 'frames', later)  11 us
    ppermute x4, starting transfers between devices, halo(): return lax.ppermute(x, ('frames', 'rows'), across)  9.76 us
    ppermute x4, waiting for transfers between devices, onward(): return lax.ppermute(x, 'frames', later)  8.53 us
    pallas_call x1, Pallas kernels, on_device(): spatial(functools.partial(spatial_pick_kernel, 0), 10, 'spatial_a')  4.39 us
    pallas_call x1, Pallas kernels, on_device(): spatial(functools.partial(spatial_pick_kernel, 1), 10, 'spatial_b')  4.38 us
    pallas_call x1, Pallas kernels, on_device(): spatial(spatial_kernel, 7, 'spatial_a2')(sc, z_a, own_a, sib_a, *weights)  4.24 us
    pallas_call x1, Pallas kernels, on_device(): spatial(spatial_kernel, 7, 'spatial_b2')(sc, z_b, own_b, sib_b, *weights)  4.24 us
  transfers between devices with their start and end apart: 13, of which 4 were waited for; matrix products, arithmetic and copies ran while one was open for 3% of the time, Pallas kernels for 21%

profile of v1, /device:TPU:25, one launch (start us, length us, event | category | flops | bytes accessed | tf_op | source)
XLA Modules:
  0.0 77.3 jit_solution(14995602212753234646)
XLA Ops:
  0.0 0.1 pad_add_fusion.sc
  0.1 0.0 copy-start
  0.1 1.1 %copy-done = bf16[1,4,320,192]{2,3,1,0:T(8,128)(2,1)S(1)} copy-done((bf16[1,4,320,192]{2,3,1,0:T(8,128)(2,1)S(1)}, bf16[1,4,320,192]{2,3,1,0:T(8,128)(2,1)}, u32[]{:S(2)}) %copy-start) | copy-done | bytes 491544
  1.1 0.7 pack.1
  1.9 0.8 collective-permute-start
  2.6 3.5 %collective-permute-start.2 = (bf16[192,640]{1,0:T(8,128)(2,1)S(1)}, bf16[192,640]{1,0:T(8,128)(2,1)S(1)}, u32[]{:S(2)}, u32[]{:S(2)}) collective-permute-start(bf16[192,640]{1,0:T(8,128)(2,1)S(1)} %get-tuple-element.18.own0), channel_id=1, source_target_pairs={{1,16},{2,17},{3,18},{4,19},{5,20},{6,21},{7,22},{8,23},{9,24},{10... | collective-permute-start | bytes 737288 | tf_op jit(solution)/shard_map/ppermute | solution.py:226
  6.1 5.3 %collective-permute-start.3 = (bf16[192,640]{1,0:T(8,128)(2,1)S(1)}, bf16[192,640]{1,0:T(8,128)(2,1)S(1)}, u32[]{:S(2)}, u32[]{:S(2)}) collective-permute-start(bf16[192,640]{1,0:T(8,128)(2,1)S(1)} %get-tuple-element.18.own0), channel_id=1, source_target_pairs={{0,16},{16,0},{32,48},{48,32},{64,80},{80,64},{96,112},{112,96},{1... | collective-permute-start | bytes 737288 | tf_op jit(solution)/shard_map/ppermute | solution.py:223
  11.4 0.0 collective-permute-done.own1
  11.4 1.9 %collective-permute-start.1 = (bf16[192,640]{1,0:T(8,128)(2,1)S(1)}, bf16[192,640]{1,0:T(8,128)(2,1)S(1)}, u32[]{:S(2)}, u32[]{:S(2)}) collective-permute-start(bf16[192,640]{1,0:T(8,128)(2,1)S(1)} %collective-permute-done.own1), channel_id=1, source_target_pairs={{1,16},{2,17},{3,18},{4,19},{5,20},{6,21},{7,22},{8,23},{9,24},{10... | collective-permute-start | bytes 737288 | tf_op jit(solution)/shard_map/ppermute | solution.py:226
  13.3 2.3 %slice_bitcast_fusion = (bf16[3,3,192,192]{3,2,1,0:T(8,128)(2,1)S(1)}, bf16[3,3,192,192]{3,2,1,0:T(8,128)(2,1)S(1)}, bf16[3,3,192,192]{3,2,1,0:T(8,128)(2,1)S(1)}, bf16[3,3,192,192]{3,2,1,0:T(8,128)(2,1)S(1)}) fusion(bf16[4,3,3,192,192]{4,3,2,1,0:T(8,128)(2,1)} %param.5), kind=kLoop, calls=%fused_computation | loop fusion | bytes 5308416 | tf_op jit(solution)/shard_map/squeeze | solution.py:237
  15.6 0.0 copy-done.2
  15.6 0.5 weights.4
  16.1 0.5 weights.5
  16.6 0.0 collective-permute-done.2.z1
  16.6 0.0 collective-permute-done.3.sib1
  16.6 2.3 %collective-permute-done.1.z0 = bf16[192,640]{1,0:T(8,128)(2,1)S(1)} collective-permute-done((bf16[192,640]{1,0:T(8,128)(2,1)S(1)}, bf16[192,640]{1,0:T(8,128)(2,1)S(1)}, u32[]{:S(2)}, u32[]{:S(2)}) %collective-permute-start.1) | collective-permute-done | bytes 245792 | tf_op jit(solution)/shard_map/ppermute | solution.py:226
  18.9 4.4 %spatial_b.1.x0 = bf16[192,640]{1,0:T(8,128)(2,1)S(1)} custom-call(s32[3]{0:T(128)S(1)} %pad_add_fusion.sc, bf16[192,640]{1,0:T(8,128)(2,1)S(1)} %collective-permute-done.1.z0, bf16[192,640]{1,0:T(8,128)(2,1)S(1)} %get-tuple-element.18.own0, bf16[192,640]{1,0:T(8,128)(2,1)S(1)} %get-tuple-element.17.sib0, bf16[192,640]{1,0:T(8,128)(2,1)S(1)} %collective-permute-done.2.z1, ...), custom_call_target="tpu_custom_call" | custom-call | flops 1274019840 | bytes 4000000 | tf_op jit(solution)/shard_map/spatial_b/pallas_call | solution.py:242
  23.3 3.1 %collective-permute-start.4 = (bf16[192,640]{1,0:T(8,128)(2,1)S(1)}, bf16[192,640]{1,0:T(8,128)(2,1)S(1)}, u32[]{:S(2)}, u32[]{:S(2)}) collective-permute-start(bf16[192,640]{1,0:T(8,128)(2,1)S(1)} %spatial_b.1.x0), channel_id=1, source_target_pairs={{0,32},{16,48},{32,64},{48,80},{64,96},{80,112},{96,128},{112,144}... | collective-permute-start | bytes 737288 | tf_op jit(solution)/shard_map/ppermute | solution.py:229
  26.4 4.4 %spatial_a.1.x0.x1 = bf16[192,640]{1,0:T(8,128)(2,1)S(1)} custom-call(s32[3]{0:T(128)S(1)} %pad_add_fusion.sc, bf16[192,640]{1,0:T(8,128)(2,1)S(1)} %collective-permute-done.1.z0, bf16[192,640]{1,0:T(8,128)(2,1)S(1)} %get-tuple-element.18.own0, bf16[192,640]{1,0:T(8,128)(2,1)S(1)} %get-tuple-element.17.sib0, bf16[192,640]{1,0:T(8,128)(2,1)S(1)} %collective-permute-done.2.z1, ...), custom_call_target="tpu_custom_call" | custom-call | flops 1274019840 | bytes 4000000 | tf_op jit(solution)/shard_map/spatial_a/pallas_call | solution.py:244
  30.8 3.1 %collective-permute-start.5 = (bf16[192,640]{1,0:T(8,128)(2,1)S(1)}, bf16[192,640]{1,0:T(8,128)(2,1)S(1)}, u32[]{:S(2)}, u32[]{:S(2)}) collective-permute-start(bf16[192,640]{1,0:T(8,128)(2,1)S(1)} %spatial_a.1.x0.x1), channel_id=1, source_target_pairs={{0,32},{16,48},{32,64},{48,80},{64,96},{80,112},{96,128},{112,144}... | collective-permute-start | bytes 737288 | tf_op jit(solution)/shard_map/ppermute | solution.py:229
  33.9 0.0 copy-done.1
  34.0 0.2 taps.3.wt
  34.2 0.0 collective-permute-done.4.x1.x2
  34.2 0.4 temporal.4.own
  34.6 2.5 %collective-permute-start.8 = (bf16[192,640]{1,0:T(8,128)(2,1)S(1)}, bf16[192,640]{1,0:T(8,128)(2,1)S(1)}, u32[]{:S(2)}, u32[]{:S(2)}) collective-permute-start(bf16[192,640]{1,0:T(8,128)(2,1)S(1)} %temporal.4.own), channel_id=1, source_target_pairs={{1,16},{2,17},{3,18},{4,19},{5,20},{6,21},{7,22},{8,23},{9,24},{10... | collective-permute-start | bytes 737288 | tf_op jit(solution)/shard_map/ppermute | solution.py:226
  37.1 4.3 %collective-permute-start.9 = (bf16[192,640]{1,0:T(8,128)(2,1)S(1)}, bf16[192,640]{1,0:T(8,128)(2,1)S(1)}, u32[]{:S(2)}, u32[]{:S(2)}) collective-permute-start(bf16[192,640]{1,0:T(8,128)(2,1)S(1)} %temporal.4.own), channel_id=1, source_target_pairs={{0,16},{16,0},{32,48},{48,32},{64,80},{80,64},{96,112},{112,96},{1... | collective-permute-start | bytes 737288 | tf_op jit(solution)/shard_map/ppermute | solution.py:223
  41.4 0.0 collective-permute-done.5.x2
  41.4 0.4 temporal.3.own
  41.8 1.9 %collective-permute-start.6 = (bf16[192,640]{1,0:T(8,128)(2,1)S(1)}, bf16[192,640]{1,0:T(8,128)(2,1)S(1)}, u32[]{:S(2)}, u32[]{:S(2)}) collective-permute-start(bf16[192,640]{1,0:T(8,128)(2,1)S(1)} %temporal.3.own), channel_id=1, source_target_pairs={{1,16},{2,17},{3,18},{4,19},{5,20},{6,21},{7,22},{8,23},{9,24},{10... | collective-permute-start | bytes 737288 | tf_op jit(solution)/shard_map/ppermute | solution.py:226
  43.7 5.1 %collective-permute-start.7 = (bf16[192,640]{1,0:T(8,128)(2,1)S(1)}, bf16[192,640]{1,0:T(8,128)(2,1)S(1)}, u32[]{:S(2)}, u32[]{:S(2)}) collective-permute-start(bf16[192,640]{1,0:T(8,128)(2,1)S(1)} %temporal.3.own), channel_id=1, source_target_pairs={{0,16},{16,0},{32,48},{48,32},{64,80},{80,64},{96,112},{112,96},{1... | collective-permute-start | bytes 737288 | tf_op jit(solution)/shard_map/ppermute | solution.py:223
  48.8 0.5 weights.6
  49.3 0.5 weights.7
  49.8 0.0 collective-permute-done.8.z
  49.8 0.0 collective-permute-done.9.sib
  49.8 4.2 %spatial_b2.1.x0 = bf16[192,640]{1,0:T(8,128)(2,1)S(1)} custom-call(s32[3]{0:T(128)S(1)} %pad_add_fusion.sc, bf16[192,640]{1,0:T(8,128)(2,1)S(1)} %collective-permute-done.8.z, bf16[192,640]{1,0:T(8,128)(2,1)S(1)} %temporal.4.own, bf16[192,640]{1,0:T(8,128)(2,1)S(1)} %collective-permute-done.9.sib, bf16[192,1728]{1,0:T(8,128)(2,1)S(1)} %get-tuple-element.23.w1, ...), custom_call_target="tpu_custom_call" | custom-call | flops 1274019840 | bytes 4000000 | tf_op jit(solution)/shard_map/spatial_b2/pallas_call | solution.py:252
  54.1 2.8 %collective-permute-start.10 = (bf16[192,640]{1,0:T(8,128)(2,1)S(1)}, bf16[192,640]{1,0:T(8,128)(2,1)S(1)}, u32[]{:S(2)}, u32[]{:S(2)}) collective-permute-start(bf16[192,640]{1,0:T(8,128)(2,1)S(1)} %spatial_b2.1.x0), channel_id=1, source_target_pairs={{0,32},{16,48},{32,64},{48,80},{64,96},{80,112},{96,128},{112,144}... | collective-permute-start | bytes 737288 | tf_op jit(solution)/shard_map/ppermute | solution.py:229
  56.9 0.0 collective-permute-done.6.z
  56.9 0.0 collective-permute-done.7.sib
  56.9 4.2 %spatial_a2.1.x1.x0 = bf16[192,640]{1,0:T(8,128)(2,1)S(1)} custom-call(s32[3]{0:T(128)S(1)} %pad_add_fusion.sc, bf16[192,640]{1,0:T(8,128)(2,1)S(1)} %collective-permute-done.6.z, bf16[192,640]{1,0:T(8,128)(2,1)S(1)} %temporal.3.own, bf16[192,640]{1,0:T(8,128)(2,1)S(1)} %collective-permute-done.7.sib, bf16[192,1728]{1,0:T(8,128)(2,1)S(1)} %get-tuple-element.23.w1, ...), custom_call_target="tpu_custom_call" | custom-call | flops 1274019840 | bytes 4000000 | tf_op jit(solution)/shard_map/spatial_a2/pallas_call | solution.py:254
  61.2 1.9 %collective-permute-start.11 = (bf16[192,640]{1,0:T(8,128)(2,1)S(1)}, bf16[192,640]{1,0:T(8,128)(2,1)S(1)}, u32[]{:S(2)}, u32[]{:S(2)}) collective-permute-start(bf16[192,640]{1,0:T(8,128)(2,1)S(1)} %spatial_a2.1.x1.x0), channel_id=1, source_target_pairs={{0,32},{16,48},{32,64},{48,80},{64,96},{80,112},{96,128},{112,144}... | collective-permute-start | bytes 737288 | tf_op jit(solution)/shard_map/ppermute | solution.py:229
  63.1 0.2 taps.2.wt
  63.3 2.2 %collective-permute-done.10.x2.x1 = bf16[192,640]{1,0:T(8,128)(2,1)S(1)} collective-permute-done((bf16[192,640]{1,0:T(8,128)(2,1)S(1)}, bf16[192,640]{1,0:T(8,128)(2,1)S(1)}, u32[]{:S(2)}, u32[]{:S(2)}) %collective-permute-start.10) | collective-permute-done | bytes 245792 | tf_op jit(solution)/shard_map/ppermute | solution.py:229
  65.5 0.4 temporal.5.late
  65.9 6.4 %collective-permute-done.11.x2 = bf16[192,640]{1,0:T(8,128)(2,1)S(1)} collective-permute-done((bf16[192,640]{1,0:T(8,128)(2,1)S(1)}, bf16[192,640]{1,0:T(8,128)(2,1)S(1)}, u32[]{:S(2)}, u32[]{:S(2)}) %collective-permute-start.11) | collective-permute-done | bytes 245792 | tf_op jit(solution)/shard_map/ppermute | solution.py:229
  72.3 0.9 %temporal_last.1 = (bf16[192,640]{1,0:T(8,128)(2,1)S(1)}, bf16[192,640]{1,0:T(8,128)(2,1)S(1)}) custom-call(s32[3]{0:T(128)S(1)} %pad_add_fusion.sc, bf16[192,576]{1,0:T(8,128)(2,1)S(1)} %taps.2.wt, bf16[192,640]{1,0:T(8,128)(2,1)S(1)} %spatial_a2.1.x1.x0, bf16[192,640]{1,0:T(8,128)(2,1)S(1)} %collective-permute-done.10.x2.x1, ...), custom_call_target="tpu_custom_call" | custom-call | bytes 1500000 | tf_op jit(solution)/shard_map/temporal_last/pallas_call | solution.py:257
  73.2 1.4 %collective-permute-start.12 = (bf16[192,640]{1,0:T(8,128)(2,1)S(1)}, bf16[192,640]{1,0:T(8,128)(2,1)S(1)}, u32[]{:S(2)}, u32[]{:S(2)}) collective-permute-start(bf16[192,640]{1,0:T(8,128)(2,1)S(1)} %get-tuple-element.28), channel_id=1, source_target_pairs={{0,16},{16,0},{32,48},{48,32},{64,80},{80,64},{96,112},{112,96},{1... | collective-permute-start | bytes 737288 | tf_op jit(solution)/shard_map/ppermute | solution.py:223
  74.6 1.1 %collective-permute-done.12.got = bf16[192,640]{1,0:T(8,128)(2,1)S(1)} collective-permute-done((bf16[192,640]{1,0:T(8,128)(2,1)S(1)}, bf16[192,640]{1,0:T(8,128)(2,1)S(1)}, u32[]{:S(2)}, u32[]{:S(2)}) %collective-permute-start.12) | collective-permute-done | bytes 245792 | tf_op jit(solution)/shard_map/ppermute | solution.py:223
  75.7 1.5 %unpack.1 = bf16[4,192,320]{2,1,0:T(8,128)(2,1)} custom-call(s32[3]{0:T(128)S(1)} %pad_add_fusion.sc, bf16[192,640]{1,0:T(8,128)(2,1)S(1)} %get-tuple-element.27.keep, bf16[192,640]{1,0:T(8,128)(2,1)S(1)} %collective-permute-done.12.got), custom_call_target="tpu_custom_call" | custom-call | bytes 1000000 | tf_op jit(solution)/shard_map/unpack/pallas_call | solution.py:261
  (4 shorter events, 0.1 us)
Async XLA Ops:
  0.1 1.1 %copy-start = (bf16[1,4,320,192]{2,3,1,0:T(8,128)(2,1)S(1)}, bf16[1,4,320,192]{2,3,1,0:T(8,128)(2,1)}, u32[]{:S(2)}) copy-start(bf16[1,4,320,192]{2,3,1,0:T(8,128)(2,1)} %param.4) | copy-start | bytes 1474564
  1.9 9.5 %collective-permute-start = (bf16[192,640]{1,0:T(8,128)(2,1)S(1)}, bf16[192,640]{1,0:T(8,128)(2,1)S(1)}, u32[]{:S(2)}, u32[]{:S(2)}) collective-permute-start(bf16[192,640]{1,0:T(8,128)(2,1)S(1)} %get-tuple-element.17.sib0), channel_id=1, source_target_pairs={{0,16},{16,0},{32,48},{48,32},{64,80},{80,64},{96,112},{112,96},{1... | collective-permute-start | bytes 737288 | tf_op jit(solution)/shard_map/ppermute | solution.py:223
  2.6 13.0 %copy-start.2 = (f32[4,192]{1,0:T(4,128)S(1)}, f32[4,192]{1,0:T(4,128)}, u32[]{:S(2)}) copy-start(f32[4,192]{1,0:T(4,128)} %param.6) | copy-start | bytes 9220
  2.6 14.0 %collective-permute-start.2 = (bf16[192,640]{1,0:T(8,128)(2,1)S(1)}, bf16[192,640]{1,0:T(8,128)(2,1)S(1)}, u32[]{:S(2)}, u32[]{:S(2)}) collective-permute-start(bf16[192,640]{1,0:T(8,128)(2,1)S(1)} %get-tuple-element.18.own0), channel_id=1, source_target_pairs={{1,16},{2,17},{3,18},{4,19},{5,20},{6,21},{7,22},{8,23},{9,24},{10... | collective-permute-start | bytes 737288 | tf_op jit(solution)/shard_map/ppermute | solution.py:226
  6.1 10.5 %collective-permute-start.3 = (bf16[192,640]{1,0:T(8,128)(2,1)S(1)}, bf16[192,640]{1,0:T(8,128)(2,1)S(1)}, u32[]{:S(2)}, u32[]{:S(2)}) collective-permute-start(bf16[192,640]{1,0:T(8,128)(2,1)S(1)} %get-tuple-element.18.own0), channel_id=1, source_target_pairs={{0,16},{16,0},{32,48},{48,32},{64,80},{80,64},{96,112},{112,96},{1... | collective-permute-start | bytes 737288 | tf_op jit(solution)/shard_map/ppermute | solution.py:223
  11.4 7.5 %collective-permute-start.1 = (bf16[192,640]{1,0:T(8,128)(2,1)S(1)}, bf16[192,640]{1,0:T(8,128)(2,1)S(1)}, u32[]{:S(2)}, u32[]{:S(2)}) collective-permute-start(bf16[192,640]{1,0:T(8,128)(2,1)S(1)} %collective-permute-done.own1), channel_id=1, source_target_pairs={{1,16},{2,17},{3,18},{4,19},{5,20},{6,21},{7,22},{8,23},{9,24},{10... | collective-permute-start | bytes 737288 | tf_op jit(solution)/shard_map/ppermute | solution.py:226
  18.9 15.0 %copy-start.1 = (bf16[2,3,192,192]{3,2,1,0:T(8,128)(2,1)S(1)}, bf16[2,3,192,192]{3,2,1,0:T(8,128)(2,1)}, u32[]{:S(2)}) copy-start(bf16[2,3,192,192]{3,2,1,0:T(8,128)(2,1)} %param.7) | copy-start | bytes 1327108
  23.3 10.9 %collective-permute-start.4 = (bf16[192,640]{1,0:T(8,128)(2,1)S(1)}, bf16[192,640]{1,0:T(8,128)(2,1)S(1)}, u32[]{:S(2)}, u32[]{:S(2)}) collective-permute-start(bf16[192,640]{1,0:T(8,128)(2,1)S(1)} %spatial_b.1.x0), channel_id=1, source_target_pairs={{0,32},{16,48},{32,64},{48,80},{64,96},{80,112},{96,128},{112,144}... | collective-permute-start | bytes 737288 | tf_op jit(solution)/shard_map/ppermute | solution.py:229
  30.8 10.6 %collective-permute-start.5 = (bf16[192,640]{1,0:T(8,128)(2,1)S(1)}, bf16[192,640]{1,0:T(8,128)(2,1)S(1)}, u32[]{:S(2)}, u32[]{:S(2)}) collective-permute-start(bf16[192,640]{1,0:T(8,128)(2,1)S(1)} %spatial_a.1.x0.x1), channel_id=1, source_target_pairs={{0,32},{16,48},{32,64},{48,80},{64,96},{80,112},{96,128},{112,144}... | collective-permute-start | bytes 737288 | tf_op jit(solution)/shard_map/ppermute | solution.py:229
  34.6 15.2 %collective-permute-start.8 = (bf16[192,640]{1,0:T(8,128)(2,1)S(1)}, bf16[192,640]{1,0:T(8,128)(2,1)S(1)}, u32[]{:S(2)}, u32[]{:S(2)}) collective-permute-start(bf16[192,640]{1,0:T(8,128)(2,1)S(1)} %temporal.4.own), channel_id=1, source_target_pairs={{1,16},{2,17},{3,18},{4,19},{5,20},{6,21},{7,22},{8,23},{9,24},{10... | collective-permute-start | bytes 737288 | tf_op jit(solution)/shard_map/ppermute | solution.py:226
  37.1 12.7 %collective-permute-start.9 = (bf16[192,640]{1,0:T(8,128)(2,1)S(1)}, bf16[192,640]{1,0:T(8,128)(2,1)S(1)}, u32[]{:S(2)}, u32[]{:S(2)}) collective-permute-start(bf16[192,640]{1,0:T(8,128)(2,1)S(1)} %temporal.4.own), channel_id=1, source_target_pairs={{0,16},{16,0},{32,48},{48,32},{64,80},{80,64},{96,112},{112,96},{1... | collective-permute-start | bytes 737288 | tf_op jit(solution)/shard_map/ppermute | solution.py:223
  41.8 15.1 %collective-permute-start.6 = (bf16[192,640]{1,0:T(8,128)(2,1)S(1)}, bf16[192,640]{1,0:T(8,128)(2,1)S(1)}, u32[]{:S(2)}, u32[]{:S(2)}) collective-permute-start(bf16[192,640]{1,0:T(8,128)(2,1)S(1)} %temporal.3.own), channel_id=1, source_target_pairs={{1,16},{2,17},{3,18},{4,19},{5,20},{6,21},{7,22},{8,23},{9,24},{10... | collective-permute-start | bytes 737288 | tf_op jit(solution)/shard_map/ppermute | solution.py:226
  43.7 13.2 %collective-permute-start.7 = (bf16[192,640]{1,0:T(8,128)(2,1)S(1)}, bf16[192,640]{1,0:T(8,128)(2,1)S(1)}, u32[]{:S(2)}, u32[]{:S(2)}) collective-permute-start(bf16[192,640]{1,0:T(8,128)(2,1)S(1)} %temporal.3.own), channel_id=1, source_target_pairs={{0,16},{16,0},{32,48},{48,32},{64,80},{80,64},{96,112},{112,96},{1... | collective-permute-start | bytes 737288 | tf_op jit(solution)/shard_map/ppermute | solution.py:223
  54.1 11.4 %collective-permute-start.10 = (bf16[192,640]{1,0:T(8,128)(2,1)S(1)}, bf16[192,640]{1,0:T(8,128)(2,1)S(1)}, u32[]{:S(2)}, u32[]{:S(2)}) collective-permute-start(bf16[192,640]{1,0:T(8,128)(2,1)S(1)} %spatial_b2.1.x0), channel_id=1, source_target_pairs={{0,32},{16,48},{32,64},{48,80},{64,96},{80,112},{96,128},{112,144}... | collective-permute-start | bytes 737288 | tf_op jit(solution)/shard_map/ppermute | solution.py:229
  61.2 11.1 %collective-permute-start.11 = (bf16[192,640]{1,0:T(8,128)(2,1)S(1)}, bf16[192,640]{1,0:T(8,128)(2,1)S(1)}, u32[]{:S(2)}, u32[]{:S(2)}) collective-permute-start(bf16[192,640]{1,0:T(8,128)(2,1)S(1)} %spatial_a2.1.x1.x0), channel_id=1, source_target_pairs={{0,32},{16,48},{32,64},{48,80},{64,96},{80,112},{96,128},{112,144}... | collective-permute-start | bytes 737288 | tf_op jit(solution)/shard_map/ppermute | solution.py:229
  73.2 2.5 %collective-permute-start.12 = (bf16[192,640]{1,0:T(8,128)(2,1)S(1)}, bf16[192,640]{1,0:T(8,128)(2,1)S(1)}, u32[]{:S(2)}, u32[]{:S(2)}) collective-permute-start(bf16[192,640]{1,0:T(8,128)(2,1)S(1)} %get-tuple-element.28), channel_id=1, source_target_pairs={{0,16},{16,0},{32,48},{48,32},{64,80},{80,64},{96,112},{112,96},{1... | collective-permute-start | bytes 737288 | tf_op jit(solution)/shard_map/ppermute | solution.py:223

commit v2 on v1

v2 whole, which is shorter than its diff:
```python
import functools

import jax
import jax.numpy as jnp
from jax import lax
from jax.experimental import pallas as pl
from jax.experimental.pallas import tpu as pltpu
from jax.sharding import PartitionSpec as P

C = 192
W = 320
PAIR = 2 * W
LANES = 128
EPS = 1e-06
F32 = jnp.float32
BF16 = jnp.bfloat16
VMEM = pl.BlockSpec(memory_space=pltpu.VMEM)
ANY = pl.BlockSpec(memory_space=pl.ANY)
LIMIT = 28 << 20


def call(kernel, outs, n_in, name, scratch=(), flops=0, moved=0, in_specs=None, out_specs=None, aliases=None):
    many = isinstance(outs, (list, tuple))
    if out_specs is None:
        out_specs = [VMEM] * len(outs) if many else VMEM
    return pl.pallas_call(
        kernel,
        out_shape=outs,
        in_specs=in_specs or [VMEM] * n_in,
        out_specs=out_specs,
        scratch_shapes=list(scratch),
        input_output_aliases=aliases or {},
        compiler_params=pltpu.CompilerParams(vmem_limit_bytes=LIMIT),
        cost_estimate=pl.CostEstimate(flops=flops, bytes_accessed=moved, transcendentals=0),
        name=name,
    )


def pair_shape():
    return jax.ShapeDtypeStruct((C, PAIR), BF16)


def core_index():
    return lax.rem(lax.axis_index("frames"), 2)


def weights_kernel(first, sw, g, *outs):
    for k in range(2):
        wt, gt = outs[2 * k : 2 * k + 2]
        for di in range(3):
            for dj in range(3):
                wt[dj * C : (dj + 1) * C, di * C : (di + 1) * C] = sw[first + k, di, dj].T
        gt[...] = jnp.broadcast_to(g[first + k : first + k + 1, :] * 0.5, (LANES, C)).T


def prepare(weights, gains, first):
    shapes = [jax.ShapeDtypeStruct((3 * C, 3 * C), BF16), jax.ShapeDtypeStruct((C, LANES), F32)]
    return call(
        functools.partial(weights_kernel, first), shapes * 2, 2, "weights", moved=3000000
    )(weights, gains)


def taps_kernel(tw, *outs):
    for k in range(2):
        for tap in range(3):
            outs[k][:, tap * C : (tap + 1) * C] = tw[k, tap].T


def prepare_taps(weights):
    shape = jax.ShapeDtypeStruct((C, 3 * C), BF16)
    return call(taps_kernel, [shape] * 2, 1, "taps", moved=1000000)(weights)


def pack_kernel(v, own, sib, rows, sems):
    core = core_index()
    order = (2 * core, 2 * core + 1, 2 - 2 * core, 3 - 2 * core)
    copies = [pltpu.make_async_copy(v.at[order[i]], rows.at[i], sems.at[i]) for i in range(4)]
    for copy in copies:
        copy.start()
    for i, dst in ((0, own), (2, sib)):
        copies[i].wait()
        dst[:, :W] = rows[i]
        copies[i + 1].wait()
        dst[:, W:] = rows[i + 1]


def unpack_rows(x, out, rows, sems, pair):
    copies = []
    for i in range(2):
        rows[i] = x[:, i * W : (i + 1) * W]
        copy = pltpu.make_async_copy(rows.at[i], out.at[2 * pair + i], sems.at[i])
        copy.start()
        copies.append(copy)
    for copy in copies:
        copy.wait()


def unpack_keep_kernel(keep, out, rows, sems):
    unpack_rows(keep, out, rows, sems, core_index())


def unpack_got_kernel(got, part, out, rows, sems):
    del part
    unpack_rows(got, out, rows, sems, 1 - core_index())


def unpack(kernel, x, *part):
    return call(
        kernel,
        jax.ShapeDtypeStruct((4, C, W), BF16),
        1 + len(part),
        "unpack",
        scratch=[pltpu.VMEM((2, C, W), BF16), pltpu.SemaphoreType.DMA((2,))],
        moved=500000,
        in_specs=[VMEM] + [ANY] * len(part),
        out_specs=ANY,
        aliases={1: 0} if part else None,
    )(x, *part)


def tiles_of(x):
    return [x[:, t * LANES : (t + 1) * LANES] for t in range(x.shape[1] // LANES)]


def activate(x, gain, valid):
    x = x.astype(F32)
    scale = lax.rsqrt(jnp.sum(x * x, axis=0, keepdims=True) * (1.0 / C) + EPS)
    if valid is not None:
        scale = scale * valid
    h = x * scale * gain
    return (h + h * jnp.tanh(h)).astype(BF16)


def between(x, y):
    low = lax.broadcasted_iota(jnp.int32, (1, LANES), 1) < LANES // 2
    turned = [pltpu.roll(t, LANES // 2, 1) for t in x[2:] + y[:3]]
    return [jnp.where(low, turned[i], turned[i + 1]) for i in range(5)]


def stack(rows, at, x, y):
    for t, (above, middle, below) in enumerate(zip(x, between(x, y), y)):
        lanes = slice(at + t * LANES, at + (t + 1) * LANES)
        rows[:C, lanes] = above
        rows[C : 2 * C, lanes] = middle
        rows[2 * C :, lanes] = below


def convolved(weight, rows):
    lane = lax.broadcasted_iota(jnp.int32, (1, LANES), 1)
    out = []
    for at in range(0, rows.shape[1], PAIR):
        product = jnp.dot(weight[...], rows[:, at : at + PAIR], preferred_element_type=F32)
        left, middle, right = (tiles_of(product[dj * C : (dj + 1) * C]) for dj in range(3))
        left = [pltpu.roll(t, 1, 1) for t in left]
        right = [pltpu.roll(t, LANES - 1, 1) for t in right]
        for t in range(5):
            a = jnp.where(lane == 0, left[t - 1] if t else 0.0, left[t])
            b = jnp.where(lane == LANES - 1, right[t + 1] if t < 4 else 0.0, right[t])
            if t == W // LANES:
                a = jnp.where(lane == W % LANES, 0.0, a)
                b = jnp.where(lane == W % LANES - 1, 0.0, b)
            out.append(middle[t] + a + b)
    return out


def spatial_body(z, own, sib, w1, g1, w2, g2, out, s1, s2):
    core, row = core_index(), lax.axis_index("rows")
    is0 = core == 0
    top = is0 & (row == 0)
    bottom = (core == 1) & (row == lax.axis_size("rows") - 1)
    gain = g1[...]
    above, mid, below = [], [], []
    for tz, to, ts in zip(z, own, sib):
        above.append(activate(jnp.where(is0, tz, ts), gain, None))
        mid.append(activate(to, gain, None))
        below.append(activate(jnp.where(is0, ts, tz), gain, None))
    stack(s1, 0, above, mid)
    stack(s1, PAIR, mid, below)
    lane = lax.broadcasted_iota(jnp.int32, (1, LANES), 1)
    gain = g2[...]
    act = []
    for t, x in enumerate(convolved(w1, s1)):
        pixel = lane + t * LANES
        outside = ((pixel < W) & top) | ((pixel >= 3 * W) & bottom)
        act.append(activate(x.astype(BF16), gain, jnp.where(outside, 0.0, 1.0).astype(F32)))
    stack(s2, 0, act[:5], act[5:])
    for t, (x, y) in enumerate(zip(own, convolved(w2, s2))):
        out[:, t * LANES : (t + 1) * LANES] = (x.astype(F32) + y).astype(BF16)


def spatial_kernel(z, own, sib, *rest):
    spatial_body(tiles_of(z), tiles_of(own), tiles_of(sib), *rest)


def spatial_pick_kernel(pick, z0, own0, sib0, z1, own1, sib1, *rest):
    mine = core_index() == pick

    def chosen(x, y):
        return [jnp.where(mine, s, t) for s, t in zip(tiles_of(x), tiles_of(y))]

    spatial_body(chosen(z0, z1), chosen(own0, own1), chosen(sib0, sib1), *rest)


def spatial(kernel, n_in, name):
    return call(
        kernel,
        pair_shape(),
        n_in,
        name,
        scratch=[pltpu.VMEM((3 * C, 2 * PAIR), BF16), pltpu.VMEM((3 * C, PAIR), BF16)],
        flops=2 * C * C * 9 * 3 * PAIR,
        moved=4000000,
    )


def mixed(wt, x0, x1, x2):
    total = x0[...].astype(F32)
    for tap, x in enumerate((x0, x1, x2)):
        total = total + jnp.dot(
            wt[:, tap * C : (tap + 1) * C], x[...], preferred_element_type=F32
        )
    return total.astype(BF16)


def temporal_kernel(wt, x0, x1, x2, out):
    out[...] = mixed(wt, x0, x1, x2)


def temporal(wt, x0, x1, x2):
    return call(
        temporal_kernel, pair_shape(), 4, "temporal", flops=2 * C * C * 3 * PAIR, moved=1300000
    )(wt, x0, x1, x2)


def temporal_last_kernel(wt, x0, x1, x2, late, keep, send):
    early = mixed(wt, x0, x1, x2)
    is0 = core_index() == 0
    other = late[...]
    keep[...] = jnp.where(is0, early, other)
    send[...] = jnp.where(is0, other, early)


def on_device(video, spatial_weights, norm_gains, temporal_weights):
    frames, rows = lax.axis_size("frames"), lax.axis_size("rows")
    swaps = [(i, i ^ 1) for i in range(frames)]
    across = []
    for f in range(frames):
        for r in range(rows):
            to = r + 1 if f % 2 else r - 1
            if 0 <= to < rows:
                across.append((f * rows + r, (f ^ 1) * rows + to))
    later = [(i, i + 2) for i in range(frames - 2)]

    def swap(x):
        return lax.ppermute(x, "frames", swaps)

    def halo(x):
        return lax.ppermute(x, ("frames", "rows"), across)

    def onward(x):
        return lax.ppermute(x, "frames", later)

    view = jnp.transpose(video[0], (0, 2, 1))
    own_m, sib_m = call(
        pack_kernel,
        [pair_shape()] * 2,
        1,
        "pack",
        scratch=[pltpu.VMEM((4, C, W), BF16), pltpu.SemaphoreType.DMA((4,))],
        moved=1000000,
        in_specs=[pl.BlockSpec(memory_space=pltpu.HBM)],
    )(view)
    own_o = swap(sib_m)
    sib_o = swap(own_m)
    z_o = halo(own_m)
    z_m = halo(own_o)
    ts = prepare_taps(temporal_weights)
    ws = [prepare(spatial_weights, norm_gains, 2 * k) for k in range(2)]

    arrays = (z_m, own_m, sib_m, z_o, own_o, sib_o)
    inner_b = spatial(functools.partial(spatial_pick_kernel, 1), 10, "spatial_b")(*arrays, *ws[0])
    before_b = onward(inner_b)
    inner_a = spatial(functools.partial(spatial_pick_kernel, 0), 10, "spatial_a")(*arrays, *ws[0])
    before_a = onward(inner_a)
    own_b = temporal(ts[0], inner_b, inner_a, before_b)
    sib_b, z_b = swap(own_b), halo(own_b)
    own_a = temporal(ts[0], inner_a, before_b, before_a)
    sib_a, z_a = swap(own_a), halo(own_a)

    inner_b = spatial(spatial_kernel, 7, "spatial_b2")(z_b, own_b, sib_b, *ws[1])
    before_b = onward(inner_b)
    inner_a = spatial(spatial_kernel, 7, "spatial_a2")(z_a, own_a, sib_a, *ws[1])
    before_a = onward(inner_a)
    late = temporal(ts[1], inner_b, inner_a, before_b)
    keep, send = call(temporal_last_kernel, [pair_shape()] * 2, 5, "temporal_last", moved=1500000)(
        ts[1], inner_a, before_b, before_a, late
    )
    got = swap(send)
    out = unpack(unpack_got_kernel, got, unpack(unpack_keep_kernel, keep))
    return jnp.transpose(out, (0, 2, 1))[None]


def solution(mesh):
    placed = (P("frames", "rows", None, None), P(), P(), P())
    return jax.shard_map(
        on_device,
        mesh=mesh,
        in_specs=placed,
        out_specs=P("frames", "rows", None, None),
        check_vma=False,
    )
```

time: 77.6 us -> 71.2 us (0.918)
  Pallas kernels: 24 us -> 17 us
  waiting for transfers between devices: 12 us -> 11.2 us
  starting transfers between devices: 37.6 us -> 38.4 us
    pallas_call x13 -> x11, Pallas kernels: 14.3 us -> 11 us  [the longest x1 2.58 us: on_device(): spatial(spatial_kernel, 7, 'spatial_a2')(z_a, own_a, sib_a, *ws[1])]
    unnamed x6 -> x12, local copies, waits for them, and re-layouts: 1.07 us -> 3.76 us
    squeeze x2 -> x0, local copies, waits for them, and re-layouts: 2.31 us -> none  [the longest x1 2.27 us: on_device(): ws = [prepare(spatial_weights[k], norm_gains[k]) for k in range(4)]]
    pallas_call x1, Pallas kernels: 4.38 us -> 2.8 us  [on_device(): spatial(functools.partial(spatial_pick_kernel, 1), 10, 'spatial_b')]
    pallas_call x1, Pallas kernels: 4.39 us -> 2.81 us  [on_device(): spatial(functools.partial(spatial_pick_kernel, 0), 10, 'spatial_a')]
    ppermute x5, waiting for transfers between devices: 1.15 us -> 0.34 us  [swap(): return lax.ppermute(x, 'frames', swaps)]
  transfers between devices with their start and end apart: 13 -> 13, of which waited for: 4 -> 4; matrix products, arithmetic and copies ran while one was open for 3% -> 0% of each run, Pallas kernels for 21% -> 17%
where the time goes in v2:
time: 71.2 us; the launch traced here: 70.8 us
  starting transfers between devices  38.4 us (54%)
  Pallas kernels  17 us (24%)
  waiting for transfers between devices  11.2 us (16%)
  local copies, waits for them, and re-layouts  3.76 us (5%)
    ppermute x5, starting transfers between devices, swap(): return lax.ppermute(x, 'frames', swaps)  17.5 us
    ppermute x4, starting transfers between devices, onward(): return lax.ppermute(x, 'frames', later)  10.9 us
    ppermute x4, starting transfers between devices, halo(): return lax.ppermute(x, ('frames', 'rows'), across)  10.1 us
    ppermute x4, waiting for transfers between devices, onward(): return lax.ppermute(x, 'frames', later)  8.78 us
    unnamed x12, local copies, waits for them, and re-layouts  3.76 us
    pallas_call x1, Pallas kernels, on_device(): spatial(functools.partial(spatial_pick_kernel, 0), 10, 'spatial_a')  2.81 us
    pallas_call x1, Pallas kernels, on_device(): spatial(functools.partial(spatial_pick_kernel, 1), 10, 'spatial_b')  2.8 us
    pallas_call x1, Pallas kernels, on_device(): spatial(spatial_kernel, 7, 'spatial_a2')(z_a, own_a, sib_a, *ws[1])  2.58 us
  transfers between devices with their start and end apart: 13, of which 4 were waited for; matrix products, arithmetic and copies ran while one was open for 0% of the time, Pallas kernels for 17%

profile of v2, /device:TPU:25, one launch (start us, length us, event | category | flops | bytes accessed | tf_op | source)
XLA Modules:
  0.0 70.8 jit_solution(16112518956520338561)
XLA Ops:
  0.0 1.1 %copy-done.2 = bf16[1,4,320,192]{2,3,1,0:T(8,128)(2,1)S(1)} copy-done((bf16[1,4,320,192]{2,3,1,0:T(8,128)(2,1)S(1)}, bf16[1,4,320,192]{2,3,1,0:T(8,128)(2,1)}, u32[]{:S(2)}) %copy-start.2) | copy-done | bytes 491544
  1.1 1.0 %pack.1 = (bf16[192,640]{1,0:T(8,128)(2,1)S(1)}, bf16[192,640]{1,0:T(8,128)(2,1)S(1)}) custom-call(bf16[4,192,320]{2,1,0:T(8,128)(2,1)S(1)} %bitcast.6), custom_call_target="tpu_custom_call" | custom-call | bytes 1000000 | tf_op jit(solution)/shard_map/pack/pallas_call | solution.py:264
  2.1 0.8 %collective-permute-start = (bf16[192,640]{1,0:T(8,128)(2,1)S(1)}, bf16[192,640]{1,0:T(8,128)(2,1)S(1)}, u32[]{:S(2)}, u32[]{:S(2)}) collective-permute-start(bf16[192,640]{1,0:T(8,128)(2,1)S(1)} %get-tuple-element.21.sib0), channel_id=1, source_target_pairs={{0,16},{16,0},{32,48},{48,32},{64,80},{80,64},{96,112},{112,96},{1... | collective-permute-start | bytes 737288 | tf_op jit(solution)/shard_map/ppermute | solution.py:255
  2.9 3.4 %collective-permute-start.2 = (bf16[192,640]{1,0:T(8,128)(2,1)S(1)}, bf16[192,640]{1,0:T(8,128)(2,1)S(1)}, u32[]{:S(2)}, u32[]{:S(2)}) collective-permute-start(bf16[192,640]{1,0:T(8,128)(2,1)S(1)} %get-tuple-element.22.own0), channel_id=1, source_target_pairs={{1,16},{2,17},{3,18},{4,19},{5,20},{6,21},{7,22},{8,23},{9,24},{10... | collective-permute-start | bytes 737288 | tf_op jit(solution)/shard_map/ppermute | solution.py:258
  6.3 5.2 %collective-permute-start.3 = (bf16[192,640]{1,0:T(8,128)(2,1)S(1)}, bf16[192,640]{1,0:T(8,128)(2,1)S(1)}, u32[]{:S(2)}, u32[]{:S(2)}) collective-permute-start(bf16[192,640]{1,0:T(8,128)(2,1)S(1)} %get-tuple-element.22.own0), channel_id=1, source_target_pairs={{0,16},{16,0},{32,48},{48,32},{64,80},{80,64},{96,112},{112,96},{1... | collective-permute-start | bytes 737288 | tf_op jit(solution)/shard_map/ppermute | solution.py:255
  11.5 0.0 collective-permute-done.own1
  11.5 1.9 %collective-permute-start.1 = (bf16[192,640]{1,0:T(8,128)(2,1)S(1)}, bf16[192,640]{1,0:T(8,128)(2,1)S(1)}, u32[]{:S(2)}, u32[]{:S(2)}) collective-permute-start(bf16[192,640]{1,0:T(8,128)(2,1)S(1)} %collective-permute-done.own1), channel_id=1, source_target_pairs={{1,16},{2,17},{3,18},{4,19},{5,20},{6,21},{7,22},{8,23},{9,24},{10... | collective-permute-start | bytes 737288 | tf_op jit(solution)/shard_map/ppermute | solution.py:258
  13.4 0.0 copy-start
  13.4 2.0 %copy-done = bf16[4,3,3,192,192]{4,3,2,1,0:T(8,128)(2,1)S(1)} copy-done((bf16[4,3,3,192,192]{4,3,2,1,0:T(8,128)(2,1)S(1)}, bf16[4,3,3,192,192]{4,3,2,1,0:T(8,128)(2,1)}, u32[]{:S(2)}) %copy-start) | copy-done | bytes 2654232
  15.4 0.7 copy-done.4
  16.1 0.9 %weights.2 = (bf16[576,576]{1,0:T(8,128)(2,1)S(1)}, f32[192,128]{1,0:T(8,128)S(1)}, bf16[576,576]{1,0:T(8,128)(2,1)S(1)}, f32[192,128]{1,0:T(8,128)S(1)}) custom-call(bf16[4,3,3,192,192]{4,3,2,1,0:T(8,128)(2,1)S(1)} %copy-done, f32[4,192]{1,0:T(4,128)S(1)} %copy-done.4), custom_call_target="tpu_custom_call" | custom-call | bytes 3000000 | tf_op jit(solution)/shard_map/weights/pallas_call | solution.py:58
  17.0 0.0 collective-permute-done.2.z1
  17.0 0.0 collective-permute-done.3.sib1
  17.0 2.0 %collective-permute-done.1.z0 = bf16[192,640]{1,0:T(8,128)(2,1)S(1)} collective-permute-done((bf16[192,640]{1,0:T(8,128)(2,1)S(1)}, bf16[192,640]{1,0:T(8,128)(2,1)S(1)}, u32[]{:S(2)}, u32[]{:S(2)}) %collective-permute-start.1) | collective-permute-done | bytes 245792 | tf_op jit(solution)/shard_map/ppermute | solution.py:258
  19.0 2.8 %spatial_b.1.x0 = bf16[192,640]{1,0:T(8,128)(2,1)S(1)} custom-call(bf16[192,640]{1,0:T(8,128)(2,1)S(1)} %collective-permute-done.1.z0, bf16[192,640]{1,0:T(8,128)(2,1)S(1)} %get-tuple-element.22.own0, bf16[192,640]{1,0:T(8,128)(2,1)S(1)} %get-tuple-element.21.sib0, bf16[192,640]{1,0:T(8,128)(2,1)S(1)} %collective-permute-done.2.z1, ...), custom_call_target="tpu_custom_call" | custom-call | flops 1274019840 | bytes 4000000 | tf_op jit(solution)/shard_map/spatial_b/pallas_call | solution.py:281
  21.8 0.0 copy-start.1
  21.8 0.0 copy-start.5
  21.8 3.4 %collective-permute-start.4 = (bf16[192,640]{1,0:T(8,128)(2,1)S(1)}, bf16[192,640]{1,0:T(8,128)(2,1)S(1)}, u32[]{:S(2)}, u32[]{:S(2)}) collective-permute-start(bf16[192,640]{1,0:T(8,128)(2,1)S(1)} %spatial_b.1.x0), channel_id=1, source_target_pairs={{0,32},{16,48},{32,64},{48,80},{64,96},{80,112},{96,128},{112,144}... | collective-permute-start | bytes 737288 | tf_op jit(solution)/shard_map/ppermute | solution.py:261
  25.2 2.8 %spatial_a.1.x0.x1 = bf16[192,640]{1,0:T(8,128)(2,1)S(1)} custom-call(bf16[192,640]{1,0:T(8,128)(2,1)S(1)} %collective-permute-done.1.z0, bf16[192,640]{1,0:T(8,128)(2,1)S(1)} %get-tuple-element.22.own0, bf16[192,640]{1,0:T(8,128)(2,1)S(1)} %get-tuple-element.21.sib0, bf16[192,640]{1,0:T(8,128)(2,1)S(1)} %collective-permute-done.2.z1, ...), custom_call_target="tpu_custom_call" | custom-call | flops 1274019840 | bytes 4000000 | tf_op jit(solution)/shard_map/spatial_a/pallas_call | solution.py:283
  28.0 3.1 %collective-permute-start.5 = (bf16[192,640]{1,0:T(8,128)(2,1)S(1)}, bf16[192,640]{1,0:T(8,128)(2,1)S(1)}, u32[]{:S(2)}, u32[]{:S(2)}) collective-permute-start(bf16[192,640]{1,0:T(8,128)(2,1)S(1)} %spatial_a.1.x0.x1), channel_id=1, source_target_pairs={{0,32},{16,48},{32,64},{48,80},{64,96},{80,112},{96,128},{112,144}... | collective-permute-start | bytes 737288 | tf_op jit(solution)/shard_map/ppermute | solution.py:261
  31.2 0.0 copy-done.3
  31.2 0.3 taps.1
  31.5 0.0 collective-permute-done.4.x1.x2
  31.5 0.4 temporal.4.own
  31.9 2.8 %collective-permute-start.8 = (bf16[192,640]{1,0:T(8,128)(2,1)S(1)}, bf16[192,640]{1,0:T(8,128)(2,1)S(1)}, u32[]{:S(2)}, u32[]{:S(2)}) collective-permute-start(bf16[192,640]{1,0:T(8,128)(2,1)S(1)} %temporal.4.own), channel_id=1, source_target_pairs={{1,16},{2,17},{3,18},{4,19},{5,20},{6,21},{7,22},{8,23},{9,24},{10... | collective-permute-start | bytes 737288 | tf_op jit(solution)/shard_map/ppermute | solution.py:258
  34.7 4.4 %collective-permute-start.9 = (bf16[192,640]{1,0:T(8,128)(2,1)S(1)}, bf16[192,640]{1,0:T(8,128)(2,1)S(1)}, u32[]{:S(2)}, u32[]{:S(2)}) collective-permute-start(bf16[192,640]{1,0:T(8,128)(2,1)S(1)} %temporal.4.own), channel_id=1, source_target_pairs={{0,16},{16,0},{32,48},{48,32},{64,80},{80,64},{96,112},{112,96},{1... | collective-permute-start | bytes 737288 | tf_op jit(solution)/shard_map/ppermute | solution.py:255
  39.1 0.0 collective-permute-done.5.x2
  39.1 0.4 temporal.3.own
  39.5 1.9 %collective-permute-start.6 = (bf16[192,640]{1,0:T(8,128)(2,1)S(1)}, bf16[192,640]{1,0:T(8,128)(2,1)S(1)}, u32[]{:S(2)}, u32[]{:S(2)}) collective-permute-start(bf16[192,640]{1,0:T(8,128)(2,1)S(1)} %temporal.3.own), channel_id=1, source_target_pairs={{1,16},{2,17},{3,18},{4,19},{5,20},{6,21},{7,22},{8,23},{9,24},{10... | collective-permute-start | bytes 737288 | tf_op jit(solution)/shard_map/ppermute | solution.py:258
  41.4 5.6 %collective-permute-start.7 = (bf16[192,640]{1,0:T(8,128)(2,1)S(1)}, bf16[192,640]{1,0:T(8,128)(2,1)S(1)}, u32[]{:S(2)}, u32[]{:S(2)}) collective-permute-start(bf16[192,640]{1,0:T(8,128)(2,1)S(1)} %temporal.3.own), channel_id=1, source_target_pairs={{0,16},{16,0},{32,48},{48,32},{64,80},{80,64},{96,112},{112,96},{1... | collective-permute-start | bytes 737288 | tf_op jit(solution)/shard_map/ppermute | solution.py:255
  47.1 0.0 copy-done.1
  47.1 0.9 %weights.3 = (bf16[576,576]{1,0:T(8,128)(2,1)S(1)}, f32[192,128]{1,0:T(8,128)S(1)}, bf16[576,576]{1,0:T(8,128)(2,1)S(1)}, f32[192,128]{1,0:T(8,128)S(1)}) custom-call(bf16[4,3,3,192,192]{4,3,2,1,0:T(8,128)(2,1)S(1)} %copy-done.1, f32[4,192]{1,0:T(4,128)S(1)} %copy-done.5), custom_call_target="tpu_custom_call" | custom-call | bytes 3000000 | tf_op jit(solution)/shard_map/weights/pallas_call | solution.py:58
  47.9 0.0 collective-permute-done.8.z
  47.9 0.0 collective-permute-done.9.sib
  48.0 2.6 %spatial_b2.1.x0 = bf16[192,640]{1,0:T(8,128)(2,1)S(1)} custom-call(bf16[192,640]{1,0:T(8,128)(2,1)S(1)} %collective-permute-done.8.z, bf16[192,640]{1,0:T(8,128)(2,1)S(1)} %temporal.4.own, bf16[192,640]{1,0:T(8,128)(2,1)S(1)} %collective-permute-done.9.sib, bf16[576,576]{1,0:T(8,128)(2,1)S(1)} %get-tuple-element.27.rest_0_, ...), custom_call_target="tpu_custom_call" | custom-call | flops 1274019840 | bytes 4000000 | tf_op jit(solution)/shard_map/spatial_b2/pallas_call | solution.py:290
  50.5 1.9 %collective-permute-start.10 = (bf16[192,640]{1,0:T(8,128)(2,1)S(1)}, bf16[192,640]{1,0:T(8,128)(2,1)S(1)}, u32[]{:S(2)}, u32[]{:S(2)}) collective-permute-start(bf16[192,640]{1,0:T(8,128)(2,1)S(1)} %spatial_b2.1.x0), channel_id=1, source_target_pairs={{0,32},{16,48},{32,64},{48,80},{64,96},{80,112},{96,128},{112,144}... | collective-permute-start | bytes 737288 | tf_op jit(solution)/shard_map/ppermute | solution.py:261
  52.5 0.0 collective-permute-done.6.z
  52.5 0.0 collective-permute-done.7.sib
  52.5 2.6 %spatial_a2.1.x1.x0 = bf16[192,640]{1,0:T(8,128)(2,1)S(1)} custom-call(bf16[192,640]{1,0:T(8,128)(2,1)S(1)} %collective-permute-done.6.z, bf16[192,640]{1,0:T(8,128)(2,1)S(1)} %temporal.3.own, bf16[192,640]{1,0:T(8,128)(2,1)S(1)} %collective-permute-done.7.sib, bf16[576,576]{1,0:T(8,128)(2,1)S(1)} %get-tuple-element.27.rest_0_, ...), custom_call_target="tpu_custom_call" | custom-call | flops 1274019840 | bytes 4000000 | tf_op jit(solution)/shard_map/spatial_a2/pallas_call | solution.py:292
  55.1 2.5 %collective-permute-start.11 = (bf16[192,640]{1,0:T(8,128)(2,1)S(1)}, bf16[192,640]{1,0:T(8,128)(2,1)S(1)}, u32[]{:S(2)}, u32[]{:S(2)}) collective-permute-start(bf16[192,640]{1,0:T(8,128)(2,1)S(1)} %spatial_a2.1.x1.x0), channel_id=1, source_target_pairs={{0,32},{16,48},{32,64},{48,80},{64,96},{80,112},{96,128},{112,144}... | collective-permute-start | bytes 737288 | tf_op jit(solution)/shard_map/ppermute | solution.py:261
  57.6 4.2 %collective-permute-done.10.x2.x1 = bf16[192,640]{1,0:T(8,128)(2,1)S(1)} collective-permute-done((bf16[192,640]{1,0:T(8,128)(2,1)S(1)}, bf16[192,640]{1,0:T(8,128)(2,1)S(1)}, u32[]{:S(2)}, u32[]{:S(2)}) %collective-permute-start.10) | collective-permute-done | bytes 245792 | tf_op jit(solution)/shard_map/ppermute | solution.py:261
  61.8 0.4 temporal.5.late
  62.2 4.5 %collective-permute-done.11.x2 = bf16[192,640]{1,0:T(8,128)(2,1)S(1)} collective-permute-done((bf16[192,640]{1,0:T(8,128)(2,1)S(1)}, bf16[192,640]{1,0:T(8,128)(2,1)S(1)}, u32[]{:S(2)}, u32[]{:S(2)}) %collective-permute-start.11) | collective-permute-done | bytes 245792 | tf_op jit(solution)/shard_map/ppermute | solution.py:261
  66.8 0.4 temporal_last.1
  67.2 1.5 %collective-permute-start.12 = (bf16[192,640]{1,0:T(8,128)(2,1)S(1)}, bf16[192,640]{1,0:T(8,128)(2,1)S(1)}, u32[]{:S(2)}, u32[]{:S(2)}) collective-permute-start(bf16[192,640]{1,0:T(8,128)(2,1)S(1)} %get-tuple-element.31), channel_id=1, source_target_pairs={{0,16},{16,0},{32,48},{48,32},{64,80},{80,64},{96,112},{112,96},{1... | collective-permute-start | bytes 737288 | tf_op jit(solution)/shard_map/ppermute | solution.py:255
  68.7 0.8 %unpack.2.part = bf16[4,192,320]{2,1,0:T(8,128)(2,1)} custom-call(bf16[192,640]{1,0:T(8,128)(2,1)S(1)} %get-tuple-element.32.keep), custom_call_target="tpu_custom_call" | custom-call | bytes 500000 | tf_op jit(solution)/shard_map/unpack/pallas_call | solution.py:108
  69.5 0.3 collective-permute-done.12.got
  69.8 0.8 %unpack.3 = bf16[4,192,320]{2,1,0:T(8,128)(2,1)} custom-call(bf16[192,640]{1,0:T(8,128)(2,1)S(1)} %collective-permute-done.12.got, bf16[4,192,320]{2,1,0:T(8,128)(2,1)} %unpack.2.part), custom_call_target="tpu_custom_call", output_to_operand_aliasing={{}: (1, {})} | custom-call | bytes 500000 | tf_op jit(solution)/shard_map/unpack/pallas_call | solution.py:108
  (4 shorter events, 0.0 us)
Async XLA Ops:
  0.0 1.1 %copy-start.2 = (bf16[1,4,320,192]{2,3,1,0:T(8,128)(2,1)S(1)}, bf16[1,4,320,192]{2,3,1,0:T(8,128)(2,1)}, u32[]{:S(2)}) copy-start(bf16[1,4,320,192]{2,3,1,0:T(8,128)(2,1)} %param.4) | copy-start | bytes 1474564
  2.1 9.4 %collective-permute-start = (bf16[192,640]{1,0:T(8,128)(2,1)S(1)}, bf16[192,640]{1,0:T(8,128)(2,1)S(1)}, u32[]{:S(2)}, u32[]{:S(2)}) collective-permute-start(bf16[192,640]{1,0:T(8,128)(2,1)S(1)} %get-tuple-element.21.sib0), channel_id=1, source_target_pairs={{0,16},{16,0},{32,48},{48,32},{64,80},{80,64},{96,112},{112,96},{1... | collective-permute-start | bytes 737288 | tf_op jit(solution)/shard_map/ppermute | solution.py:255
  2.9 14.1 %collective-permute-start.2 = (bf16[192,640]{1,0:T(8,128)(2,1)S(1)}, bf16[192,640]{1,0:T(8,128)(2,1)S(1)}, u32[]{:S(2)}, u32[]{:S(2)}) collective-permute-start(bf16[192,640]{1,0:T(8,128)(2,1)S(1)} %get-tuple-element.22.own0), channel_id=1, source_target_pairs={{1,16},{2,17},{3,18},{4,19},{5,20},{6,21},{7,22},{8,23},{9,24},{10... | collective-permute-start | bytes 737288 | tf_op jit(solution)/shard_map/ppermute | solution.py:258
  6.3 10.7 %collective-permute-start.3 = (bf16[192,640]{1,0:T(8,128)(2,1)S(1)}, bf16[192,640]{1,0:T(8,128)(2,1)S(1)}, u32[]{:S(2)}, u32[]{:S(2)}) collective-permute-start(bf16[192,640]{1,0:T(8,128)(2,1)S(1)} %get-tuple-element.22.own0), channel_id=1, source_target_pairs={{0,16},{16,0},{32,48},{48,32},{64,80},{80,64},{96,112},{112,96},{1... | collective-permute-start | bytes 737288 | tf_op jit(solution)/shard_map/ppermute | solution.py:255
  11.5 7.5 %collective-permute-start.1 = (bf16[192,640]{1,0:T(8,128)(2,1)S(1)}, bf16[192,640]{1,0:T(8,128)(2,1)S(1)}, u32[]{:S(2)}, u32[]{:S(2)}) collective-permute-start(bf16[192,640]{1,0:T(8,128)(2,1)S(1)} %collective-permute-done.own1), channel_id=1, source_target_pairs={{1,16},{2,17},{3,18},{4,19},{5,20},{6,21},{7,22},{8,23},{9,24},{10... | collective-permute-start | bytes 737288 | tf_op jit(solution)/shard_map/ppermute | solution.py:258
  13.4 2.0 %copy-start = (bf16[4,3,3,192,192]{4,3,2,1,0:T(8,128)(2,1)S(1)}, bf16[4,3,3,192,192]{4,3,2,1,0:T(8,128)(2,1)}, u32[]{:S(2)}) copy-start(bf16[4,3,3,192,192]{4,3,2,1,0:T(8,128)(2,1)} %sw.3) | copy-start | bytes 7962628
  15.4 0.7 copy-start.4
  19.0 12.2 %copy-start.3 = (bf16[2,3,192,192]{3,2,1,0:T(8,128)(2,1)S(1)}, bf16[2,3,192,192]{3,2,1,0:T(8,128)(2,1)}, u32[]{:S(2)}) copy-start(bf16[2,3,192,192]{3,2,1,0:T(8,128)(2,1)} %tw.1) | copy-start | bytes 1327108
  21.8 25.3 %copy-start.1 = (bf16[4,3,3,192,192]{4,3,2,1,0:T(8,128)(2,1)S(1)}, bf16[4,3,3,192,192]{4,3,2,1,0:T(8,128)(2,1)}, u32[]{:S(2)}) copy-start(bf16[4,3,3,192,192]{4,3,2,1,0:T(8,128)(2,1)} %sw.3) | copy-start | bytes 7962628
  21.8 25.2 %copy-start.5 = (f32[4,192]{1,0:T(4,128)S(1)}, f32[4,192]{1,0:T(4,128)}, u32[]{:S(2)}) copy-start(f32[4,192]{1,0:T(4,128)} %g.3) | copy-start | bytes 9220
  21.8 9.7 %collective-permute-start.4 = (bf16[192,640]{1,0:T(8,128)(2,1)S(1)}, bf16[192,640]{1,0:T(8,128)(2,1)S(1)}, u32[]{:S(2)}, u32[]{:S(2)}) collective-permute-start(bf16[192,640]{1,0:T(8,128)(2,1)S(1)} %spatial_b.1.x0), channel_id=1, source_target_pairs={{0,32},{16,48},{32,64},{48,80},{64,96},{80,112},{96,128},{112,144}... | collective-permute-start | bytes 737288 | tf_op jit(solution)/shard_map/ppermute | solution.py:261
  28.0 11.1 %collective-permute-start.5 = (bf16[192,640]{1,0:T(8,128)(2,1)S(1)}, bf16[192,640]{1,0:T(8,128)(2,1)S(1)}, u32[]{:S(2)}, u32[]{:S(2)}) collective-permute-start(bf16[192,640]{1,0:T(8,128)(2,1)S(1)} %spatial_a.1.x0.x1), channel_id=1, source_target_pairs={{0,32},{16,48},{32,64},{48,80},{64,96},{80,112},{96,128},{112,144}... | collective-permute-start | bytes 737288 | tf_op jit(solution)/shard_map/ppermute | solution.py:261
  31.9 16.0 %collective-permute-start.8 = (bf16[192,640]{1,0:T(8,128)(2,1)S(1)}, bf16[192,640]{1,0:T(8,128)(2,1)S(1)}, u32[]{:S(2)}, u32[]{:S(2)}) collective-permute-start(bf16[192,640]{1,0:T(8,128)(2,1)S(1)} %temporal.4.own), channel_id=1, source_target_pairs={{1,16},{2,17},{3,18},{4,19},{5,20},{6,21},{7,22},{8,23},{9,24},{10... | collective-permute-start | bytes 737288 | tf_op jit(solution)/shard_map/ppermute | solution.py:258
  34.7 13.2 %collective-permute-start.9 = (bf16[192,640]{1,0:T(8,128)(2,1)S(1)}, bf16[192,640]{1,0:T(8,128)(2,1)S(1)}, u32[]{:S(2)}, u32[]{:S(2)}) collective-permute-start(bf16[192,640]{1,0:T(8,128)(2,1)S(1)} %temporal.4.own), channel_id=1, source_target_pairs={{0,16},{16,0},{32,48},{48,32},{64,80},{80,64},{96,112},{112,96},{1... | collective-permute-start | bytes 737288 | tf_op jit(solution)/shard_map/ppermute | solution.py:255
  39.5 13.0 %collective-permute-start.6 = (bf16[192,640]{1,0:T(8,128)(2,1)S(1)}, bf16[192,640]{1,0:T(8,128)(2,1)S(1)}, u32[]{:S(2)}, u32[]{:S(2)}) collective-permute-start(bf16[192,640]{1,0:T(8,128)(2,1)S(1)} %temporal.3.own), channel_id=1, source_target_pairs={{1,16},{2,17},{3,18},{4,19},{5,20},{6,21},{7,22},{8,23},{9,24},{10... | collective-permute-start | bytes 737288 | tf_op jit(solution)/shard_map/ppermute | solution.py:258
  41.4 11.0 %collective-permute-start.7 = (bf16[192,640]{1,0:T(8,128)(2,1)S(1)}, bf16[192,640]{1,0:T(8,128)(2,1)S(1)}, u32[]{:S(2)}, u32[]{:S(2)}) collective-permute-start(bf16[192,640]{1,0:T(8,128)(2,1)S(1)} %temporal.3.own), channel_id=1, source_target_pairs={{0,16},{16,0},{32,48},{48,32},{64,80},{80,64},{96,112},{112,96},{1... | collective-permute-start | bytes 737288 | tf_op jit(solution)/shard_map/ppermute | solution.py:255
  50.5 11.3 %collective-permute-start.10 = (bf16[192,640]{1,0:T(8,128)(2,1)S(1)}, bf16[192,640]{1,0:T(8,128)(2,1)S(1)}, u32[]{:S(2)}, u32[]{:S(2)}) collective-permute-start(bf16[192,640]{1,0:T(8,128)(2,1)S(1)} %spatial_b2.1.x0), channel_id=1, source_target_pairs={{0,32},{16,48},{32,64},{48,80},{64,96},{80,112},{96,128},{112,144}... | collective-permute-start | bytes 737288 | tf_op jit(solution)/shard_map/ppermute | solution.py:261
  55.1 11.7 %collective-permute-start.11 = (bf16[192,640]{1,0:T(8,128)(2,1)S(1)}, bf16[192,640]{1,0:T(8,128)(2,1)S(1)}, u32[]{:S(2)}, u32[]{:S(2)}) collective-permute-start(bf16[192,640]{1,0:T(8,128)(2,1)S(1)} %spatial_a2.1.x1.x0), channel_id=1, source_target_pairs={{0,32},{16,48},{32,64},{48,80},{64,96},{80,112},{96,128},{112,144}... | collective-permute-start | bytes 737288 | tf_op jit(solution)/shard_map/ppermute | solution.py:261
  67.2 2.6 %collective-permute-start.12 = (bf16[192,640]{1,0:T(8,128)(2,1)S(1)}, bf16[192,640]{1,0:T(8,128)(2,1)S(1)}, u32[]{:S(2)}, u32[]{:S(2)}) collective-permute-start(bf16[192,640]{1,0:T(8,128)(2,1)S(1)} %get-tuple-element.31), channel_id=1, source_target_pairs={{0,16},{16,0},{32,48},{48,32},{64,80},{80,64},{96,112},{112,96},{1... | collective-permute-start | bytes 737288 | tf_op jit(solution)/shard_map/ppermute | solution.py:255

commit v3 on v2

--- a/solution.py
+++ b/solution.py
@@ -16,7 +16,7 @@
 BF16 = jnp.bfloat16
 VMEM = pl.BlockSpec(memory_space=pltpu.VMEM)
 ANY = pl.BlockSpec(memory_space=pl.ANY)
-LIMIT = 28 << 20
+LIMIT = 20 << 20
 
 
 def call(kernel, outs, n_in, name, scratch=(), flops=0, moved=0, in_specs=None, out_specs=None, aliases=None):
@@ -44,44 +44,63 @@
     return lax.rem(lax.axis_index("frames"), 2)
 
 
-def weights_kernel(first, sw, g, *outs):
-    for k in range(2):
-        wt, gt = outs[2 * k : 2 * k + 2]
+def weights_kernel(sw, g, tw, w0, w1, w2, w3, g0, g1, g2, g3, t0, t1, held, sems, taps, tap_sems):
+    copies = [
+        pltpu.make_async_copy(sw.at[k, di], held.at[k, di], sems.at[k, di]) for k in range(4) for di in range(3)
+    ]
+    tap_copies = [pltpu.make_async_copy(tw.at[b], taps.at[b], tap_sems.at[b]) for b in range(2)]
+    for copy in copies + tap_copies:
+        copy.start()
+    for k, gt in enumerate((g0, g1, g2, g3)):
+        gt[...] = jnp.broadcast_to(g[k : k + 1, :] * 0.5, (LANES, C)).T
+    for k, wt in enumerate((w0, w1, w2, w3)):
         for di in range(3):
+            copies[3 * k + di].wait()
             for dj in range(3):
-                wt[dj * C : (dj + 1) * C, di * C : (di + 1) * C] = sw[first + k, di, dj].T
-        gt[...] = jnp.broadcast_to(g[first + k : first + k + 1, :] * 0.5, (LANES, C)).T
-
-
-def prepare(weights, gains, first):
-    shapes = [jax.ShapeDtypeStruct((3 * C, 3 * C), BF16), jax.ShapeDtypeStruct((C, LANES), F32)]
-    return call(
-        functools.partial(weights_kernel, first), shapes * 2, 2, "weights", moved=3000000
-    )(weights, gains)
-
-
-def taps_kernel(tw, *outs):
-    for k in range(2):
+                wt[dj * C : (dj + 1) * C, di * C : (di + 1) * C] = held[k, di, dj].T
+    for b, wt in enumerate((t0, t1)):
+        tap_copies[b].wait()
         for tap in range(3):
-            outs[k][:, tap * C : (tap + 1) * C] = tw[k, tap].T
-
-
-def prepare_taps(weights):
-    shape = jax.ShapeDtypeStruct((C, 3 * C), BF16)
-    return call(taps_kernel, [shape] * 2, 1, "taps", moved=1000000)(weights)
-
-
-def pack_kernel(v, own, sib, rows, sems):
+            wt[:, tap * C : (tap + 1) * C] = taps[b, tap].T
+
+
+def in_hbm(x):
+    return pltpu.with_memory_space_constraint(x, pltpu.HBM)
+
+
+def prepare(weights, gains, taps):
+    shape = jax.ShapeDtypeStruct
+    outs = call(
+        weights_kernel,
+        [shape((3 * C, 3 * C), BF16)] * 4 + [shape((C, LANES), F32)] * 4 + [shape((C, 3 * C), BF16)] * 2,
+        3,
+        "weights",
+        scratch=[
+            pltpu.VMEM((4, 3, 3, C, C), BF16),
+            pltpu.SemaphoreType.DMA((4, 3)),
+            pltpu.VMEM((2, 3, C, C), BF16),
+            pltpu.SemaphoreType.DMA((2,)),
+        ],
+        moved=8000000,
+        in_specs=[ANY, VMEM, ANY],
+    )(in_hbm(weights), gains, in_hbm(taps))
+    return outs[:4], outs[4:8], outs[8:]
+
+
+def pack_kernel(v, both, rows, sems):
     core = core_index()
-    order = (2 * core, 2 * core + 1, 2 - 2 * core, 3 - 2 * core)
+    order = (2 - 2 * core, 3 - 2 * core, 2 * core, 2 * core + 1)
     copies = [pltpu.make_async_copy(v.at[order[i]], rows.at[i], sems.at[i]) for i in range(4)]
     for copy in copies:
         copy.start()
-    for i, dst in ((0, own), (2, sib)):
+    for i in range(4):
         copies[i].wait()
-        dst[:, :W] = rows[i]
-        copies[i + 1].wait()
-        dst[:, W:] = rows[i + 1]
+        both[i // 2, :, (i % 2) * W : (i % 2 + 1) * W] = rows[i]
+
+
+def join_kernel(mine, other, owned):
+    owned[0] = mine[1]
+    owned[1] = other[0]
 
 
 def unpack_rows(x, out, rows, sems, pair):
@@ -161,6 +180,90 @@
                 b = jnp.where(lane == W % LANES - 1, 0.0, b)
             out.append(middle[t] + a + b)
     return out
+
+
+def either(first, x, y):
+    return [jnp.where(first, s, t) for s, t in zip(x, y)]
+
+
+def near_body(own, sib, w1, g1, g2, act1, act2, s1):
+    is0 = core_index() == 0
+    gain = g1[...]
+    own = [activate(t, gain, None) for t in own]
+    sib = [activate(t, gain, None) for t in sib]
+    stack(s1, 0, either(is0, own, sib), either(is0, sib, own))
+    gain = g2[...]
+    for t, x in enumerate(convolved(w1, s1)):
+        lanes = slice(t * LANES, (t + 1) * LANES)
+        act1[:, lanes] = own[t]
+        act2[:, lanes] = activate(x.astype(BF16), gain, None)
+
+
+def near_mine_kernel(mine, *rest):
+    near_body(tiles_of(mine.at[1]), tiles_of(mine.at[0]), *rest)
+
+
+def near_other_kernel(other, *rest):
+    near_body(tiles_of(other.at[0]), tiles_of(other.at[1]), *rest)
+
+
+def near(kernel, arrays, w1, g1, g2):
+    return call(
+        kernel,
+        [pair_shape()] * 2,
+        len(arrays) + 3,
+        "near",
+        scratch=[pltpu.VMEM((3 * C, PAIR), BF16)],
+        flops=2 * C * C * 9 * PAIR,
+        moved=2000000,
+    )(*arrays, w1, g1, g2)
+
+
+def far_body(z, own, act1, act2, w1, g1, w2, g2, out, s1, s2):
+    core, row = core_index(), lax.axis_index("rows")
+    is0 = core == 0
+    top = is0 & (row == 0)
+    bottom = (core == 1) & (row == lax.axis_size("rows") - 1)
+    gain = g1[...]
+    z = [activate(t, gain, None) for t in z]
+    stack(s1, 0, either(is0, z, act1), either(is0, act1, z))
+    lane = lax.broadcasted_iota(jnp.int32, (1, LANES), 1)
+    gain = g2[...]
+    far = []
+    for t, x in enumerate(convolved(w1, s1)):
+        pixel = lane + t * LANES
+        outside = ((pixel < W) & top) | ((pixel >= W) & bottom)
+        far.append(activate(x.astype(BF16), gain, jnp.where(outside, 0.0, 1.0).astype(F32)))
+    stack(s2, 0, either(is0, far, act2), either(is0, act2, far))
+    for t, (x, y) in enumerate(zip(own, convolved(w2, s2))):
+        out[:, t * LANES : (t + 1) * LANES] = (x.astype(F32) + y).astype(BF16)
+
+
+def far_pick_kernel(pick, z, mine, other, act1_m, act2_m, act1_o, act2_o, *rest):
+    is_mine = core_index() == pick
+
+    def chosen(x, y):
+        return either(is_mine, tiles_of(x), tiles_of(y))
+
+    far_body(
+        chosen(z.at[1], z.at[0]),
+        chosen(mine.at[1], other.at[0]),
+        chosen(act1_m, act1_o),
+        chosen(act2_m, act2_o),
+        *rest,
+    )
+
+
+def far(kernel, arrays, w1, g1, w2, g2):
+    return call(
+        kernel,
+        pair_shape(),
+        len(arrays) + 4,
+        "far",
+        scratch=[pltpu.VMEM((3 * C, PAIR), BF16)] * 2,
+        flops=2 * C * C * 9 * 2 * PAIR,
+        moved=4000000,
+    )(*arrays, w1, g1, w2, g2)
 
 
 def spatial_body(z, own, sib, w1, g1, w2, g2, out, s1, s2):
@@ -192,15 +295,6 @@
     spatial_body(tiles_of(z), tiles_of(own), tiles_of(sib), *rest)
 
 
-def spatial_pick_kernel(pick, z0, own0, sib0, z1, own1, sib1, *rest):
-    mine = core_index() == pick
-
-    def chosen(x, y):
-        return [jnp.where(mine, s, t) for s, t in zip(tiles_of(x), tiles_of(y))]
-
-    spatial_body(chosen(z0, z1), chosen(own0, own1), chosen(sib0, sib1), *rest)
-
-
 def spatial(kernel, n_in, name):
     return call(
         kernel,
@@ -260,36 +354,36 @@
     def onward(x):
         return lax.ppermute(x, "frames", later)
 
-    view = jnp.transpose(video[0], (0, 2, 1))
-    own_m, sib_m = call(
+    view = in_hbm(jnp.transpose(video[0], (0, 2, 1)))
+    mine = call(
         pack_kernel,
-        [pair_shape()] * 2,
+        jax.ShapeDtypeStruct((2, C, PAIR), BF16),
         1,
         "pack",
         scratch=[pltpu.VMEM((4, C, W), BF16), pltpu.SemaphoreType.DMA((4,))],
         moved=1000000,
-        in_specs=[pl.BlockSpec(memory_space=pltpu.HBM)],
+        in_specs=[ANY],
     )(view)
-    own_o = swap(sib_m)
-    sib_o = swap(own_m)
-    z_o = halo(own_m)
-    z_m = halo(own_o)
-    ts = prepare_taps(temporal_weights)
-    ws = [prepare(spatial_weights, norm_gains, 2 * k) for k in range(2)]
-
-    arrays = (z_m, own_m, sib_m, z_o, own_o, sib_o)
-    inner_b = spatial(functools.partial(spatial_pick_kernel, 1), 10, "spatial_b")(*arrays, *ws[0])
+    other = swap(mine)
+    owned = call(join_kernel, jax.ShapeDtypeStruct((2, C, PAIR), BF16), 2, "join", moved=1000000)(mine, other)
+    z = halo(owned)
+    ws, gs, ts = prepare(spatial_weights, norm_gains, temporal_weights)
+
+    first, both = (ws[0], gs[0], gs[1]), (ws[0], gs[0], ws[1], gs[1])
+    arrays = (z, mine, other, *near(near_mine_kernel, (mine,), *first), *near(near_other_kernel, (other,), *first))
+    inner_b = far(functools.partial(far_pick_kernel, 1), arrays, *both)
     before_b = onward(inner_b)
-    inner_a = spatial(functools.partial(spatial_pick_kernel, 0), 10, "spatial_a")(*arrays, *ws[0])
+    inner_a = far(functools.partial(far_pick_kernel, 0), arrays, *both)
     before_a = onward(inner_a)
+
     own_b = temporal(ts[0], inner_b, inner_a, before_b)
     sib_b, z_b = swap(own_b), halo(own_b)
     own_a = temporal(ts[0], inner_a, before_b, before_a)
     sib_a, z_a = swap(own_a), halo(own_a)
-
-    inner_b = spatial(spatial_kernel, 7, "spatial_b2")(z_b, own_b, sib_b, *ws[1])
+    both = (ws[2], gs[2], ws[3], gs[3])
+    inner_b = spatial(spatial_kernel, 7, "spatial_b")(z_b, own_b, sib_b, *both)
     before_b = onward(inner_b)
-    inner_a = spatial(spatial_kernel, 7, "spatial_a2")(z_a, own_a, sib_a, *ws[1])
+    inner_a = spatial(spatial_kernel, 7, "spatial_a")(z_a, own_a, sib_a, *both)
     before_a = onward(inner_a)
     late = temporal(ts[1], inner_b, inner_a, before_b)
     keep, send = call(temporal_last_kernel, [pair_shape()] * 2, 5, "temporal_last", moved=1500000)(

time: 71.2 us -> 66.7 us (0.937)
  starting transfers between devices: 38.4 us -> 32 us
  Pallas kernels: 17 us -> 20.9 us
  local copies, waits for them, and re-layouts: 3.76 us -> 0.68 us
  waiting for transfers between devices: 11.2 us -> 12.5 us
    ppermute x5 -> x4, starting transfers between devices: 17.5 us -> 13.3 us  [swap(): return lax.ppermute(x, 'frames', swaps)]
    pallas_call x8 -> x9, Pallas kernels: 13.8 us -> 17.7 us  [the longest x2 4.93 us: far(): call(kernel, pair_shape(), len(arrays) + 4, 'far', scratch=[pltpu.VMEM((3...]
    unnamed x12 -> x2, local copies, waits for them, and re-layouts: 3.76 us -> 0.68 us
    ppermute x4 -> x3, starting transfers between devices: 10.1 us -> 8.16 us  [halo(): return lax.ppermute(x, ('frames', 'rows'), across)]
    ppermute x5 -> x4, waiting for transfers between devices: 0.34 us -> 1.83 us  [swap(): return lax.ppermute(x, 'frames', swaps)]
    ppermute x4 -> x3, waiting for transfers between devices: 2.03 us -> 1.23 us  [halo(): return lax.ppermute(x, ('frames', 'rows'), across)]
  transfers between devices with their start and end apart: 13 -> 11, of which waited for: 4 -> 6; matrix products, arithmetic and copies ran while one was open for 0% -> 0% of each run, Pallas kernels for 17% -> 24%
where the time goes in v3:
time: 66.7 us; the launch traced here: 66.4 us
  starting transfers between devices  32 us (48%)
  Pallas kernels  20.9 us (31%)
  waiting for transfers between devices  12.5 us (19%)
  local copies, waits for them, and re-layouts  0.68 us (1%)
    ppermute x4, starting transfers between devices, swap(): return lax.ppermute(x, 'frames', swaps)  13.3 us
    ppermute x4, starting transfers between devices, onward(): return lax.ppermute(x, 'frames', later)  10.6 us
    ppermute x4, waiting for transfers between devices, onward(): return lax.ppermute(x, 'frames', later)  9.4 us
    ppermute x3, starting transfers between devices, halo(): return lax.ppermute(x, ('frames', 'rows'), across)  8.16 us
    pallas_call x2, Pallas kernels, far(): call(kernel, pair_shape(), len(arrays) + 4, 'far', scratch=[pltpu.VMEM((3...  4.93 us
    pallas_call x1, Pallas kernels, prepare(): call(weights_kernel, [shape((3 * C, 3 * C), BF16)] * 4 + [shape((C, LANES...  3.63 us
    pallas_call x2, Pallas kernels, near(): call(kernel, [pair_shape()] * 2, len(arrays) + 3, 'near', scratch=[pltpu....  2.63 us
    pallas_call x1, Pallas kernels, on_device(): inner_a = spatial(spatial_kernel, 7, 'spatial_a')(z_a, own_a, sib_a, *both)  2.59 us
  transfers between devices with their start and end apart: 11, of which 6 were waited for; matrix products, arithmetic and copies ran while one was open for 0% of the time, Pallas kernels for 24%

profile of v3, /device:TPU:25, one launch (start us, length us, event | category | flops | bytes accessed | tf_op | source)
XLA Modules:
  0.0 66.4 jit_solution(12516331142724422997)
XLA Ops:
  0.0 1.3 %pack.1.mine = bf16[2,192,640]{2,1,0:T(8,128)(2,1)S(1)} custom-call(bf16[4,192,320]{2,1,0:T(8,128)(2,1)} %bitcast.6), custom_call_target="tpu_custom_call" | custom-call | bytes 1000000 | tf_op jit(solution)/shard_map/pack/pallas_call | solution.py:358
  1.3 0.8 %collective-permute-start = (bf16[2,192,640]{2,1,0:T(8,128)(2,1)S(1)}, bf16[2,192,640]{2,1,0:T(8,128)(2,1)S(1)}, u32[]{:S(2)}, u32[]{:S(2)}) collective-permute-start(bf16[2,192,640]{2,1,0:T(8,128)(2,1)S(1)} %pack.1.mine), channel_id=1, source_target_pairs={{0,16},{16,0},{32,48},{48,32},{64,80},{80,64},{96,112},{112,96},{1... | collective-permute-start | bytes 1474568 | tf_op jit(solution)/shard_map/ppermute | solution.py:349
  2.0 1.5 %collective-permute-done.other = bf16[2,192,640]{2,1,0:T(8,128)(2,1)S(1)} collective-permute-done((bf16[2,192,640]{2,1,0:T(8,128)(2,1)S(1)}, bf16[2,192,640]{2,1,0:T(8,128)(2,1)S(1)}, u32[]{:S(2)}, u32[]{:S(2)}) %collective-permute-start) | collective-permute-done | bytes 491552 | tf_op jit(solution)/shard_map/ppermute | solution.py:349
  3.6 3.8 %collective-permute-start.1 = (bf16[2,192,640]{2,1,0:T(8,128)(2,1)S(1)}, bf16[2,192,640]{2,1,0:T(8,128)(2,1)S(1)}, u32[]{:S(2)}, u32[]{:S(2)}) collective-permute-start(bf16[2,192,640]{2,1,0:T(8,128)(2,1)S(1)} %join.1), channel_id=1, source_target_pairs={{1,16},{2,17},{3,18},{4,19},{5,20},{6,21},{7,22},{8,23},{9,24},{10... | collective-permute-start | bytes 1474568 | tf_op jit(solution)/shard_map/ppermute | solution.py:352
  7.4 0.0 copy-start
  7.4 0.7 %copy-done = f32[4,192]{1,0:T(4,128)S(1)} copy-done((f32[4,192]{1,0:T(4,128)S(1)}, f32[4,192]{1,0:T(4,128)}, u32[]{:S(2)}) %copy-start) | copy-done | bytes 3096
  8.1 3.6 %weights.1 = (bf16[576,576]{1,0:T(8,128)(2,1)S(1)}, bf16[576,576]{1,0:T(8,128)(2,1)S(1)}, bf16[576,576]{1,0:T(8,128)(2,1)S(1)}, bf16[576,576]{1,0:T(8,128)(2,1)S...) custom-call(bf16[4,3,3,192,192]{4,3,2,1,0:T(8,128)(2,1)} %sw.1, ...), custom_call_target="tpu_custom_call" | custom-call | bytes 8000000 | tf_op jit(solution)/shard_map/weights/pallas_call | solution.py:73
  11.7 1.3 %near.2 = (bf16[192,640]{1,0:T(8,128)(2,1)S(1)}, bf16[192,640]{1,0:T(8,128)(2,1)S(1)}) custom-call(bf16[2,192,640]{2,1,0:T(8,128)(2,1)S(1)} %pack.1.mine, bf16[576,576]{1,0:T(8,128)(2,1)S(1)} %get-tuple-element.23.rest_0_, f32[192,128]{1,0:T(8,128)S(1)} %get-tuple-element.24.rest_1_, f32[192,128]{1,0:T(8,128)S(1)} %get-tuple-element.25.rest_2_.rest_3_), custom_call_target="tpu_custom_call" | custom-call | flops 424673280 | bytes 2000000 | tf_op jit(solution)/shard_map/near/pallas_call | solution.py:211
  13.0 1.3 %near.3 = (bf16[192,640]{1,0:T(8,128)(2,1)S(1)}, bf16[192,640]{1,0:T(8,128)(2,1)S(1)}) custom-call(bf16[2,192,640]{2,1,0:T(8,128)(2,1)S(1)} %collective-permute-done.other, bf16[576,576]{1,0:T(8,128)(2,1)S(1)} %get-tuple-element.23.rest_0_, f32[192,128]{1,0:T(8,128)S(1)} %get-tuple-element.24.rest_1_, f32[192,128]{1,0:T(8,128)S(1)} %get-tuple-element.25.rest_2_.rest_3_), custom_call_target="tpu_custom_call" | custom-call | flops 424673280 | bytes 2000000 | tf_op jit(solution)/shard_map/near/pallas_call | solution.py:211
  14.4 0.0 collective-permute-done.1.z
  14.4 2.5 %far.3.x0 = bf16[192,640]{1,0:T(8,128)(2,1)S(1)} custom-call(bf16[2,192,640]{2,1,0:T(8,128)(2,1)S(1)} %collective-permute-done.1.z, bf16[2,192,640]{2,1,0:T(8,128)(2,1)S(1)} %pack.1.mine, bf16[2,192,640]{2,1,0:T(8,128)(2,1)S(1)} %collective-permute-done.other, bf16[192,640]{1,0:T(8,128)(2,1)S(1)} %get-tuple-element.26.act1_m, ...), custom_call_target="tpu_custom_call" | custom-call | flops 849346560 | bytes 4000000 | tf_op jit(solution)/shard_map/far/pallas_call | solution.py:258
  16.8 3.1 %collective-permute-start.2 = (bf16[192,640]{1,0:T(8,128)(2,1)S(1)}, bf16[192,640]{1,0:T(8,128)(2,1)S(1)}, u32[]{:S(2)}, u32[]{:S(2)}) collective-permute-start(bf16[192,640]{1,0:T(8,128)(2,1)S(1)} %far.3.x0), channel_id=1, source_target_pairs={{0,32},{16,48},{32,64},{48,80},{64,96},{80,112},{96,128},{112,144}... | collective-permute-start | bytes 737288 | tf_op jit(solution)/shard_map/ppermute | solution.py:355
  20.0 2.5 %far.2.x0.x1 = bf16[192,640]{1,0:T(8,128)(2,1)S(1)} custom-call(bf16[2,192,640]{2,1,0:T(8,128)(2,1)S(1)} %collective-permute-done.1.z, bf16[2,192,640]{2,1,0:T(8,128)(2,1)S(1)} %pack.1.mine, bf16[2,192,640]{2,1,0:T(8,128)(2,1)S(1)} %collective-permute-done.other, bf16[192,640]{1,0:T(8,128)(2,1)S(1)} %get-tuple-element.26.act1_m, ...), custom_call_target="tpu_custom_call" | custom-call | flops 849346560 | bytes 4000000 | tf_op jit(solution)/shard_map/far/pallas_call | solution.py:258
  22.4 3.1 %collective-permute-start.3 = (bf16[192,640]{1,0:T(8,128)(2,1)S(1)}, bf16[192,640]{1,0:T(8,128)(2,1)S(1)}, u32[]{:S(2)}, u32[]{:S(2)}) collective-permute-start(bf16[192,640]{1,0:T(8,128)(2,1)S(1)} %far.2.x0.x1), channel_id=1, source_target_pairs={{0,32},{16,48},{32,64},{48,80},{64,96},{80,112},{96,128},{112,144}... | collective-permute-start | bytes 737288 | tf_op jit(solution)/shard_map/ppermute | solution.py:355
  25.6 0.3 collective-permute-done.2.x1.x2
  25.9 0.4 temporal.4.own
  26.3 8.3 %collective-permute-start.7 = (bf16[192,640]{1,0:T(8,128)(2,1)S(1)}, bf16[192,640]{1,0:T(8,128)(2,1)S(1)}, u32[]{:S(2)}, u32[]{:S(2)}) collective-permute-start(bf16[192,640]{1,0:T(8,128)(2,1)S(1)} %temporal.4.own), channel_id=1, source_target_pairs={{0,16},{16,0},{32,48},{48,32},{64,80},{80,64},{96,112},{112,96},{1... | collective-permute-start | bytes 737288 | tf_op jit(solution)/shard_map/ppermute | solution.py:349
  34.6 1.9 %collective-permute-start.6 = (bf16[192,640]{1,0:T(8,128)(2,1)S(1)}, bf16[192,640]{1,0:T(8,128)(2,1)S(1)}, u32[]{:S(2)}, u32[]{:S(2)}) collective-permute-start(bf16[192,640]{1,0:T(8,128)(2,1)S(1)} %temporal.4.own), channel_id=1, source_target_pairs={{1,16},{2,17},{3,18},{4,19},{5,20},{6,21},{7,22},{8,23},{9,24},{10... | collective-permute-start | bytes 737288 | tf_op jit(solution)/shard_map/ppermute | solution.py:352
  36.5 0.0 collective-permute-done.3.x2
  36.5 0.4 temporal.3.own
  36.9 1.5 %collective-permute-start.5 = (bf16[192,640]{1,0:T(8,128)(2,1)S(1)}, bf16[192,640]{1,0:T(8,128)(2,1)S(1)}, u32[]{:S(2)}, u32[]{:S(2)}) collective-permute-start(bf16[192,640]{1,0:T(8,128)(2,1)S(1)} %temporal.3.own), channel_id=1, source_target_pairs={{0,16},{16,0},{32,48},{48,32},{64,80},{80,64},{96,112},{112,96},{1... | collective-permute-start | bytes 737288 | tf_op jit(solution)/shard_map/ppermute | solution.py:349
  38.4 2.4 %collective-permute-start.4 = (bf16[192,640]{1,0:T(8,128)(2,1)S(1)}, bf16[192,640]{1,0:T(8,128)(2,1)S(1)}, u32[]{:S(2)}, u32[]{:S(2)}) collective-permute-start(bf16[192,640]{1,0:T(8,128)(2,1)S(1)} %temporal.3.own), channel_id=1, source_target_pairs={{1,16},{2,17},{3,18},{4,19},{5,20},{6,21},{7,22},{8,23},{9,24},{10... | collective-permute-start | bytes 737288 | tf_op jit(solution)/shard_map/ppermute | solution.py:352
  40.9 0.0 collective-permute-done.7.sib
  40.9 1.2 %collective-permute-done.6.z = bf16[192,640]{1,0:T(8,128)(2,1)S(1)} collective-permute-done((bf16[192,640]{1,0:T(8,128)(2,1)S(1)}, bf16[192,640]{1,0:T(8,128)(2,1)S(1)}, u32[]{:S(2)}, u32[]{:S(2)}) %collective-permute-start.6) | collective-permute-done | bytes 245792 | tf_op jit(solution)/shard_map/ppermute | solution.py:352
  42.1 2.6 %spatial_b.1.x0 = bf16[192,640]{1,0:T(8,128)(2,1)S(1)} custom-call(bf16[192,640]{1,0:T(8,128)(2,1)S(1)} %collective-permute-done.6.z, bf16[192,640]{1,0:T(8,128)(2,1)S(1)} %temporal.4.own, bf16[192,640]{1,0:T(8,128)(2,1)S(1)} %collective-permute-done.7.sib, bf16[576,576]{1,0:T(8,128)(2,1)S(1)} %get-tuple-element.31.rest_0_, ...), custom_call_target="tpu_custom_call" | custom-call | flops 1274019840 | bytes 4000000 | tf_op jit(solution)/shard_map/spatial_b/pallas_call | solution.py:384
  44.7 1.9 %collective-permute-start.8 = (bf16[192,640]{1,0:T(8,128)(2,1)S(1)}, bf16[192,640]{1,0:T(8,128)(2,1)S(1)}, u32[]{:S(2)}, u32[]{:S(2)}) collective-permute-start(bf16[192,640]{1,0:T(8,128)(2,1)S(1)} %spatial_b.1.x0), channel_id=1, source_target_pairs={{0,32},{16,48},{32,64},{48,80},{64,96},{80,112},{96,128},{112,144}... | collective-permute-start | bytes 737288 | tf_op jit(solution)/shard_map/ppermute | solution.py:355
  46.6 0.0 collective-permute-done.5.sib
  46.7 0.0 collective-permute-done.4.z
  46.7 2.6 %spatial_a.1.x1.x0 = bf16[192,640]{1,0:T(8,128)(2,1)S(1)} custom-call(bf16[192,640]{1,0:T(8,128)(2,1)S(1)} %collective-permute-done.4.z, bf16[192,640]{1,0:T(8,128)(2,1)S(1)} %temporal.3.own, bf16[192,640]{1,0:T(8,128)(2,1)S(1)} %collective-permute-done.5.sib, bf16[576,576]{1,0:T(8,128)(2,1)S(1)} %get-tuple-element.31.rest_0_, ...), custom_call_target="tpu_custom_call" | custom-call | flops 1274019840 | bytes 4000000 | tf_op jit(solution)/shard_map/spatial_a/pallas_call | solution.py:386
  49.3 2.4 %collective-permute-start.9 = (bf16[192,640]{1,0:T(8,128)(2,1)S(1)}, bf16[192,640]{1,0:T(8,128)(2,1)S(1)}, u32[]{:S(2)}, u32[]{:S(2)}) collective-permute-start(bf16[192,640]{1,0:T(8,128)(2,1)S(1)} %spatial_a.1.x1.x0), channel_id=1, source_target_pairs={{0,32},{16,48},{32,64},{48,80},{64,96},{80,112},{96,128},{112,144}... | collective-permute-start | bytes 737288 | tf_op jit(solution)/shard_map/ppermute | solution.py:355
  51.7 2.1 %collective-permute-done.8.x2.x1 = bf16[192,640]{1,0:T(8,128)(2,1)S(1)} collective-permute-done((bf16[192,640]{1,0:T(8,128)(2,1)S(1)}, bf16[192,640]{1,0:T(8,128)(2,1)S(1)}, u32[]{:S(2)}, u32[]{:S(2)}) %collective-permute-start.8) | collective-permute-done | bytes 245792 | tf_op jit(solution)/shard_map/ppermute | solution.py:355
  53.8 0.4 temporal.5.late
  54.2 7.0 %collective-permute-done.9.x2 = bf16[192,640]{1,0:T(8,128)(2,1)S(1)} collective-permute-done((bf16[192,640]{1,0:T(8,128)(2,1)S(1)}, bf16[192,640]{1,0:T(8,128)(2,1)S(1)}, u32[]{:S(2)}, u32[]{:S(2)}) %collective-permute-start.9) | collective-permute-done | bytes 245792 | tf_op jit(solution)/shard_map/ppermute | solution.py:355
  61.2 0.4 temporal_last.1
  61.6 2.7 %collective-permute-start.10 = (bf16[192,640]{1,0:T(8,128)(2,1)S(1)}, bf16[192,640]{1,0:T(8,128)(2,1)S(1)}, u32[]{:S(2)}, u32[]{:S(2)}) collective-permute-start(bf16[192,640]{1,0:T(8,128)(2,1)S(1)} %get-tuple-element.35), channel_id=1, source_target_pairs={{0,16},{16,0},{32,48},{48,32},{64,80},{80,64},{96,112},{112,96},{1... | collective-permute-start | bytes 737288 | tf_op jit(solution)/shard_map/ppermute | solution.py:349
  64.3 0.8 %unpack.2.part = bf16[4,192,320]{2,1,0:T(8,128)(2,1)} custom-call(bf16[192,640]{1,0:T(8,128)(2,1)S(1)} %get-tuple-element.36.keep), custom_call_target="tpu_custom_call" | custom-call | bytes 500000 | tf_op jit(solution)/shard_map/unpack/pallas_call | solution.py:127
  65.1 0.3 collective-permute-done.10.got
  65.5 0.8 %unpack.3 = bf16[4,192,320]{2,1,0:T(8,128)(2,1)} custom-call(bf16[192,640]{1,0:T(8,128)(2,1)S(1)} %collective-permute-done.10.got, bf16[4,192,320]{2,1,0:T(8,128)(2,1)} %unpack.2.part), custom_call_target="tpu_custom_call", output_to_operand_aliasing={{}: (1, {})} | custom-call | bytes 500000 | tf_op jit(solution)/shard_map/unpack/pallas_call | solution.py:127
  (1 shorter events, 0.0 us)
Async XLA Ops:
  1.3 2.3 %collective-permute-start = (bf16[2,192,640]{2,1,0:T(8,128)(2,1)S(1)}, bf16[2,192,640]{2,1,0:T(8,128)(2,1)S(1)}, u32[]{:S(2)}, u32[]{:S(2)}) collective-permute-start(bf16[2,192,640]{2,1,0:T(8,128)(2,1)S(1)} %pack.1.mine), channel_id=1, source_target_pairs={{0,16},{16,0},{32,48},{48,32},{64,80},{80,64},{96,112},{112,96},{1... | collective-permute-start | bytes 1474568 | tf_op jit(solution)/shard_map/ppermute | solution.py:349
  3.6 10.8 %collective-permute-start.1 = (bf16[2,192,640]{2,1,0:T(8,128)(2,1)S(1)}, bf16[2,192,640]{2,1,0:T(8,128)(2,1)S(1)}, u32[]{:S(2)}, u32[]{:S(2)}) collective-permute-start(bf16[2,192,640]{2,1,0:T(8,128)(2,1)S(1)} %join.1), channel_id=1, source_target_pairs={{1,16},{2,17},{3,18},{4,19},{5,20},{6,21},{7,22},{8,23},{9,24},{10... | collective-permute-start | bytes 1474568 | tf_op jit(solution)/shard_map/ppermute | solution.py:352
  7.4 0.7 %copy-start = (f32[4,192]{1,0:T(4,128)S(1)}, f32[4,192]{1,0:T(4,128)}, u32[]{:S(2)}) copy-start(f32[4,192]{1,0:T(4,128)} %g.1) | copy-start | bytes 9220
  16.8 9.1 %collective-permute-start.2 = (bf16[192,640]{1,0:T(8,128)(2,1)S(1)}, bf16[192,640]{1,0:T(8,128)(2,1)S(1)}, u32[]{:S(2)}, u32[]{:S(2)}) collective-permute-start(bf16[192,640]{1,0:T(8,128)(2,1)S(1)} %far.3.x0), channel_id=1, source_target_pairs={{0,32},{16,48},{32,64},{48,80},{64,96},{80,112},{96,128},{112,144}... | collective-permute-start | bytes 737288 | tf_op jit(solution)/shard_map/ppermute | solution.py:355
  22.4 14.1 %collective-permute-start.3 = (bf16[192,640]{1,0:T(8,128)(2,1)S(1)}, bf16[192,640]{1,0:T(8,128)(2,1)S(1)}, u32[]{:S(2)}, u32[]{:S(2)}) collective-permute-start(bf16[192,640]{1,0:T(8,128)(2,1)S(1)} %far.2.x0.x1), channel_id=1, source_target_pairs={{0,32},{16,48},{32,64},{48,80},{64,96},{80,112},{96,128},{112,144}... | collective-permute-start | bytes 737288 | tf_op jit(solution)/shard_map/ppermute | solution.py:355
  26.3 14.6 %collective-permute-start.7 = (bf16[192,640]{1,0:T(8,128)(2,1)S(1)}, bf16[192,640]{1,0:T(8,128)(2,1)S(1)}, u32[]{:S(2)}, u32[]{:S(2)}) collective-permute-start(bf16[192,640]{1,0:T(8,128)(2,1)S(1)} %temporal.4.own), channel_id=1, source_target_pairs={{0,16},{16,0},{32,48},{48,32},{64,80},{80,64},{96,112},{112,96},{1... | collective-permute-start | bytes 737288 | tf_op jit(solution)/shard_map/ppermute | solution.py:349
  34.6 7.5 %collective-permute-start.6 = (bf16[192,640]{1,0:T(8,128)(2,1)S(1)}, bf16[192,640]{1,0:T(8,128)(2,1)S(1)}, u32[]{:S(2)}, u32[]{:S(2)}) collective-permute-start(bf16[192,640]{1,0:T(8,128)(2,1)S(1)} %temporal.4.own), channel_id=1, source_target_pairs={{1,16},{2,17},{3,18},{4,19},{5,20},{6,21},{7,22},{8,23},{9,24},{10... | collective-permute-start | bytes 737288 | tf_op jit(solution)/shard_map/ppermute | solution.py:352
  36.9 9.7 %collective-permute-start.5 = (bf16[192,640]{1,0:T(8,128)(2,1)S(1)}, bf16[192,640]{1,0:T(8,128)(2,1)S(1)}, u32[]{:S(2)}, u32[]{:S(2)}) collective-permute-start(bf16[192,640]{1,0:T(8,128)(2,1)S(1)} %temporal.3.own), channel_id=1, source_target_pairs={{0,16},{16,0},{32,48},{48,32},{64,80},{80,64},{96,112},{112,96},{1... | collective-permute-start | bytes 737288 | tf_op jit(solution)/shard_map/ppermute | solution.py:349
  38.4 8.2 %collective-permute-start.4 = (bf16[192,640]{1,0:T(8,128)(2,1)S(1)}, bf16[192,640]{1,0:T(8,128)(2,1)S(1)}, u32[]{:S(2)}, u32[]{:S(2)}) collective-permute-start(bf16[192,640]{1,0:T(8,128)(2,1)S(1)} %temporal.3.own), channel_id=1, source_target_pairs={{1,16},{2,17},{3,18},{4,19},{5,20},{6,21},{7,22},{8,23},{9,24},{10... | collective-permute-start | bytes 737288 | tf_op jit(solution)/shard_map/ppermute | solution.py:352
  44.7 9.1 %collective-permute-start.8 = (bf16[192,640]{1,0:T(8,128)(2,1)S(1)}, bf16[192,640]{1,0:T(8,128)(2,1)S(1)}, u32[]{:S(2)}, u32[]{:S(2)}) collective-permute-start(bf16[192,640]{1,0:T(8,128)(2,1)S(1)} %spatial_b.1.x0), channel_id=1, source_target_pairs={{0,32},{16,48},{32,64},{48,80},{64,96},{80,112},{96,128},{112,144}... | collective-permute-start | bytes 737288 | tf_op jit(solution)/shard_map/ppermute | solution.py:355
  49.3 11.9 %collective-permute-start.9 = (bf16[192,640]{1,0:T(8,128)(2,1)S(1)}, bf16[192,640]{1,0:T(8,128)(2,1)S(1)}, u32[]{:S(2)}, u32[]{:S(2)}) collective-permute-start(bf16[192,640]{1,0:T(8,128)(2,1)S(1)} %spatial_a.1.x1.x0), channel_id=1, source_target_pairs={{0,32},{16,48},{32,64},{48,80},{64,96},{80,112},{96,128},{112,144}... | collective-permute-start | bytes 737288 | tf_op jit(solution)/shard_map/ppermute | solution.py:355
  61.6 3.9 %collective-permute-start.10 = (bf16[192,640]{1,0:T(8,128)(2,1)S(1)}, bf16[192,640]{1,0:T(8,128)(2,1)S(1)}, u32[]{:S(2)}, u32[]{:S(2)}) collective-permute-start(bf16[192,640]{1,0:T(8,128)(2,1)S(1)} %get-tuple-element.35), channel_id=1, source_target_pairs={{0,16},{16,0},{32,48},{48,32},{64,80},{80,64},{96,112},{112,96},{1... | collective-permute-start | bytes 737288 | tf_op jit(solution)/shard_map/ppermute | solution.py:349

commit v4 on v3

--- a/solution.py
+++ b/solution.py
@@ -44,22 +44,32 @@
     return lax.rem(lax.axis_index("frames"), 2)
 
 
-def weights_kernel(sw, g, tw, w0, w1, w2, w3, g0, g1, g2, g3, t0, t1, held, sems, taps, tap_sems):
-    copies = [
-        pltpu.make_async_copy(sw.at[k, di], held.at[k, di], sems.at[k, di]) for k in range(4) for di in range(3)
-    ]
-    tap_copies = [pltpu.make_async_copy(tw.at[b], taps.at[b], tap_sems.at[b]) for b in range(2)]
-    for copy in copies + tap_copies:
+def gain_column(g, k):
+    return jnp.broadcast_to(g[k : k + 1, :] * 0.5, (LANES, C)).T
+
+
+def transpose_taps(source, wt):
+    for di in range(3):
+        for dj in range(3):
+            wt[dj * C : (dj + 1) * C, di * C : (di + 1) * C] = source[di, dj].T
+
+
+def weights_kernel(sw, g, tw, w0, w1, w2, w3, g0, g1, g2, g3, t0, t1, held, taps, gains, sems, more_sems):
+    gain_copy = pltpu.make_async_copy(g, gains, more_sems.at[0])
+    tap_copy = pltpu.make_async_copy(tw, taps, more_sems.at[1])
+    copies = [pltpu.make_async_copy(sw.at[k], held.at[k], sems.at[k]) for k in range(4)]
+    gain_copy.start()
+    for copy in copies:
         copy.start()
+    tap_copy.start()
+    gain_copy.wait()
     for k, gt in enumerate((g0, g1, g2, g3)):
-        gt[...] = jnp.broadcast_to(g[k : k + 1, :] * 0.5, (LANES, C)).T
+        gt[...] = gain_column(gains, k)
     for k, wt in enumerate((w0, w1, w2, w3)):
-        for di in range(3):
-            copies[3 * k + di].wait()
-            for dj in range(3):
-                wt[dj * C : (dj + 1) * C, di * C : (di + 1) * C] = held[k, di, dj].T
+        copies[k].wait()
+        transpose_taps(held.at[k], wt)
+    tap_copy.wait()
     for b, wt in enumerate((t0, t1)):
-        tap_copies[b].wait()
         for tap in range(3):
             wt[:, tap * C : (tap + 1) * C] = taps[b, tap].T
 
@@ -77,13 +87,14 @@
         "weights",
         scratch=[
             pltpu.VMEM((4, 3, 3, C, C), BF16),
-            pltpu.SemaphoreType.DMA((4, 3)),
             pltpu.VMEM((2, 3, C, C), BF16),
+            pltpu.VMEM((4, C), F32),
+            pltpu.SemaphoreType.DMA((4,)),
             pltpu.SemaphoreType.DMA((2,)),
         ],
-        moved=8000000,
-        in_specs=[ANY, VMEM, ANY],
-    )(in_hbm(weights), gains, in_hbm(taps))
+        moved=6000000,
+        in_specs=[ANY] * 3,
+    )(in_hbm(weights), in_hbm(gains), in_hbm(taps))
     return outs[:4], outs[4:8], outs[8:]
 
 
@@ -199,24 +210,20 @@
         act2[:, lanes] = activate(x.astype(BF16), gain, None)
 
 
-def near_mine_kernel(mine, *rest):
-    near_body(tiles_of(mine.at[1]), tiles_of(mine.at[0]), *rest)
-
-
-def near_other_kernel(other, *rest):
-    near_body(tiles_of(other.at[0]), tiles_of(other.at[1]), *rest)
-
-
-def near(kernel, arrays, w1, g1, g2):
+def near_kernel(which, pairs, *rest):
+    near_body(tiles_of(pairs.at[which]), tiles_of(pairs.at[1 - which]), *rest)
+
+
+def near(which, pairs, w1, g1, g2):
     return call(
-        kernel,
+        functools.partial(near_kernel, which),
         [pair_shape()] * 2,
-        len(arrays) + 3,
+        4,
         "near",
         scratch=[pltpu.VMEM((3 * C, PAIR), BF16)],
         flops=2 * C * C * 9 * PAIR,
         moved=2000000,
-    )(*arrays, w1, g1, g2)
+    )(pairs, w1, g1, g2)
 
 
 def far_body(z, own, act1, act2, w1, g1, w2, g2, out, s1, s2):
@@ -239,7 +246,7 @@
         out[:, t * LANES : (t + 1) * LANES] = (x.astype(F32) + y).astype(BF16)
 
 
-def far_pick_kernel(pick, z, mine, other, act1_m, act2_m, act1_o, act2_o, *rest):
+def far_pick_kernel(pick, z, owned, act1_m, act2_m, act1_o, act2_o, *rest):
     is_mine = core_index() == pick
 
     def chosen(x, y):
@@ -247,7 +254,7 @@
 
     far_body(
         chosen(z.at[1], z.at[0]),
-        chosen(mine.at[1], other.at[0]),
+        chosen(owned.at[0], owned.at[1]),
         chosen(act1_m, act1_o),
         chosen(act2_m, act2_o),
         *rest,
@@ -326,8 +333,19 @@
     )(wt, x0, x1, x2)
 
 
-def temporal_last_kernel(wt, x0, x1, x2, late, keep, send):
-    early = mixed(wt, x0, x1, x2)
+def temporal_late_kernel(wt, x0, x1, x2, y0, out, part):
+    out[...] = mixed(wt, x0, x1, x2)
+    total = y0[...].astype(F32)
+    for tap, y in enumerate((y0, x2)):
+        total = total + jnp.dot(
+            wt[:, tap * C : (tap + 1) * C], y[...], preferred_element_type=F32
+        )
+    part[...] = total
+
+
+def temporal_last_kernel(wt, part, y2, late, keep, send):
+    early = part[...] + jnp.dot(wt[:, 2 * C :], y2[...], preferred_element_type=F32)
+    early = early.astype(BF16)
     is0 = core_index() == 0
     other = late[...]
     keep[...] = jnp.where(is0, early, other)
@@ -365,29 +383,36 @@
         in_specs=[ANY],
     )(view)
     other = swap(mine)
-    owned = call(join_kernel, jax.ShapeDtypeStruct((2, C, PAIR), BF16), 2, "join", moved=1000000)(mine, other)
+    owned = call(join_kernel, jax.ShapeDtypeStruct((2, C, PAIR), BF16), 2, "join", moved=1000)(mine, other)
     z = halo(owned)
-    ws, gs, ts = prepare(spatial_weights, norm_gains, temporal_weights)
-
-    first, both = (ws[0], gs[0], gs[1]), (ws[0], gs[0], ws[1], gs[1])
-    arrays = (z, mine, other, *near(near_mine_kernel, (mine,), *first), *near(near_other_kernel, (other,), *first))
-    inner_b = far(functools.partial(far_pick_kernel, 1), arrays, *both)
+    (w0, w1, w2, w3), (g0, g1, g2, g3), ts = prepare(spatial_weights, norm_gains, temporal_weights)
+
+    near_m = near(1, mine, w0, g0, g1)
+    near_o = near(0, other, w0, g0, g1)
+    arrays = (z, owned, *near_m, *near_o)
+    inner_b = far(functools.partial(far_pick_kernel, 1), arrays, w0, g0, w1, g1)
     before_b = onward(inner_b)
-    inner_a = far(functools.partial(far_pick_kernel, 0), arrays, *both)
+    inner_a = far(functools.partial(far_pick_kernel, 0), arrays, w0, g0, w1, g1)
     before_a = onward(inner_a)
 
     own_b = temporal(ts[0], inner_b, inner_a, before_b)
-    sib_b, z_b = swap(own_b), halo(own_b)
+    z_b, sib_b = halo(own_b), swap(own_b)
     own_a = temporal(ts[0], inner_a, before_b, before_a)
-    sib_a, z_a = swap(own_a), halo(own_a)
-    both = (ws[2], gs[2], ws[3], gs[3])
+    z_a, sib_a = halo(own_a), swap(own_a)
+    both = (w2, g2, w3, g3)
     inner_b = spatial(spatial_kernel, 7, "spatial_b")(z_b, own_b, sib_b, *both)
     before_b = onward(inner_b)
     inner_a = spatial(spatial_kernel, 7, "spatial_a")(z_a, own_a, sib_a, *both)
     before_a = onward(inner_a)
-    late = temporal(ts[1], inner_b, inner_a, before_b)
-    keep, send = call(temporal_last_kernel, [pair_shape()] * 2, 5, "temporal_last", moved=1500000)(
-        ts[1], inner_a, before_b, before_a, late
+    late, part = call(
+        temporal_late_kernel,
+        [pair_shape(), jax.ShapeDtypeStruct((C, PAIR), F32)],
+        5,
+        "temporal_late",
+        moved=2000000,
+    )(ts[1], inner_b, inner_a, before_b, inner_a)
+    keep, send = call(temporal_last_kernel, [pair_shape()] * 2, 4, "temporal_last", moved=1500000)(
+        ts[1], part, before_a, late
     )
     got = swap(send)
     out = unpack(unpack_got_kernel, got, unpack(unpack_keep_kernel, keep))

time: 66.7 us -> 65.7 us (0.985)
  local copies, waits for them, and re-layouts: 0.68 us -> 0 us
    unnamed x2 -> x0, local copies, waits for them, and re-layouts: 0.68 us -> none
    pallas_call x3 -> x4, Pallas kernels: 3.04 us -> 3.42 us  [the longest x2 2.63 us: near(): call(functools.partial(near_kernel, which), [pair_shape()] * 2, 4, 'near'...]
  transfers between devices with their start and end apart: 11 -> 11, of which waited for: 6 -> 8; matrix products, arithmetic and copies ran while one was open for 0% -> 0% of each run, Pallas kernels for 24% -> 24%
where the time goes in v4:
time: 65.7 us; the launch traced here: 65.4 us
  starting transfers between devices  31.9 us (49%)
  Pallas kernels  20.6 us (31%)
  waiting for transfers between devices  12.6 us (19%)
    ppermute x4, starting transfers between devices, swap(): return lax.ppermute(x, 'frames', swaps)  13.4 us
    ppermute x4, starting transfers between devices, onward(): return lax.ppermute(x, 'frames', later)  10.7 us
    ppermute x4, waiting for transfers between devices, onward(): return lax.ppermute(x, 'frames', later)  9.17 us
    ppermute x3, starting transfers between devices, halo(): return lax.ppermute(x, ('frames', 'rows'), across)  7.8 us
    pallas_call x2, Pallas kernels, far(): call(kernel, pair_shape(), len(arrays) + 4, 'far', scratch=[pltpu.VMEM((3...  4.89 us
    pallas_call x1, Pallas kernels, prepare(): call(weights_kernel, [shape((3 * C, 3 * C), BF16)] * 4 + [shape((C, LANES...  3.47 us
    pallas_call x2, Pallas kernels, near(): call(functools.partial(near_kernel, which), [pair_shape()] * 2, 4, 'near'...  2.63 us
    pallas_call x1, Pallas kernels, on_device(): inner_a = spatial(spatial_kernel, 7, 'spatial_a')(z_a, own_a, sib_a, *both)  2.58 us
  transfers between devices with their start and end apart: 11, of which 8 were waited for; matrix products, arithmetic and copies ran while one was open for 0% of the time, Pallas kernels for 24%

profile of v4, /device:TPU:25, one launch (start us, length us, event | category | flops | bytes accessed | tf_op | source)
XLA Modules:
  0.0 65.4 jit_solution(13105242252340493865)
XLA Ops:
  0.0 1.3 %pack.1.mine.pairs = bf16[2,192,640]{2,1,0:T(8,128)(2,1)S(1)} custom-call(bf16[4,192,320]{2,1,0:T(8,128)(2,1)} %bitcast.6), custom_call_target="tpu_custom_call" | custom-call | bytes 1000000 | tf_op jit(solution)/shard_map/pack/pallas_call | solution.py:376
  1.3 0.8 %collective-permute-start = (bf16[2,192,640]{2,1,0:T(8,128)(2,1)S(1)}, bf16[2,192,640]{2,1,0:T(8,128)(2,1)S(1)}, u32[]{:S(2)}, u32[]{:S(2)}) collective-permute-start(bf16[2,192,640]{2,1,0:T(8,128)(2,1)S(1)} %pack.1.mine.pairs), channel_id=1, source_target_pairs={{0,16},{16,0},{32,48},{48,32},{64,80},{80,64},{96,112},{112,96},{1... | collective-permute-start | bytes 1474568 | tf_op jit(solution)/shard_map/ppermute | solution.py:367
  2.0 1.5 %collective-permute-done.other.pairs = bf16[2,192,640]{2,1,0:T(8,128)(2,1)S(1)} collective-permute-done((bf16[2,192,640]{2,1,0:T(8,128)(2,1)S(1)}, bf16[2,192,640]{2,1,0:T(8,128)(2,1)S(1)}, u32[]{:S(2)}, u32[]{:S(2)}) %collective-permute-start) | collective-permute-done | bytes 491552 | tf_op jit(solution)/shard_map/ppermute | solution.py:367
  3.6 3.8 %collective-permute-start.1 = (bf16[2,192,640]{2,1,0:T(8,128)(2,1)S(1)}, bf16[2,192,640]{2,1,0:T(8,128)(2,1)S(1)}, u32[]{:S(2)}, u32[]{:S(2)}) collective-permute-start(bf16[2,192,640]{2,1,0:T(8,128)(2,1)S(1)} %join.1.owned), channel_id=1, source_target_pairs={{1,16},{2,17},{3,18},{4,19},{5,20},{6,21},{7,22},{8,23},{9,24},{10... | collective-permute-start | bytes 1474568 | tf_op jit(solution)/shard_map/ppermute | solution.py:370
  7.4 3.5 %weights.1 = (bf16[576,576]{1,0:T(8,128)(2,1)S(1)}, bf16[576,576]{1,0:T(8,128)(2,1)S(1)}, bf16[576,576]{1,0:T(8,128)(2,1)S(1)}, bf16[576,576]{1,0:T(8,128)(2,1)S...) custom-call(bf16[4,3,3,192,192]{4,3,2,1,0:T(8,128)(2,1)} %sw.1, ...), custom_call_target="tpu_custom_call" | custom-call | bytes 6000000 | tf_op jit(solution)/shard_map/weights/pallas_call | solution.py:83
  10.9 1.3 %near.2 = (bf16[192,640]{1,0:T(8,128)(2,1)S(1)}, bf16[192,640]{1,0:T(8,128)(2,1)S(1)}) custom-call(bf16[2,192,640]{2,1,0:T(8,128)(2,1)S(1)} %pack.1.mine.pairs, bf16[576,576]{1,0:T(8,128)(2,1)S(1)} %get-tuple-element.25.rest_0_, f32[192,128]{1,0:T(8,128)S(1)} %get-tuple-element.26.rest_1_, f32[192,128]{1,0:T(8,128)S(1)} %get-tuple-element.27.rest_2_.rest_3_), custom_call_target="tpu_custom_call" | custom-call | flops 424673280 | bytes 2000000 | tf_op jit(solution)/shard_map/near/pallas_call | solution.py:218
  12.2 1.3 %near.3 = (bf16[192,640]{1,0:T(8,128)(2,1)S(1)}, bf16[192,640]{1,0:T(8,128)(2,1)S(1)}) custom-call(bf16[2,192,640]{2,1,0:T(8,128)(2,1)S(1)} %collective-permute-done.other.pairs, bf16[576,576]{1,0:T(8,128)(2,1)S(1)} %get-tuple-element.25.rest_0_, f32[192,128]{1,0:T(8,128)S(1)} %get-tuple-element.26.rest_1_, f32[192,128]{1,0:T(8,128)S(1)} %get-tuple-element.27.rest_2_.rest_3_), custom_call_target="tpu_custom_call" | custom-call | flops 424673280 | bytes 2000000 | tf_op jit(solution)/shard_map/near/pallas_call | solution.py:218
  13.5 0.7 %collective-permute-done.1.z = bf16[2,192,640]{2,1,0:T(8,128)(2,1)S(1)} collective-permute-done((bf16[2,192,640]{2,1,0:T(8,128)(2,1)S(1)}, bf16[2,192,640]{2,1,0:T(8,128)(2,1)S(1)}, u32[]{:S(2)}, u32[]{:S(2)}) %collective-permute-start.1) | collective-permute-done | bytes 491552 | tf_op jit(solution)/shard_map/ppermute | solution.py:370
  14.2 2.4 %far.2.x0 = bf16[192,640]{1,0:T(8,128)(2,1)S(1)} custom-call(bf16[2,192,640]{2,1,0:T(8,128)(2,1)S(1)} %collective-permute-done.1.z, bf16[2,192,640]{2,1,0:T(8,128)(2,1)S(1)} %join.1.owned, bf16[192,640]{1,0:T(8,128)(2,1)S(1)} %get-tuple-element.28.act1_m, bf16[192,640]{1,0:T(8,128)(2,1)S(1)} %get-tuple-element.29.act2_m, ...), custom_call_target="tpu_custom_call" | custom-call | flops 849346560 | bytes 4000000 | tf_op jit(solution)/shard_map/far/pallas_call | solution.py:265
  16.6 3.1 %collective-permute-start.2 = (bf16[192,640]{1,0:T(8,128)(2,1)S(1)}, bf16[192,640]{1,0:T(8,128)(2,1)S(1)}, u32[]{:S(2)}, u32[]{:S(2)}) collective-permute-start(bf16[192,640]{1,0:T(8,128)(2,1)S(1)} %far.2.x0), channel_id=1, source_target_pairs={{0,32},{16,48},{32,64},{48,80},{64,96},{80,112},{96,128},{112,144}... | collective-permute-start | bytes 737288 | tf_op jit(solution)/shard_map/ppermute | solution.py:373
  19.8 2.4 %far.3.x1.x0 = bf16[192,640]{1,0:T(8,128)(2,1)S(1)} custom-call(bf16[2,192,640]{2,1,0:T(8,128)(2,1)S(1)} %collective-permute-done.1.z, bf16[2,192,640]{2,1,0:T(8,128)(2,1)S(1)} %join.1.owned, bf16[192,640]{1,0:T(8,128)(2,1)S(1)} %get-tuple-element.28.act1_m, bf16[192,640]{1,0:T(8,128)(2,1)S(1)} %get-tuple-element.29.act2_m, ...), custom_call_target="tpu_custom_call" | custom-call | flops 849346560 | bytes 4000000 | tf_op jit(solution)/shard_map/far/pallas_call | solution.py:265
  22.2 3.1 %collective-permute-start.5 = (bf16[192,640]{1,0:T(8,128)(2,1)S(1)}, bf16[192,640]{1,0:T(8,128)(2,1)S(1)}, u32[]{:S(2)}, u32[]{:S(2)}) collective-permute-start(bf16[192,640]{1,0:T(8,128)(2,1)S(1)} %far.3.x1.x0), channel_id=1, source_target_pairs={{0,32},{16,48},{32,64},{48,80},{64,96},{80,112},{96,128},{112,144}... | collective-permute-start | bytes 737288 | tf_op jit(solution)/shard_map/ppermute | solution.py:373
  25.3 0.3 collective-permute-done.2.x2.x1
  25.7 0.4 temporal.2.own
  26.1 7.7 %collective-permute-start.4 = (bf16[192,640]{1,0:T(8,128)(2,1)S(1)}, bf16[192,640]{1,0:T(8,128)(2,1)S(1)}, u32[]{:S(2)}, u32[]{:S(2)}) collective-permute-start(bf16[192,640]{1,0:T(8,128)(2,1)S(1)} %temporal.2.own), channel_id=1, source_target_pairs={{0,16},{16,0},{32,48},{48,32},{64,80},{80,64},{96,112},{112,96},{1... | collective-permute-start | bytes 737288 | tf_op jit(solution)/shard_map/ppermute | solution.py:367
  33.8 1.9 %collective-permute-start.3 = (bf16[192,640]{1,0:T(8,128)(2,1)S(1)}, bf16[192,640]{1,0:T(8,128)(2,1)S(1)}, u32[]{:S(2)}, u32[]{:S(2)}) collective-permute-start(bf16[192,640]{1,0:T(8,128)(2,1)S(1)} %temporal.2.own), channel_id=1, source_target_pairs={{1,16},{2,17},{3,18},{4,19},{5,20},{6,21},{7,22},{8,23},{9,24},{10... | collective-permute-start | bytes 737288 | tf_op jit(solution)/shard_map/ppermute | solution.py:370
  35.7 0.0 collective-permute-done.5.x2
  35.7 0.4 temporal.3.own
  36.1 2.3 %collective-permute-start.7 = (bf16[192,640]{1,0:T(8,128)(2,1)S(1)}, bf16[192,640]{1,0:T(8,128)(2,1)S(1)}, u32[]{:S(2)}, u32[]{:S(2)}) collective-permute-start(bf16[192,640]{1,0:T(8,128)(2,1)S(1)} %temporal.3.own), channel_id=1, source_target_pairs={{0,16},{16,0},{32,48},{48,32},{64,80},{80,64},{96,112},{112,96},{1... | collective-permute-start | bytes 737288 | tf_op jit(solution)/shard_map/ppermute | solution.py:367
  38.4 2.1 %collective-permute-start.6 = (bf16[192,640]{1,0:T(8,128)(2,1)S(1)}, bf16[192,640]{1,0:T(8,128)(2,1)S(1)}, u32[]{:S(2)}, u32[]{:S(2)}) collective-permute-start(bf16[192,640]{1,0:T(8,128)(2,1)S(1)} %temporal.3.own), channel_id=1, source_target_pairs={{1,16},{2,17},{3,18},{4,19},{5,20},{6,21},{7,22},{8,23},{9,24},{10... | collective-permute-start | bytes 737288 | tf_op jit(solution)/shard_map/ppermute | solution.py:370
  40.5 0.0 collective-permute-done.4.sib
  40.5 0.8 %collective-permute-done.3.z = bf16[192,640]{1,0:T(8,128)(2,1)S(1)} collective-permute-done((bf16[192,640]{1,0:T(8,128)(2,1)S(1)}, bf16[192,640]{1,0:T(8,128)(2,1)S(1)}, u32[]{:S(2)}, u32[]{:S(2)}) %collective-permute-start.3) | collective-permute-done | bytes 245792 | tf_op jit(solution)/shard_map/ppermute | solution.py:370
  41.3 2.6 %spatial_b.1.x0 = bf16[192,640]{1,0:T(8,128)(2,1)S(1)} custom-call(bf16[192,640]{1,0:T(8,128)(2,1)S(1)} %collective-permute-done.3.z, bf16[192,640]{1,0:T(8,128)(2,1)S(1)} %temporal.2.own, bf16[192,640]{1,0:T(8,128)(2,1)S(1)} %collective-permute-done.4.sib, bf16[576,576]{1,0:T(8,128)(2,1)S(1)} %get-tuple-element.33.rest_0_, ...), custom_call_target="tpu_custom_call" | custom-call | flops 1274019840 | bytes 4000000 | tf_op jit(solution)/shard_map/spatial_b/pallas_call | solution.py:403
  43.9 1.9 %collective-permute-start.8 = (bf16[192,640]{1,0:T(8,128)(2,1)S(1)}, bf16[192,640]{1,0:T(8,128)(2,1)S(1)}, u32[]{:S(2)}, u32[]{:S(2)}) collective-permute-start(bf16[192,640]{1,0:T(8,128)(2,1)S(1)} %spatial_b.1.x0), channel_id=1, source_target_pairs={{0,32},{16,48},{32,64},{48,80},{64,96},{80,112},{96,128},{112,144}... | collective-permute-start | bytes 737288 | tf_op jit(solution)/shard_map/ppermute | solution.py:373
  45.8 0.0 collective-permute-done.7.sib
  45.8 0.1 collective-permute-done.6.z
  45.9 2.6 %spatial_a.1.x1.y0 = bf16[192,640]{1,0:T(8,128)(2,1)S(1)} custom-call(bf16[192,640]{1,0:T(8,128)(2,1)S(1)} %collective-permute-done.6.z, bf16[192,640]{1,0:T(8,128)(2,1)S(1)} %temporal.3.own, bf16[192,640]{1,0:T(8,128)(2,1)S(1)} %collective-permute-done.7.sib, bf16[576,576]{1,0:T(8,128)(2,1)S(1)} %get-tuple-element.33.rest_0_, ...), custom_call_target="tpu_custom_call" | custom-call | flops 1274019840 | bytes 4000000 | tf_op jit(solution)/shard_map/spatial_a/pallas_call | solution.py:405
  48.5 2.5 %collective-permute-start.9 = (bf16[192,640]{1,0:T(8,128)(2,1)S(1)}, bf16[192,640]{1,0:T(8,128)(2,1)S(1)}, u32[]{:S(2)}, u32[]{:S(2)}) collective-permute-start(bf16[192,640]{1,0:T(8,128)(2,1)S(1)} %spatial_a.1.x1.y0), channel_id=1, source_target_pairs={{0,32},{16,48},{32,64},{48,80},{64,96},{80,112},{96,128},{112,144}... | collective-permute-start | bytes 737288 | tf_op jit(solution)/shard_map/ppermute | solution.py:373
  51.0 1.9 %collective-permute-done.8.x2 = bf16[192,640]{1,0:T(8,128)(2,1)S(1)} collective-permute-done((bf16[192,640]{1,0:T(8,128)(2,1)S(1)}, bf16[192,640]{1,0:T(8,128)(2,1)S(1)}, u32[]{:S(2)}, u32[]{:S(2)}) %collective-permute-start.8) | collective-permute-done | bytes 245792 | tf_op jit(solution)/shard_map/ppermute | solution.py:373
  52.9 0.6 temporal_late.1
  53.5 6.9 %collective-permute-done.9.y2 = bf16[192,640]{1,0:T(8,128)(2,1)S(1)} collective-permute-done((bf16[192,640]{1,0:T(8,128)(2,1)S(1)}, bf16[192,640]{1,0:T(8,128)(2,1)S(1)}, u32[]{:S(2)}, u32[]{:S(2)}) %collective-permute-start.9) | collective-permute-done | bytes 245792 | tf_op jit(solution)/shard_map/ppermute | solution.py:373
  60.4 0.2 temporal_last.1
  60.6 2.7 %collective-permute-start.10 = (bf16[192,640]{1,0:T(8,128)(2,1)S(1)}, bf16[192,640]{1,0:T(8,128)(2,1)S(1)}, u32[]{:S(2)}, u32[]{:S(2)}) collective-permute-start(bf16[192,640]{1,0:T(8,128)(2,1)S(1)} %get-tuple-element.39), channel_id=1, source_target_pairs={{0,16},{16,0},{32,48},{48,32},{64,80},{80,64},{96,112},{112,96},{1... | collective-permute-start | bytes 737288 | tf_op jit(solution)/shard_map/ppermute | solution.py:367
  63.3 0.8 %unpack.2.part = bf16[4,192,320]{2,1,0:T(8,128)(2,1)} custom-call(bf16[192,640]{1,0:T(8,128)(2,1)S(1)} %get-tuple-element.40.keep), custom_call_target="tpu_custom_call" | custom-call | bytes 500000 | tf_op jit(solution)/shard_map/unpack/pallas_call | solution.py:138
  64.1 0.3 collective-permute-done.10.got
  64.4 0.8 %unpack.3 = bf16[4,192,320]{2,1,0:T(8,128)(2,1)} custom-call(bf16[192,640]{1,0:T(8,128)(2,1)S(1)} %collective-permute-done.10.got, bf16[4,192,320]{2,1,0:T(8,128)(2,1)} %unpack.2.part), custom_call_target="tpu_custom_call", output_to_operand_aliasing={{}: (1, {})} | custom-call | bytes 500000 | tf_op jit(solution)/shard_map/unpack/pallas_call | solution.py:138
  (1 shorter events, 0.0 us)
Async XLA Ops:
  1.3 2.3 %collective-permute-start = (bf16[2,192,640]{2,1,0:T(8,128)(2,1)S(1)}, bf16[2,192,640]{2,1,0:T(8,128)(2,1)S(1)}, u32[]{:S(2)}, u32[]{:S(2)}) collective-permute-start(bf16[2,192,640]{2,1,0:T(8,128)(2,1)S(1)} %pack.1.mine.pairs), channel_id=1, source_target_pairs={{0,16},{16,0},{32,48},{48,32},{64,80},{80,64},{96,112},{112,96},{1... | collective-permute-start | bytes 1474568 | tf_op jit(solution)/shard_map/ppermute | solution.py:367
  3.6 10.6 %collective-permute-start.1 = (bf16[2,192,640]{2,1,0:T(8,128)(2,1)S(1)}, bf16[2,192,640]{2,1,0:T(8,128)(2,1)S(1)}, u32[]{:S(2)}, u32[]{:S(2)}) collective-permute-start(bf16[2,192,640]{2,1,0:T(8,128)(2,1)S(1)} %join.1.owned), channel_id=1, source_target_pairs={{1,16},{2,17},{3,18},{4,19},{5,20},{6,21},{7,22},{8,23},{9,24},{10... | collective-permute-start | bytes 1474568 | tf_op jit(solution)/shard_map/ppermute | solution.py:370
  16.6 9.1 %collective-permute-start.2 = (bf16[192,640]{1,0:T(8,128)(2,1)S(1)}, bf16[192,640]{1,0:T(8,128)(2,1)S(1)}, u32[]{:S(2)}, u32[]{:S(2)}) collective-permute-start(bf16[192,640]{1,0:T(8,128)(2,1)S(1)} %far.2.x0), channel_id=1, source_target_pairs={{0,32},{16,48},{32,64},{48,80},{64,96},{80,112},{96,128},{112,144}... | collective-permute-start | bytes 737288 | tf_op jit(solution)/shard_map/ppermute | solution.py:373
  22.2 13.5 %collective-permute-start.5 = (bf16[192,640]{1,0:T(8,128)(2,1)S(1)}, bf16[192,640]{1,0:T(8,128)(2,1)S(1)}, u32[]{:S(2)}, u32[]{:S(2)}) collective-permute-start(bf16[192,640]{1,0:T(8,128)(2,1)S(1)} %far.3.x1.x0), channel_id=1, source_target_pairs={{0,32},{16,48},{32,64},{48,80},{64,96},{80,112},{96,128},{112,144}... | collective-permute-start | bytes 737288 | tf_op jit(solution)/shard_map/ppermute | solution.py:373
  26.1 14.4 %collective-permute-start.4 = (bf16[192,640]{1,0:T(8,128)(2,1)S(1)}, bf16[192,640]{1,0:T(8,128)(2,1)S(1)}, u32[]{:S(2)}, u32[]{:S(2)}) collective-permute-start(bf16[192,640]{1,0:T(8,128)(2,1)S(1)} %temporal.2.own), channel_id=1, source_target_pairs={{0,16},{16,0},{32,48},{48,32},{64,80},{80,64},{96,112},{112,96},{1... | collective-permute-start | bytes 737288 | tf_op jit(solution)/shard_map/ppermute | solution.py:367
  33.8 7.5 %collective-permute-start.3 = (bf16[192,640]{1,0:T(8,128)(2,1)S(1)}, bf16[192,640]{1,0:T(8,128)(2,1)S(1)}, u32[]{:S(2)}, u32[]{:S(2)}) collective-permute-start(bf16[192,640]{1,0:T(8,128)(2,1)S(1)} %temporal.2.own), channel_id=1, source_target_pairs={{1,16},{2,17},{3,18},{4,19},{5,20},{6,21},{7,22},{8,23},{9,24},{10... | collective-permute-start | bytes 737288 | tf_op jit(solution)/shard_map/ppermute | solution.py:370
  36.1 9.7 %collective-permute-start.7 = (bf16[192,640]{1,0:T(8,128)(2,1)S(1)}, bf16[192,640]{1,0:T(8,128)(2,1)S(1)}, u32[]{:S(2)}, u32[]{:S(2)}) collective-permute-start(bf16[192,640]{1,0:T(8,128)(2,1)S(1)} %temporal.3.own), channel_id=1, source_target_pairs={{0,16},{16,0},{32,48},{48,32},{64,80},{80,64},{96,112},{112,96},{1... | collective-permute-start | bytes 737288 | tf_op jit(solution)/shard_map/ppermute | solution.py:367
  38.4 7.5 %collective-permute-start.6 = (bf16[192,640]{1,0:T(8,128)(2,1)S(1)}, bf16[192,640]{1,0:T(8,128)(2,1)S(1)}, u32[]{:S(2)}, u32[]{:S(2)}) collective-permute-start(bf16[192,640]{1,0:T(8,128)(2,1)S(1)} %temporal.3.own), channel_id=1, source_target_pairs={{1,16},{2,17},{3,18},{4,19},{5,20},{6,21},{7,22},{8,23},{9,24},{10... | collective-permute-start | bytes 737288 | tf_op jit(solution)/shard_map/ppermute | solution.py:370
  43.9 9.1 %collective-permute-start.8 = (bf16[192,640]{1,0:T(8,128)(2,1)S(1)}, bf16[192,640]{1,0:T(8,128)(2,1)S(1)}, u32[]{:S(2)}, u32[]{:S(2)}) collective-permute-start(bf16[192,640]{1,0:T(8,128)(2,1)S(1)} %spatial_b.1.x0), channel_id=1, source_target_pairs={{0,32},{16,48},{32,64},{48,80},{64,96},{80,112},{96,128},{112,144}... | collective-permute-start | bytes 737288 | tf_op jit(solution)/shard_map/ppermute | solution.py:373
  48.5 11.9 %collective-permute-start.9 = (bf16[192,640]{1,0:T(8,128)(2,1)S(1)}, bf16[192,640]{1,0:T(8,128)(2,1)S(1)}, u32[]{:S(2)}, u32[]{:S(2)}) collective-permute-start(bf16[192,640]{1,0:T(8,128)(2,1)S(1)} %spatial_a.1.x1.y0), channel_id=1, source_target_pairs={{0,32},{16,48},{32,64},{48,80},{64,96},{80,112},{96,128},{112,144}... | collective-permute-start | bytes 737288 | tf_op jit(solution)/shard_map/ppermute | solution.py:373
  60.6 3.8 %collective-permute-start.10 = (bf16[192,640]{1,0:T(8,128)(2,1)S(1)}, bf16[192,640]{1,0:T(8,128)(2,1)S(1)}, u32[]{:S(2)}, u32[]{:S(2)}) collective-permute-start(bf16[192,640]{1,0:T(8,128)(2,1)S(1)} %get-tuple-element.39), channel_id=1, source_target_pairs={{0,16},{16,0},{32,48},{48,32},{64,80},{80,64},{96,112},{112,96},{1... | collective-permute-start | bytes 737288 | tf_op jit(solution)/shard_map/ppermute | solution.py:367

commit v5 on v4

--- a/solution.py
+++ b/solution.py
@@ -109,9 +109,15 @@
         both[i // 2, :, (i % 2) * W : (i % 2 + 1) * W] = rows[i]
 
 
-def join_kernel(mine, other, owned):
+def pack_pair(rows, pair, dst):
+    dst[:, :W] = rows[2 * pair]
+    dst[:, W:] = rows[2 * pair + 1]
+
+
+def join_kernel(mine, other, owned, sib):
     owned[0] = mine[1]
-    owned[1] = other[0]
+    pack_pair(other, core_index(), owned.at[1])
+    pack_pair(other, 1 - core_index(), sib)
 
 
 def unpack_rows(x, out, rows, sems, pair):
@@ -210,20 +216,24 @@
         act2[:, lanes] = activate(x.astype(BF16), gain, None)
 
 
-def near_kernel(which, pairs, *rest):
-    near_body(tiles_of(pairs.at[which]), tiles_of(pairs.at[1 - which]), *rest)
-
-
-def near(which, pairs, w1, g1, g2):
+def near_mine_kernel(mine, *rest):
+    near_body(tiles_of(mine.at[1]), tiles_of(mine.at[0]), *rest)
+
+
+def near_other_kernel(owned, sib, *rest):
+    near_body(tiles_of(owned.at[1]), tiles_of(sib), *rest)
+
+
+def near(kernel, arrays, w1, g1, g2):
     return call(
-        functools.partial(near_kernel, which),
+        kernel,
         [pair_shape()] * 2,
-        4,
+        len(arrays) + 3,
         "near",
         scratch=[pltpu.VMEM((3 * C, PAIR), BF16)],
         flops=2 * C * C * 9 * PAIR,
         moved=2000000,
-    )(pairs, w1, g1, g2)
+    )(*arrays, w1, g1, g2)
 
 
 def far_body(z, own, act1, act2, w1, g1, w2, g2, out, s1, s2):
@@ -372,7 +382,8 @@
     def onward(x):
         return lax.ppermute(x, "frames", later)
 
-    view = in_hbm(jnp.transpose(video[0], (0, 2, 1)))
+    raw = jnp.transpose(video[0], (0, 2, 1))
+    view = in_hbm(raw)
     mine = call(
         pack_kernel,
         jax.ShapeDtypeStruct((2, C, PAIR), BF16),
@@ -382,13 +393,15 @@
         moved=1000000,
         in_specs=[ANY],
     )(view)
-    other = swap(mine)
-    owned = call(join_kernel, jax.ShapeDtypeStruct((2, C, PAIR), BF16), 2, "join", moved=1000)(mine, other)
+    arrived = pltpu.with_memory_space_constraint(swap(raw), pltpu.VMEM)
+    owned, sib_o = call(join_kernel, [jax.ShapeDtypeStruct((2, C, PAIR), BF16), pair_shape()], 2, "join", moved=1000)(
+        mine, arrived
+    )
     z = halo(owned)
     (w0, w1, w2, w3), (g0, g1, g2, g3), ts = prepare(spatial_weights, norm_gains, temporal_weights)
 
-    near_m = near(1, mine, w0, g0, g1)
-    near_o = near(0, other, w0, g0, g1)
+    near_m = near(near_mine_kernel, (mine,), w0, g0, g1)
+    near_o = near(near_other_kernel, (owned, sib_o), w0, g0, g1)
     arrays = (z, owned, *near_m, *near_o)
     inner_b = far(functools.partial(far_pick_kernel, 1), arrays, w0, g0, w1, g1)
     before_b = onward(inner_b)

time: 65.7 us -> 64.8 us (0.986)
  waiting for transfers between devices: 12.6 us -> 11.6 us
    ppermute x4, waiting for transfers between devices: 1.83 us -> 0.9 us  [swap(): return lax.ppermute(x, 'frames', swaps)]
  transfers between devices with their start and end apart: 11 -> 11, of which waited for: 8 -> 8; matrix products, arithmetic and copies ran while one was open for 0% -> 0% of each run, Pallas kernels for 24% -> 27%
where the time goes in v5:
time: 64.8 us; the launch traced here: 64.5 us
  starting transfers between devices  31.8 us (49%)
  Pallas kernels  20.8 us (32%)
  waiting for transfers between devices  11.6 us (18%)
    ppermute x4, starting transfers between devices, swap(): return lax.ppermute(x, 'frames', swaps)  13.3 us
    ppermute x4, starting transfers between devices, onward(): return lax.ppermute(x, 'frames', later)  10.7 us
    ppermute x4, waiting for transfers between devices, onward(): return lax.ppermute(x, 'frames', later)  9.17 us
    ppermute x3, starting transfers between devices, halo(): return lax.ppermute(x, ('frames', 'rows'), across)  7.8 us
    pallas_call x2, Pallas kernels, far(): call(kernel, pair_shape(), len(arrays) + 4, 'far', scratch=[pltpu.VMEM((3...  4.89 us
    pallas_call x1, Pallas kernels, prepare(): call(weights_kernel, [shape((3 * C, 3 * C), BF16)] * 4 + [shape((C, LANES...  3.47 us
    pallas_call x2, Pallas kernels, near(): call(kernel, [pair_shape()] * 2, len(arrays) + 3, 'near', scratch=[pltpu....  2.62 us
    pallas_call x1, Pallas kernels, on_device(): inner_b = spatial(spatial_kernel, 7, 'spatial_b')(z_b, own_b, sib_b, *both)  2.58 us
  transfers between devices with their start and end apart: 11, of which 8 were waited for; matrix products, arithmetic and copies ran while one was open for 0% of the time, Pallas kernels for 27%

profile of v5, /device:TPU:25, one launch (start us, length us, event | category | flops | bytes accessed | tf_op | source)
XLA Modules:
  0.0 64.5 jit_solution(13115060608597940267)
XLA Ops:
  0.0 0.7 %collective-permute-start = (bf16[4,192,320]{2,1,0:T(8,128)(2,1)}, bf16[4,192,320]{2,1,0:T(8,128)(2,1)S(1)}, u32[]{:S(2)}, u32[]{:S(2)}) collective-permute-start(bf16[4,192,320]{2,1,0:T(8,128)(2,1)} %bitcast.6), channel_id=1, source_target_pairs={{0,16},{16,0},{32,48},{48,32},{64,80},{80,64},{96,112},{112,96},{1... | collective-permute-start | bytes 1474568 | tf_op jit(solution)/shard_map/ppermute | solution.py:377
  0.7 1.3 %pack.1.mine = bf16[2,192,640]{2,1,0:T(8,128)(2,1)S(1)} custom-call(bf16[4,192,320]{2,1,0:T(8,128)(2,1)} %bitcast.7), custom_call_target="tpu_custom_call" | custom-call | bytes 1000000 | tf_op jit(solution)/shard_map/pack/pallas_call | solution.py:387
  2.0 0.6 collective-permute-done.other
  2.5 0.2 join.1
  2.7 3.8 %collective-permute-start.1 = (bf16[2,192,640]{2,1,0:T(8,128)(2,1)S(1)}, bf16[2,192,640]{2,1,0:T(8,128)(2,1)S(1)}, u32[]{:S(2)}, u32[]{:S(2)}) collective-permute-start(bf16[2,192,640]{2,1,0:T(8,128)(2,1)S(1)} %get-tuple-element.27.owned), channel_id=1, source_target_pairs={{1,16},{2,17},{3,18},{4,19},{5,20},{6,21},{7,22},{8,23},{9,24},{10... | collective-permute-start | bytes 1474568 | tf_op jit(solution)/shard_map/ppermute | solution.py:380
  6.5 3.5 %weights.1 = (bf16[576,576]{1,0:T(8,128)(2,1)S(1)}, bf16[576,576]{1,0:T(8,128)(2,1)S(1)}, bf16[576,576]{1,0:T(8,128)(2,1)S(1)}, bf16[576,576]{1,0:T(8,128)(2,1)S...) custom-call(bf16[4,3,3,192,192]{4,3,2,1,0:T(8,128)(2,1)} %sw.1, ...), custom_call_target="tpu_custom_call" | custom-call | bytes 6000000 | tf_op jit(solution)/shard_map/weights/pallas_call | solution.py:83
  10.0 1.3 %near.2 = (bf16[192,640]{1,0:T(8,128)(2,1)S(1)}, bf16[192,640]{1,0:T(8,128)(2,1)S(1)}) custom-call(bf16[2,192,640]{2,1,0:T(8,128)(2,1)S(1)} %pack.1.mine, bf16[576,576]{1,0:T(8,128)(2,1)S(1)} %get-tuple-element.28.rest_0_, f32[192,128]{1,0:T(8,128)S(1)} %get-tuple-element.29.rest_1_, f32[192,128]{1,0:T(8,128)S(1)} %get-tuple-element.30.rest_2_.rest_3_), custom_call_target="tpu_custom_call" | custom-call | flops 424673280 | bytes 2000000 | tf_op jit(solution)/shard_map/near/pallas_call | solution.py:228
  11.3 1.3 %near.3 = (bf16[192,640]{1,0:T(8,128)(2,1)S(1)}, bf16[192,640]{1,0:T(8,128)(2,1)S(1)}) custom-call(bf16[2,192,640]{2,1,0:T(8,128)(2,1)S(1)} %get-tuple-element.27.owned, bf16[192,640]{1,0:T(8,128)(2,1)S(1)} %get-tuple-element.33.sib, bf16[576,576]{1,0:T(8,128)(2,1)S(1)} %get-tuple-element.28.rest_0_, f32[192,128]{1,0:T(8,128)S(1)} %get-tuple-element.29.rest_1_, ...), custom_call_target="tpu_custom_call" | custom-call | flops 424673280 | bytes 2000000 | tf_op jit(solution)/shard_map/near/pallas_call | solution.py:228
  12.6 0.7 %collective-permute-done.1.z = bf16[2,192,640]{2,1,0:T(8,128)(2,1)S(1)} collective-permute-done((bf16[2,192,640]{2,1,0:T(8,128)(2,1)S(1)}, bf16[2,192,640]{2,1,0:T(8,128)(2,1)S(1)}, u32[]{:S(2)}, u32[]{:S(2)}) %collective-permute-start.1) | collective-permute-done | bytes 491552 | tf_op jit(solution)/shard_map/ppermute | solution.py:380
  13.3 2.4 %far.2.x0 = bf16[192,640]{1,0:T(8,128)(2,1)S(1)} custom-call(bf16[2,192,640]{2,1,0:T(8,128)(2,1)S(1)} %collective-permute-done.1.z, bf16[2,192,640]{2,1,0:T(8,128)(2,1)S(1)} %get-tuple-element.27.owned, bf16[192,640]{1,0:T(8,128)(2,1)S(1)} %get-tuple-element.31.act1_m, bf16[192,640]{1,0:T(8,128)(2,1)S(1)} %get-tuple-element.32.act2_m, ...), custom_call_target="tpu_custom_call" | custom-call | flops 849346560 | bytes 4000000 | tf_op jit(solution)/shard_map/far/pallas_call | solution.py:275
  15.7 3.1 %collective-permute-start.2 = (bf16[192,640]{1,0:T(8,128)(2,1)S(1)}, bf16[192,640]{1,0:T(8,128)(2,1)S(1)}, u32[]{:S(2)}, u32[]{:S(2)}) collective-permute-start(bf16[192,640]{1,0:T(8,128)(2,1)S(1)} %far.2.x0), channel_id=1, source_target_pairs={{0,32},{16,48},{32,64},{48,80},{64,96},{80,112},{96,128},{112,144}... | collective-permute-start | bytes 737288 | tf_op jit(solution)/shard_map/ppermute | solution.py:383
  18.9 2.4 %far.3.x1.x0 = bf16[192,640]{1,0:T(8,128)(2,1)S(1)} custom-call(bf16[2,192,640]{2,1,0:T(8,128)(2,1)S(1)} %collective-permute-done.1.z, bf16[2,192,640]{2,1,0:T(8,128)(2,1)S(1)} %get-tuple-element.27.owned, bf16[192,640]{1,0:T(8,128)(2,1)S(1)} %get-tuple-element.31.act1_m, bf16[192,640]{1,0:T(8,128)(2,1)S(1)} %get-tuple-element.32.act2_m, ...), custom_call_target="tpu_custom_call" | custom-call | flops 849346560 | bytes 4000000 | tf_op jit(solution)/shard_map/far/pallas_call | solution.py:275
  21.3 3.1 %collective-permute-start.5 = (bf16[192,640]{1,0:T(8,128)(2,1)S(1)}, bf16[192,640]{1,0:T(8,128)(2,1)S(1)}, u32[]{:S(2)}, u32[]{:S(2)}) collective-permute-start(bf16[192,640]{1,0:T(8,128)(2,1)S(1)} %far.3.x1.x0), channel_id=1, source_target_pairs={{0,32},{16,48},{32,64},{48,80},{64,96},{80,112},{96,128},{112,144}... | collective-permute-start | bytes 737288 | tf_op jit(solution)/shard_map/ppermute | solution.py:383
  24.4 0.3 collective-permute-done.2.x2.x1
  24.8 0.4 temporal.2.own
  25.2 7.7 %collective-permute-start.4 = (bf16[192,640]{1,0:T(8,128)(2,1)S(1)}, bf16[192,640]{1,0:T(8,128)(2,1)S(1)}, u32[]{:S(2)}, u32[]{:S(2)}) collective-permute-start(bf16[192,640]{1,0:T(8,128)(2,1)S(1)} %temporal.2.own), channel_id=1, source_target_pairs={{0,16},{16,0},{32,48},{48,32},{64,80},{80,64},{96,112},{112,96},{1... | collective-permute-start | bytes 737288 | tf_op jit(solution)/shard_map/ppermute | solution.py:377
  32.9 1.9 %collective-permute-start.3 = (bf16[192,640]{1,0:T(8,128)(2,1)S(1)}, bf16[192,640]{1,0:T(8,128)(2,1)S(1)}, u32[]{:S(2)}, u32[]{:S(2)}) collective-permute-start(bf16[192,640]{1,0:T(8,128)(2,1)S(1)} %temporal.2.own), channel_id=1, source_target_pairs={{1,16},{2,17},{3,18},{4,19},{5,20},{6,21},{7,22},{8,23},{9,24},{10... | collective-permute-start | bytes 737288 | tf_op jit(solution)/shard_map/ppermute | solution.py:380
  34.8 0.0 collective-permute-done.5.x2
  34.8 0.4 temporal.3.own
  35.2 2.3 %collective-permute-start.7 = (bf16[192,640]{1,0:T(8,128)(2,1)S(1)}, bf16[192,640]{1,0:T(8,128)(2,1)S(1)}, u32[]{:S(2)}, u32[]{:S(2)}) collective-permute-start(bf16[192,640]{1,0:T(8,128)(2,1)S(1)} %temporal.3.own), channel_id=1, source_target_pairs={{0,16},{16,0},{32,48},{48,32},{64,80},{80,64},{96,112},{112,96},{1... | collective-permute-start | bytes 737288 | tf_op jit(solution)/shard_map/ppermute | solution.py:377
  37.5 2.1 %collective-permute-start.6 = (bf16[192,640]{1,0:T(8,128)(2,1)S(1)}, bf16[192,640]{1,0:T(8,128)(2,1)S(1)}, u32[]{:S(2)}, u32[]{:S(2)}) collective-permute-start(bf16[192,640]{1,0:T(8,128)(2,1)S(1)} %temporal.3.own), channel_id=1, source_target_pairs={{1,16},{2,17},{3,18},{4,19},{5,20},{6,21},{7,22},{8,23},{9,24},{10... | collective-permute-start | bytes 737288 | tf_op jit(solution)/shard_map/ppermute | solution.py:380
  39.6 0.0 collective-permute-done.4.sib
  39.6 0.8 %collective-permute-done.3.z = bf16[192,640]{1,0:T(8,128)(2,1)S(1)} collective-permute-done((bf16[192,640]{1,0:T(8,128)(2,1)S(1)}, bf16[192,640]{1,0:T(8,128)(2,1)S(1)}, u32[]{:S(2)}, u32[]{:S(2)}) %collective-permute-start.3) | collective-permute-done | bytes 245792 | tf_op jit(solution)/shard_map/ppermute | solution.py:380
  40.4 2.6 %spatial_b.1.x0 = bf16[192,640]{1,0:T(8,128)(2,1)S(1)} custom-call(bf16[192,640]{1,0:T(8,128)(2,1)S(1)} %collective-permute-done.3.z, bf16[192,640]{1,0:T(8,128)(2,1)S(1)} %temporal.2.own, bf16[192,640]{1,0:T(8,128)(2,1)S(1)} %collective-permute-done.4.sib, bf16[576,576]{1,0:T(8,128)(2,1)S(1)} %get-tuple-element.37.rest_0_, ...), custom_call_target="tpu_custom_call" | custom-call | flops 1274019840 | bytes 4000000 | tf_op jit(solution)/shard_map/spatial_b/pallas_call | solution.py:416
  43.0 1.9 %collective-permute-start.8 = (bf16[192,640]{1,0:T(8,128)(2,1)S(1)}, bf16[192,640]{1,0:T(8,128)(2,1)S(1)}, u32[]{:S(2)}, u32[]{:S(2)}) collective-permute-start(bf16[192,640]{1,0:T(8,128)(2,1)S(1)} %spatial_b.1.x0), channel_id=1, source_target_pairs={{0,32},{16,48},{32,64},{48,80},{64,96},{80,112},{96,128},{112,144}... | collective-permute-start | bytes 737288 | tf_op jit(solution)/shard_map/ppermute | solution.py:383
  44.9 0.0 collective-permute-done.7.sib
  44.9 0.1 collective-permute-done.6.z
  45.0 2.6 %spatial_a.1.x1.y0 = bf16[192,640]{1,0:T(8,128)(2,1)S(1)} custom-call(bf16[192,640]{1,0:T(8,128)(2,1)S(1)} %collective-permute-done.6.z, bf16[192,640]{1,0:T(8,128)(2,1)S(1)} %temporal.3.own, bf16[192,640]{1,0:T(8,128)(2,1)S(1)} %collective-permute-done.7.sib, bf16[576,576]{1,0:T(8,128)(2,1)S(1)} %get-tuple-element.37.rest_0_, ...), custom_call_target="tpu_custom_call" | custom-call | flops 1274019840 | bytes 4000000 | tf_op jit(solution)/shard_map/spatial_a/pallas_call | solution.py:418
  47.6 2.5 %collective-permute-start.9 = (bf16[192,640]{1,0:T(8,128)(2,1)S(1)}, bf16[192,640]{1,0:T(8,128)(2,1)S(1)}, u32[]{:S(2)}, u32[]{:S(2)}) collective-permute-start(bf16[192,640]{1,0:T(8,128)(2,1)S(1)} %spatial_a.1.x1.y0), channel_id=1, source_target_pairs={{0,32},{16,48},{32,64},{48,80},{64,96},{80,112},{96,128},{112,144}... | collective-permute-start | bytes 737288 | tf_op jit(solution)/shard_map/ppermute | solution.py:383
  50.1 1.9 %collective-permute-done.8.x2 = bf16[192,640]{1,0:T(8,128)(2,1)S(1)} collective-permute-done((bf16[192,640]{1,0:T(8,128)(2,1)S(1)}, bf16[192,640]{1,0:T(8,128)(2,1)S(1)}, u32[]{:S(2)}, u32[]{:S(2)}) %collective-permute-start.8) | collective-permute-done | bytes 245792 | tf_op jit(solution)/shard_map/ppermute | solution.py:383
  52.0 0.6 temporal_late.1
  52.6 6.9 %collective-permute-done.9.y2 = bf16[192,640]{1,0:T(8,128)(2,1)S(1)} collective-permute-done((bf16[192,640]{1,0:T(8,128)(2,1)S(1)}, bf16[192,640]{1,0:T(8,128)(2,1)S(1)}, u32[]{:S(2)}, u32[]{:S(2)}) %collective-permute-start.9) | collective-permute-done | bytes 245792 | tf_op jit(solution)/shard_map/ppermute | solution.py:383
  59.5 0.2 temporal_last.1
  59.7 2.7 %collective-permute-start.10 = (bf16[192,640]{1,0:T(8,128)(2,1)S(1)}, bf16[192,640]{1,0:T(8,128)(2,1)S(1)}, u32[]{:S(2)}, u32[]{:S(2)}) collective-permute-start(bf16[192,640]{1,0:T(8,128)(2,1)S(1)} %get-tuple-element.43), channel_id=1, source_target_pairs={{0,16},{16,0},{32,48},{48,32},{64,80},{80,64},{96,112},{112,96},{1... | collective-permute-start | bytes 737288 | tf_op jit(solution)/shard_map/ppermute | solution.py:377
  62.4 0.8 %unpack.2.part = bf16[4,192,320]{2,1,0:T(8,128)(2,1)} custom-call(bf16[192,640]{1,0:T(8,128)(2,1)S(1)} %get-tuple-element.44.keep), custom_call_target="tpu_custom_call" | custom-call | bytes 500000 | tf_op jit(solution)/shard_map/unpack/pallas_call | solution.py:144
  63.2 0.3 collective-permute-done.10.got
  63.6 0.8 %unpack.3 = bf16[4,192,320]{2,1,0:T(8,128)(2,1)} custom-call(bf16[192,640]{1,0:T(8,128)(2,1)S(1)} %collective-permute-done.10.got, bf16[4,192,320]{2,1,0:T(8,128)(2,1)} %unpack.2.part), custom_call_target="tpu_custom_call", output_to_operand_aliasing={{}: (1, {})} | custom-call | bytes 500000 | tf_op jit(solution)/shard_map/unpack/pallas_call | solution.py:144
Async XLA Ops:
  0.0 2.5 %collective-permute-start = (bf16[4,192,320]{2,1,0:T(8,128)(2,1)}, bf16[4,192,320]{2,1,0:T(8,128)(2,1)S(1)}, u32[]{:S(2)}, u32[]{:S(2)}) collective-permute-start(bf16[4,192,320]{2,1,0:T(8,128)(2,1)} %bitcast.6), channel_id=1, source_target_pairs={{0,16},{16,0},{32,48},{48,32},{64,80},{80,64},{96,112},{112,96},{1... | collective-permute-start | bytes 1474568 | tf_op jit(solution)/shard_map/ppermute | solution.py:377
  2.7 10.6 %collective-permute-start.1 = (bf16[2,192,640]{2,1,0:T(8,128)(2,1)S(1)}, bf16[2,192,640]{2,1,0:T(8,128)(2,1)S(1)}, u32[]{:S(2)}, u32[]{:S(2)}) collective-permute-start(bf16[2,192,640]{2,1,0:T(8,128)(2,1)S(1)} %get-tuple-element.27.owned), channel_id=1, source_target_pairs={{1,16},{2,17},{3,18},{4,19},{5,20},{6,21},{7,22},{8,23},{9,24},{10... | collective-permute-start | bytes 1474568 | tf_op jit(solution)/shard_map/ppermute | solution.py:380
  15.7 9.1 %collective-permute-start.2 = (bf16[192,640]{1,0:T(8,128)(2,1)S(1)}, bf16[192,640]{1,0:T(8,128)(2,1)S(1)}, u32[]{:S(2)}, u32[]{:S(2)}) collective-permute-start(bf16[192,640]{1,0:T(8,128)(2,1)S(1)} %far.2.x0), channel_id=1, source_target_pairs={{0,32},{16,48},{32,64},{48,80},{64,96},{80,112},{96,128},{112,144}... | collective-permute-start | bytes 737288 | tf_op jit(solution)/shard_map/ppermute | solution.py:383
  21.3 13.5 %collective-permute-start.5 = (bf16[192,640]{1,0:T(8,128)(2,1)S(1)}, bf16[192,640]{1,0:T(8,128)(2,1)S(1)}, u32[]{:S(2)}, u32[]{:S(2)}) collective-permute-start(bf16[192,640]{1,0:T(8,128)(2,1)S(1)} %far.3.x1.x0), channel_id=1, source_target_pairs={{0,32},{16,48},{32,64},{48,80},{64,96},{80,112},{96,128},{112,144}... | collective-permute-start | bytes 737288 | tf_op jit(solution)/shard_map/ppermute | solution.py:383
  25.2 14.4 %collective-permute-start.4 = (bf16[192,640]{1,0:T(8,128)(2,1)S(1)}, bf16[192,640]{1,0:T(8,128)(2,1)S(1)}, u32[]{:S(2)}, u32[]{:S(2)}) collective-permute-start(bf16[192,640]{1,0:T(8,128)(2,1)S(1)} %temporal.2.own), channel_id=1, source_target_pairs={{0,16},{16,0},{32,48},{48,32},{64,80},{80,64},{96,112},{112,96},{1... | collective-permute-start | bytes 737288 | tf_op jit(solution)/shard_map/ppermute | solution.py:377
  32.9 7.5 %collective-permute-start.3 = (bf16[192,640]{1,0:T(8,128)(2,1)S(1)}, bf16[192,640]{1,0:T(8,128)(2,1)S(1)}, u32[]{:S(2)}, u32[]{:S(2)}) collective-permute-start(bf16[192,640]{1,0:T(8,128)(2,1)S(1)} %temporal.2.own), channel_id=1, source_target_pairs={{1,16},{2,17},{3,18},{4,19},{5,20},{6,21},{7,22},{8,23},{9,24},{10... | collective-permute-start | bytes 737288 | tf_op jit(solution)/shard_map/ppermute | solution.py:380
  35.2 9.7 %collective-permute-start.7 = (bf16[192,640]{1,0:T(8,128)(2,1)S(1)}, bf16[192,640]{1,0:T(8,128)(2,1)S(1)}, u32[]{:S(2)}, u32[]{:S(2)}) collective-permute-start(bf16[192,640]{1,0:T(8,128)(2,1)S(1)} %temporal.3.own), channel_id=1, source_target_pairs={{0,16},{16,0},{32,48},{48,32},{64,80},{80,64},{96,112},{112,96},{1... | collective-permute-start | bytes 737288 | tf_op jit(solution)/shard_map/ppermute | solution.py:377
  37.5 7.5 %collective-permute-start.6 = (bf16[192,640]{1,0:T(8,128)(2,1)S(1)}, bf16[192,640]{1,0:T(8,128)(2,1)S(1)}, u32[]{:S(2)}, u32[]{:S(2)}) collective-permute-start(bf16[192,640]{1,0:T(8,128)(2,1)S(1)} %temporal.3.own), channel_id=1, source_target_pairs={{1,16},{2,17},{3,18},{4,19},{5,20},{6,21},{7,22},{8,23},{9,24},{10... | collective-permute-start | bytes 737288 | tf_op jit(solution)/shard_map/ppermute | solution.py:380
  43.0 9.1 %collective-permute-start.8 = (bf16[192,640]{1,0:T(8,128)(2,1)S(1)}, bf16[192,640]{1,0:T(8,128)(2,1)S(1)}, u32[]{:S(2)}, u32[]{:S(2)}) collective-permute-start(bf16[192,640]{1,0:T(8,128)(2,1)S(1)} %spatial_b.1.x0), channel_id=1, source_target_pairs={{0,32},{16,48},{32,64},{48,80},{64,96},{80,112},{96,128},{112,144}... | collective-permute-start | bytes 737288 | tf_op jit(solution)/shard_map/ppermute | solution.py:383
  47.6 11.9 %collective-permute-start.9 = (bf16[192,640]{1,0:T(8,128)(2,1)S(1)}, bf16[192,640]{1,0:T(8,128)(2,1)S(1)}, u32[]{:S(2)}, u32[]{:S(2)}) collective-permute-start(bf16[192,640]{1,0:T(8,128)(2,1)S(1)} %spatial_a.1.x1.y0), channel_id=1, source_target_pairs={{0,32},{16,48},{32,64},{48,80},{64,96},{80,112},{96,128},{112,144}... | collective-permute-start | bytes 737288 | tf_op jit(solution)/shard_map/ppermute | solution.py:383
  59.7 3.8 %collective-permute-start.10 = (bf16[192,640]{1,0:T(8,128)(2,1)S(1)}, bf16[192,640]{1,0:T(8,128)(2,1)S(1)}, u32[]{:S(2)}, u32[]{:S(2)}) collective-permute-start(bf16[192,640]{1,0:T(8,128)(2,1)S(1)} %get-tuple-element.43), channel_id=1, source_target_pairs={{0,16},{16,0},{32,48},{48,32},{64,80},{80,64},{96,112},{112,96},{1... | collective-permute-start | bytes 737288 | tf_op jit(solution)/shard_map/ppermute | solution.py:377

commit v6 on v5

--- a/solution.py
+++ b/solution.py
@@ -48,13 +48,13 @@
     return jnp.broadcast_to(g[k : k + 1, :] * 0.5, (LANES, C)).T
 
 
-def transpose_taps(source, wt):
-    for di in range(3):
+def transpose_taps(source, wt, order):
+    for place, di in enumerate(order):
         for dj in range(3):
-            wt[dj * C : (dj + 1) * C, di * C : (di + 1) * C] = source[di, dj].T
-
-
-def weights_kernel(sw, g, tw, w0, w1, w2, w3, g0, g1, g2, g3, t0, t1, held, taps, gains, sems, more_sems):
+            wt[dj * C : (dj + 1) * C, place * C : (place + 1) * C] = source[di, dj].T
+
+
+def weights_kernel(sw, g, tw, w0, w1, w2, w3, far0, far1, g0, g1, g2, g3, t0, t1, held, taps, gains, sems, more_sems):
     gain_copy = pltpu.make_async_copy(g, gains, more_sems.at[0])
     tap_copy = pltpu.make_async_copy(tw, taps, more_sems.at[1])
     copies = [pltpu.make_async_copy(sw.at[k], held.at[k], sems.at[k]) for k in range(4)]
@@ -65,9 +65,13 @@
     gain_copy.wait()
     for k, gt in enumerate((g0, g1, g2, g3)):
         gt[...] = gain_column(gains, k)
+    core = core_index()
+    by_core = (2 * core, 1, 2 - 2 * core)
     for k, wt in enumerate((w0, w1, w2, w3)):
         copies[k].wait()
-        transpose_taps(held.at[k], wt)
+        transpose_taps(held.at[k], wt, range(3))
+        if k < 2:
+            transpose_taps(held.at[k], (far0, far1)[k], by_core)
     tap_copy.wait()
     for b, wt in enumerate((t0, t1)):
         for tap in range(3):
@@ -82,7 +86,7 @@
     shape = jax.ShapeDtypeStruct
     outs = call(
         weights_kernel,
-        [shape((3 * C, 3 * C), BF16)] * 4 + [shape((C, LANES), F32)] * 4 + [shape((C, 3 * C), BF16)] * 2,
+        [shape((3 * C, 3 * C), BF16)] * 6 + [shape((C, LANES), F32)] * 4 + [shape((C, 3 * C), BF16)] * 2,
         3,
         "weights",
         scratch=[
@@ -95,7 +99,7 @@
         moved=6000000,
         in_specs=[ANY] * 3,
     )(in_hbm(weights), in_hbm(gains), in_hbm(taps))
-    return outs[:4], outs[4:8], outs[8:]
+    return outs[:6], outs[6:10], outs[10:]
 
 
 def pack_kernel(v, both, rows, sems):
@@ -181,12 +185,26 @@
         rows[2 * C :, lanes] = below
 
 
+def put(rows, tiles, place, at=0):
+    for t, x in enumerate(tiles):
+        lanes = slice(at + t * LANES, at + (t + 1) * LANES)
+        rows[place * C : (place + 1) * C, lanes] = x
+
+
+def either(first, x, y):
+    return [jnp.where(first, s, t) for s, t in zip(x, y)]
+
+
+def middle(is0, far, near):
+    return between(either(is0, far, near), either(is0, near, far))
+
+
 def convolved(weight, rows):
     lane = lax.broadcasted_iota(jnp.int32, (1, LANES), 1)
     out = []
     for at in range(0, rows.shape[1], PAIR):
         product = jnp.dot(weight[...], rows[:, at : at + PAIR], preferred_element_type=F32)
-        left, middle, right = (tiles_of(product[dj * C : (dj + 1) * C]) for dj in range(3))
+        left, mid, right = (tiles_of(product[dj * C : (dj + 1) * C]) for dj in range(3))
         left = [pltpu.roll(t, 1, 1) for t in left]
         right = [pltpu.roll(t, LANES - 1, 1) for t in right]
         for t in range(5):
@@ -195,92 +213,80 @@
             if t == W // LANES:
                 a = jnp.where(lane == W % LANES, 0.0, a)
                 b = jnp.where(lane == W % LANES - 1, 0.0, b)
-            out.append(middle[t] + a + b)
+            out.append(mid[t] + a + b)
     return out
 
 
-def either(first, x, y):
-    return [jnp.where(first, s, t) for s, t in zip(x, y)]
-
-
-def near_body(own, sib, w1, g1, g2, act1, act2, s1):
+def inside(t):
+    core, row = core_index(), lax.axis_index("rows")
+    top = (core == 0) & (row == 0)
+    bottom = (core == 1) & (row == lax.axis_size("rows") - 1)
+    pixel = lax.broadcasted_iota(jnp.int32, (1, LANES), 1) + t * LANES
+    outside = ((pixel < W) & top) | ((pixel >= W) & bottom)
+    return jnp.where(outside, 0.0, 1.0).astype(F32)
+
+
+def near_pick_kernel(pick, mine, owned, sib_o, w1, g1, w2, g2, part1, part2, s1, s2):
     is0 = core_index() == 0
-    gain = g1[...]
-    own = [activate(t, gain, None) for t in own]
-    sib = [activate(t, gain, None) for t in sib]
-    stack(s1, 0, either(is0, own, sib), either(is0, sib, own))
-    gain = g2[...]
-    for t, x in enumerate(convolved(w1, s1)):
-        lanes = slice(t * LANES, (t + 1) * LANES)
-        act1[:, lanes] = own[t]
-        act2[:, lanes] = activate(x.astype(BF16), gain, None)
-
-
-def near_mine_kernel(mine, *rest):
-    near_body(tiles_of(mine.at[1]), tiles_of(mine.at[0]), *rest)
-
-
-def near_other_kernel(owned, sib, *rest):
-    near_body(tiles_of(owned.at[1]), tiles_of(sib), *rest)
-
-
-def near(kernel, arrays, w1, g1, g2):
+    is_mine = core_index() == pick
+    own = either(is_mine, tiles_of(mine.at[1]), tiles_of(owned.at[1]))
+    sib = either(is_mine, tiles_of(mine.at[0]), tiles_of(sib_o))
+    act = [activate(t, g1[...], None) for t in own]
+    other = [activate(t, g1[...], None) for t in sib]
+    none = [jnp.zeros_like(t) for t in act]
+    put(s1, act, 0)
+    put(s1, middle(is0, act, other), 1)
+    put(s1, other, 2)
+    inner = [activate(x.astype(BF16), g2[...], None) for x in convolved(w1, s1)]
+    put(s2, middle(is0, none, act), 0)
+    put(s2, act, 1)
+    for t, x in enumerate(convolved(w1.at[:, C:], s2)):
+        part1[:, t * LANES : (t + 1) * LANES] = x
+    put(s2, middle(is0, none, inner), 0)
+    put(s2, inner, 1)
+    for t, (x, y) in enumerate(zip(own, convolved(w2.at[:, C:], s2))):
+        part2[:, t * LANES : (t + 1) * LANES] = x.astype(F32) + y
+
+
+def near(pick, mine, owned, sib_o, *weights):
     return call(
-        kernel,
-        [pair_shape()] * 2,
-        len(arrays) + 3,
+        functools.partial(near_pick_kernel, pick),
+        [jax.ShapeDtypeStruct((C, PAIR), F32)] * 2,
+        7,
         "near",
-        scratch=[pltpu.VMEM((3 * C, PAIR), BF16)],
+        scratch=[pltpu.VMEM((3 * C, PAIR), BF16), pltpu.VMEM((2 * C, PAIR), BF16)],
         flops=2 * C * C * 9 * PAIR,
         moved=2000000,
-    )(*arrays, w1, g1, g2)
-
-
-def far_body(z, own, act1, act2, w1, g1, w2, g2, out, s1, s2):
-    core, row = core_index(), lax.axis_index("rows")
-    is0 = core == 0
-    top = is0 & (row == 0)
-    bottom = (core == 1) & (row == lax.axis_size("rows") - 1)
-    gain = g1[...]
-    z = [activate(t, gain, None) for t in z]
-    stack(s1, 0, either(is0, z, act1), either(is0, act1, z))
-    lane = lax.broadcasted_iota(jnp.int32, (1, LANES), 1)
-    gain = g2[...]
-    far = []
-    for t, x in enumerate(convolved(w1, s1)):
-        pixel = lane + t * LANES
-        outside = ((pixel < W) & top) | ((pixel >= W) & bottom)
-        far.append(activate(x.astype(BF16), gain, jnp.where(outside, 0.0, 1.0).astype(F32)))
-    stack(s2, 0, either(is0, far, act2), either(is0, act2, far))
-    for t, (x, y) in enumerate(zip(own, convolved(w2, s2))):
-        out[:, t * LANES : (t + 1) * LANES] = (x.astype(F32) + y).astype(BF16)
-
-
-def far_pick_kernel(pick, z, owned, act1_m, act2_m, act1_o, act2_o, *rest):
+    )(mine, owned, sib_o, *weights)
+
+
+def far_pick_kernel(pick, z, part1, part2, w1, g1, w2, g2, out, s2):
+    is0 = core_index() == 0
     is_mine = core_index() == pick
-
-    def chosen(x, y):
-        return either(is_mine, tiles_of(x), tiles_of(y))
-
-    far_body(
-        chosen(z.at[1], z.at[0]),
-        chosen(owned.at[0], owned.at[1]),
-        chosen(act1_m, act1_o),
-        chosen(act2_m, act2_o),
-        *rest,
-    )
-
-
-def far(kernel, arrays, w1, g1, w2, g2):
+    far = either(is_mine, tiles_of(z.at[1]), tiles_of(z.at[0]))
+    far = [activate(t, g1[...], None) for t in far]
+    none = [jnp.zeros_like(t) for t in far]
+    put(s2, far, 0)
+    put(s2, middle(is0, far, none), 1)
+    inner = []
+    for t, (x, y) in enumerate(zip(tiles_of(part1), convolved(w1.at[:, : 2 * C], s2))):
+        inner.append(activate((x + y).astype(BF16), g2[...], inside(t)))
+    put(s2, inner, 0)
+    put(s2, middle(is0, inner, none), 1)
+    for t, (x, y) in enumerate(zip(tiles_of(part2), convolved(w2.at[:, : 2 * C], s2))):
+        out[:, t * LANES : (t + 1) * LANES] = (x + y).astype(BF16)
+
+
+def far(pick, z, part1, part2, *weights):
     return call(
-        kernel,
+        functools.partial(far_pick_kernel, pick),
         pair_shape(),
-        len(arrays) + 4,
+        7,
         "far",
-        scratch=[pltpu.VMEM((3 * C, PAIR), BF16)] * 2,
+        scratch=[pltpu.VMEM((2 * C, PAIR), BF16)],
         flops=2 * C * C * 9 * 2 * PAIR,
         moved=4000000,
-    )(*arrays, w1, g1, w2, g2)
+    )(z, part1, part2, *weights)
 
 
 def spatial_body(z, own, sib, w1, g1, w2, g2, out, s1, s2):
@@ -289,11 +295,9 @@
     top = is0 & (row == 0)
     bottom = (core == 1) & (row == lax.axis_size("rows") - 1)
     gain = g1[...]
-    above, mid, below = [], [], []
-    for tz, to, ts in zip(z, own, sib):
-        above.append(activate(jnp.where(is0, tz, ts), gain, None))
-        mid.append(activate(to, gain, None))
-        below.append(activate(jnp.where(is0, ts, tz), gain, None))
+    above = [activate(t, gain, None) for t in either(is0, z, sib)]
+    mid = [activate(t, gain, None) for t in own]
+    below = [activate(t, gain, None) for t in either(is0, sib, z)]
     stack(s1, 0, above, mid)
     stack(s1, PAIR, mid, below)
     lane = lax.broadcasted_iota(jnp.int32, (1, LANES), 1)
@@ -310,6 +314,17 @@
 
 def spatial_kernel(z, own, sib, *rest):
     spatial_body(tiles_of(z), tiles_of(own), tiles_of(sib), *rest)
+
+
+def spatial_pick_kernel(pick, z, mine, owned, sib_o, *rest):
+    is_mine = core_index() == pick
+
+    def chosen(x, y):
+        return either(is_mine, tiles_of(x), tiles_of(y))
+
+    spatial_body(
+        chosen(z.at[1], z.at[0]), chosen(mine.at[1], owned.at[1]), chosen(mine.at[0], sib_o), *rest
+    )
 
 
 def spatial(kernel, n_in, name):
@@ -398,14 +413,14 @@
         mine, arrived
     )
     z = halo(owned)
-    (w0, w1, w2, w3), (g0, g1, g2, g3), ts = prepare(spatial_weights, norm_gains, temporal_weights)
-
-    near_m = near(near_mine_kernel, (mine,), w0, g0, g1)
-    near_o = near(near_other_kernel, (owned, sib_o), w0, g0, g1)
-    arrays = (z, owned, *near_m, *near_o)
-    inner_b = far(functools.partial(far_pick_kernel, 1), arrays, w0, g0, w1, g1)
+    (w0, w1, w2, w3, far0, far1), (g0, g1, g2, g3), ts = prepare(spatial_weights, norm_gains, temporal_weights)
+
+    block = (w0, g0, w1, g1)
+    by_core = (far0, g0, far1, g1)
+    parts = near(1, mine, owned, sib_o, *by_core)
+    inner_b = far(1, z, *parts, *by_core)
     before_b = onward(inner_b)
-    inner_a = far(functools.partial(far_pick_kernel, 0), arrays, w0, g0, w1, g1)
+    inner_a = spatial(functools.partial(spatial_pick_kernel, 0), 8, "spatial_a1")(z, mine, owned, sib_o, *block)
     before_a = onward(inner_a)
 
     own_b = temporal(ts[0], inner_b, inner_a, before_b)

time: 64.8 us -> 63.8 us (0.985)
  waiting for transfers between devices: 11.6 us -> 9.95 us
  starting transfers between devices: 31.8 us -> 32.5 us
    ppermute x4, waiting for transfers between devices: 9.17 us -> 8.23 us  [onward(): return lax.ppermute(x, 'frames', later)]
    ppermute x3, waiting for transfers between devices: 1.55 us -> 0.82 us  [halo(): return lax.ppermute(x, ('frames', 'rows'), across)]
    pallas_call x5 -> x4, Pallas kernels: 11 us -> 10.9 us  [the longest x1 4.17 us: prepare(): call(weights_kernel, [shape((3 * C, 3 * C), BF16)] * 6 + [shape((C, LANES...]
  transfers between devices with their start and end apart: 11 -> 11, of which waited for: 8 -> 7; matrix products, arithmetic and copies ran while one was open for 0% -> 0% of each run, Pallas kernels for 27% -> 28%
where the time goes in v6:
time: 63.8 us; the launch traced here: 63.5 us
  starting transfers between devices  32.5 us (51%)
  Pallas kernels  20.7 us (32%)
  waiting for transfers between devices  9.95 us (16%)
    ppermute x4, starting transfers between devices, swap(): return lax.ppermute(x, 'frames', swaps)  13.5 us
    ppermute x4, starting transfers between devices, onward(): return lax.ppermute(x, 'frames', later)  11.3 us
    ppermute x4, waiting for transfers between devices, onward(): return lax.ppermute(x, 'frames', later)  8.23 us
    ppermute x3, starting transfers between devices, halo(): return lax.ppermute(x, ('frames', 'rows'), across)  7.8 us
    pallas_call x1, Pallas kernels, prepare(): call(weights_kernel, [shape((3 * C, 3 * C), BF16)] * 6 + [shape((C, LANES...  4.17 us
    pallas_call x1, Pallas kernels, on_device(): spatial(functools.partial(spatial_pick_kernel, 0), 8, 'spatial_a1')  2.7 us
    pallas_call x1, Pallas kernels, on_device(): inner_b = spatial(spatial_kernel, 7, 'spatial_b')(z_b, own_b, sib_b, *both)  2.58 us
    pallas_call x1, Pallas kernels, on_device(): inner_a = spatial(spatial_kernel, 7, 'spatial_a')(z_a, own_a, sib_a, *both)  2.58 us
  transfers between devices with their start and end apart: 11, of which 7 were waited for; matrix products, arithmetic and copies ran while one was open for 0% of the time, Pallas kernels for 28%

profile of v6, /device:TPU:25, one launch (start us, length us, event | category | flops | bytes accessed | tf_op | source)
XLA Modules:
  0.0 63.5 jit_solution(4959460106820945310)
XLA Ops:
  0.0 0.7 %collective-permute-start = (bf16[4,192,320]{2,1,0:T(8,128)(2,1)}, bf16[4,192,320]{2,1,0:T(8,128)(2,1)S(1)}, u32[]{:S(2)}, u32[]{:S(2)}) collective-permute-start(bf16[4,192,320]{2,1,0:T(8,128)(2,1)} %bitcast.6), channel_id=1, source_target_pairs={{0,16},{16,0},{32,48},{48,32},{64,80},{80,64},{96,112},{112,96},{1... | collective-permute-start | bytes 1474568 | tf_op jit(solution)/shard_map/ppermute | solution.py:392
  0.7 1.3 %pack.1.mine = bf16[2,192,640]{2,1,0:T(8,128)(2,1)S(1)} custom-call(bf16[4,192,320]{2,1,0:T(8,128)(2,1)} %bitcast.7), custom_call_target="tpu_custom_call" | custom-call | bytes 1000000 | tf_op jit(solution)/shard_map/pack/pallas_call | solution.py:402
  2.0 0.6 collective-permute-done.other
  2.5 0.2 join.1
  2.7 3.8 %collective-permute-start.1 = (bf16[2,192,640]{2,1,0:T(8,128)(2,1)S(1)}, bf16[2,192,640]{2,1,0:T(8,128)(2,1)S(1)}, u32[]{:S(2)}, u32[]{:S(2)}) collective-permute-start(bf16[2,192,640]{2,1,0:T(8,128)(2,1)S(1)} %get-tuple-element.27.owned), channel_id=1, source_target_pairs={{1,16},{2,17},{3,18},{4,19},{5,20},{6,21},{7,22},{8,23},{9,24},{10... | collective-permute-start | bytes 1474568 | tf_op jit(solution)/shard_map/ppermute | solution.py:395
  6.5 4.2 %weights.1 = (bf16[576,576]{1,0:T(8,128)(2,1)S(1)}, bf16[576,576]{1,0:T(8,128)(2,1)S(1)}, bf16[576,576]{1,0:T(8,128)(2,1)S(1)}, bf16[576,576]{1,0:T(8,128)(2,1)S...) custom-call(bf16[4,3,3,192,192]{4,3,2,1,0:T(8,128)(2,1)} %sw.1, ...), custom_call_target="tpu_custom_call" | custom-call | bytes 6000000 | tf_op jit(solution)/shard_map/weights/pallas_call | solution.py:87
  10.7 2.3 %near.1 = (f32[192,640]{1,0:T(8,128)S(1)}, f32[192,640]{1,0:T(8,128)S(1)}) custom-call(bf16[2,192,640]{2,1,0:T(8,128)(2,1)S(1)} %pack.1.mine, bf16[2,192,640]{2,1,0:T(8,128)(2,1)S(1)} %get-tuple-element.27.owned, bf16[192,640]{1,0:T(8,128)(2,1)S(1)} %get-tuple-element.28.sib_o, bf16[576,576]{1,0:T(8,128)(2,1)S(1)} %get-tuple-element.29.w1, ...), custom_call_target="tpu_custom_call" | custom-call | flops 424673280 | bytes 2000000 | tf_op jit(solution)/shard_map/near/pallas_call | solution.py:252
  13.0 0.3 collective-permute-done.1.z
  13.3 1.7 %far.1.x0 = bf16[192,640]{1,0:T(8,128)(2,1)S(1)} custom-call(bf16[2,192,640]{2,1,0:T(8,128)(2,1)S(1)} %collective-permute-done.1.z, f32[192,640]{1,0:T(8,128)S(1)} %get-tuple-element.33.part1, f32[192,640]{1,0:T(8,128)S(1)} %get-tuple-element.34.part2, bf16[576,576]{1,0:T(8,128)(2,1)S(1)} %get-tuple-element.29.w1, ...), custom_call_target="tpu_custom_call" | custom-call | flops 849346560 | bytes 4000000 | tf_op jit(solution)/shard_map/far/pallas_call | solution.py:281
  15.0 3.1 %collective-permute-start.2 = (bf16[192,640]{1,0:T(8,128)(2,1)S(1)}, bf16[192,640]{1,0:T(8,128)(2,1)S(1)}, u32[]{:S(2)}, u32[]{:S(2)}) collective-permute-start(bf16[192,640]{1,0:T(8,128)(2,1)S(1)} %far.1.x0), channel_id=1, source_target_pairs={{0,32},{16,48},{32,64},{48,80},{64,96},{80,112},{96,128},{112,144}... | collective-permute-start | bytes 737288 | tf_op jit(solution)/shard_map/ppermute | solution.py:398
  18.2 2.7 %spatial_a1.1.x1.x0 = bf16[192,640]{1,0:T(8,128)(2,1)S(1)} custom-call(bf16[2,192,640]{2,1,0:T(8,128)(2,1)S(1)} %collective-permute-done.1.z, bf16[2,192,640]{2,1,0:T(8,128)(2,1)S(1)} %pack.1.mine, bf16[2,192,640]{2,1,0:T(8,128)(2,1)S(1)} %get-tuple-element.27.owned, bf16[192,640]{1,0:T(8,128)(2,1)S(1)} %get-tuple-element.28.sib_o, ...), custom_call_target="tpu_custom_call" | custom-call | flops 1274019840 | bytes 4000000 | tf_op jit(solution)/shard_map/spatial_a1/pallas_call | solution.py:423
  20.9 3.1 %collective-permute-start.5 = (bf16[192,640]{1,0:T(8,128)(2,1)S(1)}, bf16[192,640]{1,0:T(8,128)(2,1)S(1)}, u32[]{:S(2)}, u32[]{:S(2)}) collective-permute-start(bf16[192,640]{1,0:T(8,128)(2,1)S(1)} %spatial_a1.1.x1.x0), channel_id=1, source_target_pairs={{0,32},{16,48},{32,64},{48,80},{64,96},{80,112},{96,128},{112,144}... | collective-permute-start | bytes 737288 | tf_op jit(solution)/shard_map/ppermute | solution.py:398
  24.0 0.1 collective-permute-done.2.x2.x1
  24.1 0.4 temporal.2.own
  24.5 7.4 %collective-permute-start.4 = (bf16[192,640]{1,0:T(8,128)(2,1)S(1)}, bf16[192,640]{1,0:T(8,128)(2,1)S(1)}, u32[]{:S(2)}, u32[]{:S(2)}) collective-permute-start(bf16[192,640]{1,0:T(8,128)(2,1)S(1)} %temporal.2.own), channel_id=1, source_target_pairs={{0,16},{16,0},{32,48},{48,32},{64,80},{80,64},{96,112},{112,96},{1... | collective-permute-start | bytes 737288 | tf_op jit(solution)/shard_map/ppermute | solution.py:392
  31.9 1.9 %collective-permute-start.3 = (bf16[192,640]{1,0:T(8,128)(2,1)S(1)}, bf16[192,640]{1,0:T(8,128)(2,1)S(1)}, u32[]{:S(2)}, u32[]{:S(2)}) collective-permute-start(bf16[192,640]{1,0:T(8,128)(2,1)S(1)} %temporal.2.own), channel_id=1, source_target_pairs={{1,16},{2,17},{3,18},{4,19},{5,20},{6,21},{7,22},{8,23},{9,24},{10... | collective-permute-start | bytes 737288 | tf_op jit(solution)/shard_map/ppermute | solution.py:395
  33.8 0.0 collective-permute-done.5.x2
  33.8 0.4 temporal.3.own
  34.2 2.6 %collective-permute-start.7 = (bf16[192,640]{1,0:T(8,128)(2,1)S(1)}, bf16[192,640]{1,0:T(8,128)(2,1)S(1)}, u32[]{:S(2)}, u32[]{:S(2)}) collective-permute-start(bf16[192,640]{1,0:T(8,128)(2,1)S(1)} %temporal.3.own), channel_id=1, source_target_pairs={{0,16},{16,0},{32,48},{48,32},{64,80},{80,64},{96,112},{112,96},{1... | collective-permute-start | bytes 737288 | tf_op jit(solution)/shard_map/ppermute | solution.py:392
  36.8 2.1 %collective-permute-start.6 = (bf16[192,640]{1,0:T(8,128)(2,1)S(1)}, bf16[192,640]{1,0:T(8,128)(2,1)S(1)}, u32[]{:S(2)}, u32[]{:S(2)}) collective-permute-start(bf16[192,640]{1,0:T(8,128)(2,1)S(1)} %temporal.3.own), channel_id=1, source_target_pairs={{1,16},{2,17},{3,18},{4,19},{5,20},{6,21},{7,22},{8,23},{9,24},{10... | collective-permute-start | bytes 737288 | tf_op jit(solution)/shard_map/ppermute | solution.py:395
  38.9 0.0 collective-permute-done.4.sib
  38.9 0.5 collective-permute-done.3.z
  39.4 2.6 %spatial_b.1.x0 = bf16[192,640]{1,0:T(8,128)(2,1)S(1)} custom-call(bf16[192,640]{1,0:T(8,128)(2,1)S(1)} %collective-permute-done.3.z, bf16[192,640]{1,0:T(8,128)(2,1)S(1)} %temporal.2.own, bf16[192,640]{1,0:T(8,128)(2,1)S(1)} %collective-permute-done.4.sib, bf16[576,576]{1,0:T(8,128)(2,1)S(1)} %get-tuple-element.37.rest_0_, ...), custom_call_target="tpu_custom_call" | custom-call | flops 1274019840 | bytes 4000000 | tf_op jit(solution)/shard_map/spatial_b/pallas_call | solution.py:431
  42.0 2.3 %collective-permute-start.8 = (bf16[192,640]{1,0:T(8,128)(2,1)S(1)}, bf16[192,640]{1,0:T(8,128)(2,1)S(1)}, u32[]{:S(2)}, u32[]{:S(2)}) collective-permute-start(bf16[192,640]{1,0:T(8,128)(2,1)S(1)} %spatial_b.1.x0), channel_id=1, source_target_pairs={{0,32},{16,48},{32,64},{48,80},{64,96},{80,112},{96,128},{112,144}... | collective-permute-start | bytes 737288 | tf_op jit(solution)/shard_map/ppermute | solution.py:398
  44.3 0.0 collective-permute-done.7.sib
  44.3 0.0 collective-permute-done.6.z
  44.3 2.6 %spatial_a.1.x1.y0 = bf16[192,640]{1,0:T(8,128)(2,1)S(1)} custom-call(bf16[192,640]{1,0:T(8,128)(2,1)S(1)} %collective-permute-done.6.z, bf16[192,640]{1,0:T(8,128)(2,1)S(1)} %temporal.3.own, bf16[192,640]{1,0:T(8,128)(2,1)S(1)} %collective-permute-done.7.sib, bf16[576,576]{1,0:T(8,128)(2,1)S(1)} %get-tuple-element.37.rest_0_, ...), custom_call_target="tpu_custom_call" | custom-call | flops 1274019840 | bytes 4000000 | tf_op jit(solution)/shard_map/spatial_a/pallas_call | solution.py:433
  46.9 2.7 %collective-permute-start.9 = (bf16[192,640]{1,0:T(8,128)(2,1)S(1)}, bf16[192,640]{1,0:T(8,128)(2,1)S(1)}, u32[]{:S(2)}, u32[]{:S(2)}) collective-permute-start(bf16[192,640]{1,0:T(8,128)(2,1)S(1)} %spatial_a.1.x1.y0), channel_id=1, source_target_pairs={{0,32},{16,48},{32,64},{48,80},{64,96},{80,112},{96,128},{112,144}... | collective-permute-start | bytes 737288 | tf_op jit(solution)/shard_map/ppermute | solution.py:398
  49.7 1.4 %collective-permute-done.8.x2 = bf16[192,640]{1,0:T(8,128)(2,1)S(1)} collective-permute-done((bf16[192,640]{1,0:T(8,128)(2,1)S(1)}, bf16[192,640]{1,0:T(8,128)(2,1)S(1)}, u32[]{:S(2)}, u32[]{:S(2)}) %collective-permute-start.8) | collective-permute-done | bytes 245792 | tf_op jit(solution)/shard_map/ppermute | solution.py:398
  51.0 0.6 temporal_late.1
  51.6 6.7 %collective-permute-done.9.y2 = bf16[192,640]{1,0:T(8,128)(2,1)S(1)} collective-permute-done((bf16[192,640]{1,0:T(8,128)(2,1)S(1)}, bf16[192,640]{1,0:T(8,128)(2,1)S(1)}, u32[]{:S(2)}, u32[]{:S(2)}) %collective-permute-start.9) | collective-permute-done | bytes 245792 | tf_op jit(solution)/shard_map/ppermute | solution.py:398
  58.4 0.2 temporal_last.1
  58.6 2.8 %collective-permute-start.10 = (bf16[192,640]{1,0:T(8,128)(2,1)S(1)}, bf16[192,640]{1,0:T(8,128)(2,1)S(1)}, u32[]{:S(2)}, u32[]{:S(2)}) collective-permute-start(bf16[192,640]{1,0:T(8,128)(2,1)S(1)} %get-tuple-element.43), channel_id=1, source_target_pairs={{0,16},{16,0},{32,48},{48,32},{64,80},{80,64},{96,112},{112,96},{1... | collective-permute-start | bytes 737288 | tf_op jit(solution)/shard_map/ppermute | solution.py:392
  61.4 0.8 %unpack.2.part = bf16[4,192,320]{2,1,0:T(8,128)(2,1)} custom-call(bf16[192,640]{1,0:T(8,128)(2,1)S(1)} %get-tuple-element.44.keep), custom_call_target="tpu_custom_call" | custom-call | bytes 500000 | tf_op jit(solution)/shard_map/unpack/pallas_call | solution.py:148
  62.2 0.3 collective-permute-done.10.got
  62.6 0.8 %unpack.3 = bf16[4,192,320]{2,1,0:T(8,128)(2,1)} custom-call(bf16[192,640]{1,0:T(8,128)(2,1)S(1)} %collective-permute-done.10.got, bf16[4,192,320]{2,1,0:T(8,128)(2,1)} %unpack.2.part), custom_call_target="tpu_custom_call", output_to_operand_aliasing={{}: (1, {})} | custom-call | bytes 500000 | tf_op jit(solution)/shard_map/unpack/pallas_call | solution.py:148
Async XLA Ops:
  0.0 2.5 %collective-permute-start = (bf16[4,192,320]{2,1,0:T(8,128)(2,1)}, bf16[4,192,320]{2,1,0:T(8,128)(2,1)S(1)}, u32[]{:S(2)}, u32[]{:S(2)}) collective-permute-start(bf16[4,192,320]{2,1,0:T(8,128)(2,1)} %bitcast.6), channel_id=1, source_target_pairs={{0,16},{16,0},{32,48},{48,32},{64,80},{80,64},{96,112},{112,96},{1... | collective-permute-start | bytes 1474568 | tf_op jit(solution)/shard_map/ppermute | solution.py:392
  2.7 10.6 %collective-permute-start.1 = (bf16[2,192,640]{2,1,0:T(8,128)(2,1)S(1)}, bf16[2,192,640]{2,1,0:T(8,128)(2,1)S(1)}, u32[]{:S(2)}, u32[]{:S(2)}) collective-permute-start(bf16[2,192,640]{2,1,0:T(8,128)(2,1)S(1)} %get-tuple-element.27.owned), channel_id=1, source_target_pairs={{1,16},{2,17},{3,18},{4,19},{5,20},{6,21},{7,22},{8,23},{9,24},{10... | collective-permute-start | bytes 1474568 | tf_op jit(solution)/shard_map/ppermute | solution.py:395
  15.0 9.1 %collective-permute-start.2 = (bf16[192,640]{1,0:T(8,128)(2,1)S(1)}, bf16[192,640]{1,0:T(8,128)(2,1)S(1)}, u32[]{:S(2)}, u32[]{:S(2)}) collective-permute-start(bf16[192,640]{1,0:T(8,128)(2,1)S(1)} %far.1.x0), channel_id=1, source_target_pairs={{0,32},{16,48},{32,64},{48,80},{64,96},{80,112},{96,128},{112,144}... | collective-permute-start | bytes 737288 | tf_op jit(solution)/shard_map/ppermute | solution.py:398
  20.9 13.0 %collective-permute-start.5 = (bf16[192,640]{1,0:T(8,128)(2,1)S(1)}, bf16[192,640]{1,0:T(8,128)(2,1)S(1)}, u32[]{:S(2)}, u32[]{:S(2)}) collective-permute-start(bf16[192,640]{1,0:T(8,128)(2,1)S(1)} %spatial_a1.1.x1.x0), channel_id=1, source_target_pairs={{0,32},{16,48},{32,64},{48,80},{64,96},{80,112},{96,128},{112,144}... | collective-permute-start | bytes 737288 | tf_op jit(solution)/shard_map/ppermute | solution.py:398
  24.5 14.4 %collective-permute-start.4 = (bf16[192,640]{1,0:T(8,128)(2,1)S(1)}, bf16[192,640]{1,0:T(8,128)(2,1)S(1)}, u32[]{:S(2)}, u32[]{:S(2)}) collective-permute-start(bf16[192,640]{1,0:T(8,128)(2,1)S(1)} %temporal.2.own), channel_id=1, source_target_pairs={{0,16},{16,0},{32,48},{48,32},{64,80},{80,64},{96,112},{112,96},{1... | collective-permute-start | bytes 737288 | tf_op jit(solution)/shard_map/ppermute | solution.py:392
  31.9 7.5 %collective-permute-start.3 = (bf16[192,640]{1,0:T(8,128)(2,1)S(1)}, bf16[192,640]{1,0:T(8,128)(2,1)S(1)}, u32[]{:S(2)}, u32[]{:S(2)}) collective-permute-start(bf16[192,640]{1,0:T(8,128)(2,1)S(1)} %temporal.2.own), channel_id=1, source_target_pairs={{1,16},{2,17},{3,18},{4,19},{5,20},{6,21},{7,22},{8,23},{9,24},{10... | collective-permute-start | bytes 737288 | tf_op jit(solution)/shard_map/ppermute | solution.py:395
  34.2 10.0 %collective-permute-start.7 = (bf16[192,640]{1,0:T(8,128)(2,1)S(1)}, bf16[192,640]{1,0:T(8,128)(2,1)S(1)}, u32[]{:S(2)}, u32[]{:S(2)}) collective-permute-start(bf16[192,640]{1,0:T(8,128)(2,1)S(1)} %temporal.3.own), channel_id=1, source_target_pairs={{0,16},{16,0},{32,48},{48,32},{64,80},{80,64},{96,112},{112,96},{1... | collective-permute-start | bytes 737288 | tf_op jit(solution)/shard_map/ppermute | solution.py:392
  36.8 7.5 %collective-permute-start.6 = (bf16[192,640]{1,0:T(8,128)(2,1)S(1)}, bf16[192,640]{1,0:T(8,128)(2,1)S(1)}, u32[]{:S(2)}, u32[]{:S(2)}) collective-permute-start(bf16[192,640]{1,0:T(8,128)(2,1)S(1)} %temporal.3.own), channel_id=1, source_target_pairs={{1,16},{2,17},{3,18},{4,19},{5,20},{6,21},{7,22},{8,23},{9,24},{10... | collective-permute-start | bytes 737288 | tf_op jit(solution)/shard_map/ppermute | solution.py:395
  42.0 9.1 %collective-permute-start.8 = (bf16[192,640]{1,0:T(8,128)(2,1)S(1)}, bf16[192,640]{1,0:T(8,128)(2,1)S(1)}, u32[]{:S(2)}, u32[]{:S(2)}) collective-permute-start(bf16[192,640]{1,0:T(8,128)(2,1)S(1)} %spatial_b.1.x0), channel_id=1, source_target_pairs={{0,32},{16,48},{32,64},{48,80},{64,96},{80,112},{96,128},{112,144}... | collective-permute-start | bytes 737288 | tf_op jit(solution)/shard_map/ppermute | solution.py:398
  46.9 11.5 %collective-permute-start.9 = (bf16[192,640]{1,0:T(8,128)(2,1)S(1)}, bf16[192,640]{1,0:T(8,128)(2,1)S(1)}, u32[]{:S(2)}, u32[]{:S(2)}) collective-permute-start(bf16[192,640]{1,0:T(8,128)(2,1)S(1)} %spatial_a.1.x1.y0), channel_id=1, source_target_pairs={{0,32},{16,48},{32,64},{48,80},{64,96},{80,112},{96,128},{112,144}... | collective-permute-start | bytes 737288 | tf_op jit(solution)/shard_map/ppermute | solution.py:398
  58.6 4.0 %collective-permute-start.10 = (bf16[192,640]{1,0:T(8,128)(2,1)S(1)}, bf16[192,640]{1,0:T(8,128)(2,1)S(1)}, u32[]{:S(2)}, u32[]{:S(2)}) collective-permute-start(bf16[192,640]{1,0:T(8,128)(2,1)S(1)} %get-tuple-element.43), channel_id=1, source_target_pairs={{0,16},{16,0},{32,48},{48,32},{64,80},{80,64},{96,112},{112,96},{1... | collective-permute-start | bytes 737288 | tf_op jit(solution)/shard_map/ppermute | solution.py:392

commit v7 on v6

--- a/solution.py
+++ b/solution.py
@@ -135,27 +135,33 @@
         copy.wait()
 
 
-def unpack_keep_kernel(keep, out, rows, sems):
-    unpack_rows(keep, out, rows, sems, core_index())
-
-
-def unpack_got_kernel(got, part, out, rows, sems):
+def store_later_kernel(mine, other, out, rows, sems):
+    @pl.when(core_index() == 1)
+    def _():
+        unpack_rows(mine, out, rows, sems, 1)
+        unpack_rows(other, out, rows, sems, 0)
+
+
+def store_earlier_kernel(pair, x, part, out, rows, sems):
     del part
-    unpack_rows(got, out, rows, sems, 1 - core_index())
-
-
-def unpack(kernel, x, *part):
+
+    @pl.when(core_index() == 0)
+    def _():
+        unpack_rows(x, out, rows, sems, pair)
+
+
+def store(kernel, arrays, *part):
     return call(
         kernel,
         jax.ShapeDtypeStruct((4, C, W), BF16),
-        1 + len(part),
-        "unpack",
+        len(arrays) + len(part),
+        "store",
         scratch=[pltpu.VMEM((2, C, W), BF16), pltpu.SemaphoreType.DMA((2,))],
         moved=500000,
-        in_specs=[VMEM] + [ANY] * len(part),
+        in_specs=[VMEM] * len(arrays) + [ANY] * len(part),
         out_specs=ANY,
-        aliases={1: 0} if part else None,
-    )(x, *part)
+        aliases={len(arrays): 0} if part else None,
+    )(*arrays, *part)
 
 
 def tiles_of(x):
@@ -368,13 +374,9 @@
     part[...] = total
 
 
-def temporal_last_kernel(wt, part, y2, late, keep, send):
-    early = part[...] + jnp.dot(wt[:, 2 * C :], y2[...], preferred_element_type=F32)
-    early = early.astype(BF16)
-    is0 = core_index() == 0
-    other = late[...]
-    keep[...] = jnp.where(is0, early, other)
-    send[...] = jnp.where(is0, other, early)
+def temporal_last_kernel(wt, part, y2, out):
+    last = jnp.dot(wt[:, 2 * C :], y2[...], preferred_element_type=F32)
+    out[...] = (part[...] + last).astype(BF16)
 
 
 def on_device(video, spatial_weights, norm_gains, temporal_weights):
@@ -439,11 +441,12 @@
         "temporal_late",
         moved=2000000,
     )(ts[1], inner_b, inner_a, before_b, inner_a)
-    keep, send = call(temporal_last_kernel, [pair_shape()] * 2, 4, "temporal_last", moved=1500000)(
-        ts[1], part, before_a, late
-    )
-    got = swap(send)
-    out = unpack(unpack_got_kernel, got, unpack(unpack_keep_kernel, keep))
+    late_other = swap(late)
+    out = store(store_later_kernel, (late, late_other))
+    early = call(temporal_last_kernel, pair_shape(), 3, "temporal_last", moved=1500000)(ts[1], part, before_a)
+    early_other = swap(early)
+    out = store(functools.partial(store_earlier_kernel, 0), (early,), out)
+    out = store(functools.partial(store_earlier_kernel, 1), (early_other,), out)
     return jnp.transpose(out, (0, 2, 1))[None]
 
 

time: 63.8 us -> 63.6 us (level)
  waiting for transfers between devices: 9.95 us -> 2.89 us
  starting transfers between devices: 32.5 us -> 39.3 us
    ppermute x4, waiting for transfers between devices: 8.23 us -> 1.5 us  [onward(): return lax.ppermute(x, 'frames', later)]
    ppermute x4 -> x5, starting transfers between devices: 13.5 us -> 20.2 us  [swap(): return lax.ppermute(x, 'frames', swaps)]
    pallas_call x3 -> x4, Pallas kernels: 1.82 us -> 1.88 us  [the longest x3 1.65 us: store(): call(kernel, jax.ShapeDtypeStruct((4, C, W), BF16), len(arrays) + len(par...]
  transfers between devices with their start and end apart: 11 -> 12, of which waited for: 7 -> 5; matrix products, arithmetic and copies ran while one was open for 0% -> 0% of each run, Pallas kernels for 28% -> 30%
where the time goes in v7:
time: 63.6 us; the launch traced here: 63.3 us
  starting transfers between devices  39.3 us (62%)
  Pallas kernels  20.8 us (33%)
  waiting for transfers between devices  2.89 us (5%)
    ppermute x5, starting transfers between devices, swap(): return lax.ppermute(x, 'frames', swaps)  20.2 us
    ppermute x4, starting transfers between devices, onward(): return lax.ppermute(x, 'frames', later)  11.3 us
    ppermute x3, starting transfers between devices, halo(): return lax.ppermute(x, ('frames', 'rows'), across)  7.8 us
    pallas_call x1, Pallas kernels, prepare(): call(weights_kernel, [shape((3 * C, 3 * C), BF16)] * 6 + [shape((C, LANES...  4.17 us
    pallas_call x1, Pallas kernels, on_device(): spatial(functools.partial(spatial_pick_kernel, 0), 8, 'spatial_a1')  2.7 us
    pallas_call x1, Pallas kernels, on_device(): inner_b = spatial(spatial_kernel, 7, 'spatial_b')(z_b, own_b, sib_b, *both)  2.58 us
    pallas_call x1, Pallas kernels, on_device(): inner_a = spatial(spatial_kernel, 7, 'spatial_a')(z_a, own_a, sib_a, *both)  2.58 us
    pallas_call x1, Pallas kernels, near(): call(functools.partial(near_pick_kernel, pick), [jax.ShapeDtypeStruct((C,...  2.3 us
  transfers between devices with their start and end apart: 12, of which 5 were waited for; matrix products, arithmetic and copies ran while one was open for 0% of the time, Pallas kernels for 30%

profile of v7, /device:TPU:25, one launch (start us, length us, event | category | flops | bytes accessed | tf_op | source)
XLA Modules:
  0.0 63.3 jit_solution(5012135131583190354)
XLA Ops:
  0.0 0.7 %collective-permute-start = (bf16[4,192,320]{2,1,0:T(8,128)(2,1)}, bf16[4,192,320]{2,1,0:T(8,128)(2,1)S(1)}, u32[]{:S(2)}, u32[]{:S(2)}) collective-permute-start(bf16[4,192,320]{2,1,0:T(8,128)(2,1)} %bitcast.6), channel_id=1, source_target_pairs={{0,16},{16,0},{32,48},{48,32},{64,80},{80,64},{96,112},{112,96},{1... | collective-permute-start | bytes 1474568 | tf_op jit(solution)/shard_map/ppermute | solution.py:394
  0.7 1.3 %pack.1.mine = bf16[2,192,640]{2,1,0:T(8,128)(2,1)S(1)} custom-call(bf16[4,192,320]{2,1,0:T(8,128)(2,1)} %bitcast.7), custom_call_target="tpu_custom_call" | custom-call | bytes 1000000 | tf_op jit(solution)/shard_map/pack/pallas_call | solution.py:404
  2.0 0.6 collective-permute-done.other
  2.5 0.2 join.1
  2.7 3.8 %collective-permute-start.1 = (bf16[2,192,640]{2,1,0:T(8,128)(2,1)S(1)}, bf16[2,192,640]{2,1,0:T(8,128)(2,1)S(1)}, u32[]{:S(2)}, u32[]{:S(2)}) collective-permute-start(bf16[2,192,640]{2,1,0:T(8,128)(2,1)S(1)} %get-tuple-element.25.owned), channel_id=1, source_target_pairs={{1,16},{2,17},{3,18},{4,19},{5,20},{6,21},{7,22},{8,23},{9,24},{10... | collective-permute-start | bytes 1474568 | tf_op jit(solution)/shard_map/ppermute | solution.py:397
  6.5 4.2 %weights.1 = (bf16[576,576]{1,0:T(8,128)(2,1)S(1)}, bf16[576,576]{1,0:T(8,128)(2,1)S(1)}, bf16[576,576]{1,0:T(8,128)(2,1)S(1)}, bf16[576,576]{1,0:T(8,128)(2,1)S...) custom-call(bf16[4,3,3,192,192]{4,3,2,1,0:T(8,128)(2,1)} %sw.1, ...), custom_call_target="tpu_custom_call" | custom-call | bytes 6000000 | tf_op jit(solution)/shard_map/weights/pallas_call | solution.py:87
  10.7 2.3 %near.1 = (f32[192,640]{1,0:T(8,128)S(1)}, f32[192,640]{1,0:T(8,128)S(1)}) custom-call(bf16[2,192,640]{2,1,0:T(8,128)(2,1)S(1)} %pack.1.mine, bf16[2,192,640]{2,1,0:T(8,128)(2,1)S(1)} %get-tuple-element.25.owned, bf16[192,640]{1,0:T(8,128)(2,1)S(1)} %get-tuple-element.26.sib_o, bf16[576,576]{1,0:T(8,128)(2,1)S(1)} %get-tuple-element.27.w1, ...), custom_call_target="tpu_custom_call" | custom-call | flops 424673280 | bytes 2000000 | tf_op jit(solution)/shard_map/near/pallas_call | solution.py:258
  13.0 0.3 collective-permute-done.1.z
  13.3 1.7 %far.1.x0 = bf16[192,640]{1,0:T(8,128)(2,1)S(1)} custom-call(bf16[2,192,640]{2,1,0:T(8,128)(2,1)S(1)} %collective-permute-done.1.z, f32[192,640]{1,0:T(8,128)S(1)} %get-tuple-element.31.part1, f32[192,640]{1,0:T(8,128)S(1)} %get-tuple-element.32.part2, bf16[576,576]{1,0:T(8,128)(2,1)S(1)} %get-tuple-element.27.w1, ...), custom_call_target="tpu_custom_call" | custom-call | flops 849346560 | bytes 4000000 | tf_op jit(solution)/shard_map/far/pallas_call | solution.py:287
  15.0 3.1 %collective-permute-start.2 = (bf16[192,640]{1,0:T(8,128)(2,1)S(1)}, bf16[192,640]{1,0:T(8,128)(2,1)S(1)}, u32[]{:S(2)}, u32[]{:S(2)}) collective-permute-start(bf16[192,640]{1,0:T(8,128)(2,1)S(1)} %far.1.x0), channel_id=1, source_target_pairs={{0,32},{16,48},{32,64},{48,80},{64,96},{80,112},{96,128},{112,144}... | collective-permute-start | bytes 737288 | tf_op jit(solution)/shard_map/ppermute | solution.py:400
  18.2 2.7 %spatial_a1.1.x1.x0 = bf16[192,640]{1,0:T(8,128)(2,1)S(1)} custom-call(bf16[2,192,640]{2,1,0:T(8,128)(2,1)S(1)} %collective-permute-done.1.z, bf16[2,192,640]{2,1,0:T(8,128)(2,1)S(1)} %pack.1.mine, bf16[2,192,640]{2,1,0:T(8,128)(2,1)S(1)} %get-tuple-element.25.owned, bf16[192,640]{1,0:T(8,128)(2,1)S(1)} %get-tuple-element.26.sib_o, ...), custom_call_target="tpu_custom_call" | custom-call | flops 1274019840 | bytes 4000000 | tf_op jit(solution)/shard_map/spatial_a1/pallas_call | solution.py:425
  20.9 3.1 %collective-permute-start.5 = (bf16[192,640]{1,0:T(8,128)(2,1)S(1)}, bf16[192,640]{1,0:T(8,128)(2,1)S(1)}, u32[]{:S(2)}, u32[]{:S(2)}) collective-permute-start(bf16[192,640]{1,0:T(8,128)(2,1)S(1)} %spatial_a1.1.x1.x0), channel_id=1, source_target_pairs={{0,32},{16,48},{32,64},{48,80},{64,96},{80,112},{96,128},{112,144}... | collective-permute-start | bytes 737288 | tf_op jit(solution)/shard_map/ppermute | solution.py:400
  24.0 0.1 collective-permute-done.2.x2.x1
  24.1 0.4 temporal.2.own
  24.5 7.4 %collective-permute-start.4 = (bf16[192,640]{1,0:T(8,128)(2,1)S(1)}, bf16[192,640]{1,0:T(8,128)(2,1)S(1)}, u32[]{:S(2)}, u32[]{:S(2)}) collective-permute-start(bf16[192,640]{1,0:T(8,128)(2,1)S(1)} %temporal.2.own), channel_id=1, source_target_pairs={{0,16},{16,0},{32,48},{48,32},{64,80},{80,64},{96,112},{112,96},{1... | collective-permute-start | bytes 737288 | tf_op jit(solution)/shard_map/ppermute | solution.py:394
  31.9 1.9 %collective-permute-start.3 = (bf16[192,640]{1,0:T(8,128)(2,1)S(1)}, bf16[192,640]{1,0:T(8,128)(2,1)S(1)}, u32[]{:S(2)}, u32[]{:S(2)}) collective-permute-start(bf16[192,640]{1,0:T(8,128)(2,1)S(1)} %temporal.2.own), channel_id=1, source_target_pairs={{1,16},{2,17},{3,18},{4,19},{5,20},{6,21},{7,22},{8,23},{9,24},{10... | collective-permute-start | bytes 737288 | tf_op jit(solution)/shard_map/ppermute | solution.py:397
  33.8 0.0 collective-permute-done.5.x2
  33.8 0.4 temporal.3.own
  34.2 2.6 %collective-permute-start.7 = (bf16[192,640]{1,0:T(8,128)(2,1)S(1)}, bf16[192,640]{1,0:T(8,128)(2,1)S(1)}, u32[]{:S(2)}, u32[]{:S(2)}) collective-permute-start(bf16[192,640]{1,0:T(8,128)(2,1)S(1)} %temporal.3.own), channel_id=1, source_target_pairs={{0,16},{16,0},{32,48},{48,32},{64,80},{80,64},{96,112},{112,96},{1... | collective-permute-start | bytes 737288 | tf_op jit(solution)/shard_map/ppermute | solution.py:394
  36.8 2.1 %collective-permute-start.6 = (bf16[192,640]{1,0:T(8,128)(2,1)S(1)}, bf16[192,640]{1,0:T(8,128)(2,1)S(1)}, u32[]{:S(2)}, u32[]{:S(2)}) collective-permute-start(bf16[192,640]{1,0:T(8,128)(2,1)S(1)} %temporal.3.own), channel_id=1, source_target_pairs={{1,16},{2,17},{3,18},{4,19},{5,20},{6,21},{7,22},{8,23},{9,24},{10... | collective-permute-start | bytes 737288 | tf_op jit(solution)/shard_map/ppermute | solution.py:397
  38.9 0.0 collective-permute-done.4.sib
  38.9 0.5 collective-permute-done.3.z
  39.4 2.6 %spatial_b.1.x0 = bf16[192,640]{1,0:T(8,128)(2,1)S(1)} custom-call(bf16[192,640]{1,0:T(8,128)(2,1)S(1)} %collective-permute-done.3.z, bf16[192,640]{1,0:T(8,128)(2,1)S(1)} %temporal.2.own, bf16[192,640]{1,0:T(8,128)(2,1)S(1)} %collective-permute-done.4.sib, bf16[576,576]{1,0:T(8,128)(2,1)S(1)} %get-tuple-element.35.rest_0_, ...), custom_call_target="tpu_custom_call" | custom-call | flops 1274019840 | bytes 4000000 | tf_op jit(solution)/shard_map/spatial_b/pallas_call | solution.py:433
  42.0 2.3 %collective-permute-start.8 = (bf16[192,640]{1,0:T(8,128)(2,1)S(1)}, bf16[192,640]{1,0:T(8,128)(2,1)S(1)}, u32[]{:S(2)}, u32[]{:S(2)}) collective-permute-start(bf16[192,640]{1,0:T(8,128)(2,1)S(1)} %spatial_b.1.x0), channel_id=1, source_target_pairs={{0,32},{16,48},{32,64},{48,80},{64,96},{80,112},{96,128},{112,144}... | collective-permute-start | bytes 737288 | tf_op jit(solution)/shard_map/ppermute | solution.py:400
  44.3 0.0 collective-permute-done.7.sib
  44.3 0.0 collective-permute-done.6.z
  44.3 2.6 %spatial_a.1.x1.y0 = bf16[192,640]{1,0:T(8,128)(2,1)S(1)} custom-call(bf16[192,640]{1,0:T(8,128)(2,1)S(1)} %collective-permute-done.6.z, bf16[192,640]{1,0:T(8,128)(2,1)S(1)} %temporal.3.own, bf16[192,640]{1,0:T(8,128)(2,1)S(1)} %collective-permute-done.7.sib, bf16[576,576]{1,0:T(8,128)(2,1)S(1)} %get-tuple-element.35.rest_0_, ...), custom_call_target="tpu_custom_call" | custom-call | flops 1274019840 | bytes 4000000 | tf_op jit(solution)/shard_map/spatial_a/pallas_call | solution.py:435
  46.9 2.7 %collective-permute-start.9 = (bf16[192,640]{1,0:T(8,128)(2,1)S(1)}, bf16[192,640]{1,0:T(8,128)(2,1)S(1)}, u32[]{:S(2)}, u32[]{:S(2)}) collective-permute-start(bf16[192,640]{1,0:T(8,128)(2,1)S(1)} %spatial_a.1.x1.y0), channel_id=1, source_target_pairs={{0,32},{16,48},{32,64},{48,80},{64,96},{80,112},{96,128},{112,144}... | collective-permute-start | bytes 737288 | tf_op jit(solution)/shard_map/ppermute | solution.py:400
  49.7 1.4 %collective-permute-done.8.x2 = bf16[192,640]{1,0:T(8,128)(2,1)S(1)} collective-permute-done((bf16[192,640]{1,0:T(8,128)(2,1)S(1)}, bf16[192,640]{1,0:T(8,128)(2,1)S(1)}, u32[]{:S(2)}, u32[]{:S(2)}) %collective-permute-start.8) | collective-permute-done | bytes 245792 | tf_op jit(solution)/shard_map/ppermute | solution.py:400
  51.0 0.6 temporal_late.1
  51.6 6.7 %collective-permute-start.11 = (bf16[192,640]{1,0:T(8,128)(2,1)S(1)}, bf16[192,640]{1,0:T(8,128)(2,1)S(1)}, u32[]{:S(2)}, u32[]{:S(2)}) collective-permute-start(bf16[192,640]{1,0:T(8,128)(2,1)S(1)} %get-tuple-element.40.mine), channel_id=1, source_target_pairs={{0,16},{16,0},{32,48},{48,32},{64,80},{80,64},{96,112},{112,96},{1... | collective-permute-start | bytes 737288 | tf_op jit(solution)/shard_map/ppermute | solution.py:394
  58.4 0.0 collective-permute-done.9.y2
  58.4 0.2 temporal_last.1.x
  58.6 2.8 %collective-permute-start.10 = (bf16[192,640]{1,0:T(8,128)(2,1)S(1)}, bf16[192,640]{1,0:T(8,128)(2,1)S(1)}, u32[]{:S(2)}, u32[]{:S(2)}) collective-permute-start(bf16[192,640]{1,0:T(8,128)(2,1)S(1)} %temporal_last.1.x), channel_id=1, source_target_pairs={{0,16},{16,0},{32,48},{48,32},{64,80},{80,64},{96,112},{112,96},{1... | collective-permute-start | bytes 737288 | tf_op jit(solution)/shard_map/ppermute | solution.py:394
  61.4 0.0 collective-permute-done.11.other
  61.4 1.6 %store.3.part = bf16[4,192,320]{2,1,0:T(8,128)(2,1)} custom-call(bf16[192,640]{1,0:T(8,128)(2,1)S(1)} %get-tuple-element.40.mine, bf16[192,640]{1,0:T(8,128)(2,1)S(1)} %collective-permute-done.11.other), custom_call_target="tpu_custom_call" | custom-call | bytes 500000 | tf_op jit(solution)/shard_map/store/pallas_call | solution.py:154
  63.1 0.0 collective-permute-done.10.x
  (2 shorter events, 0.1 us)
Async XLA Ops:
  0.0 2.5 %collective-permute-start = (bf16[4,192,320]{2,1,0:T(8,128)(2,1)}, bf16[4,192,320]{2,1,0:T(8,128)(2,1)S(1)}, u32[]{:S(2)}, u32[]{:S(2)}) collective-permute-start(bf16[4,192,320]{2,1,0:T(8,128)(2,1)} %bitcast.6), channel_id=1, source_target_pairs={{0,16},{16,0},{32,48},{48,32},{64,80},{80,64},{96,112},{112,96},{1... | collective-permute-start | bytes 1474568 | tf_op jit(solution)/shard_map/ppermute | solution.py:394
  2.7 10.6 %collective-permute-start.1 = (bf16[2,192,640]{2,1,0:T(8,128)(2,1)S(1)}, bf16[2,192,640]{2,1,0:T(8,128)(2,1)S(1)}, u32[]{:S(2)}, u32[]{:S(2)}) collective-permute-start(bf16[2,192,640]{2,1,0:T(8,128)(2,1)S(1)} %get-tuple-element.25.owned), channel_id=1, source_target_pairs={{1,16},{2,17},{3,18},{4,19},{5,20},{6,21},{7,22},{8,23},{9,24},{10... | collective-permute-start | bytes 1474568 | tf_op jit(solution)/shard_map/ppermute | solution.py:397
  15.0 9.1 %collective-permute-start.2 = (bf16[192,640]{1,0:T(8,128)(2,1)S(1)}, bf16[192,640]{1,0:T(8,128)(2,1)S(1)}, u32[]{:S(2)}, u32[]{:S(2)}) collective-permute-start(bf16[192,640]{1,0:T(8,128)(2,1)S(1)} %far.1.x0), channel_id=1, source_target_pairs={{0,32},{16,48},{32,64},{48,80},{64,96},{80,112},{96,128},{112,144}... | collective-permute-start | bytes 737288 | tf_op jit(solution)/shard_map/ppermute | solution.py:400
  20.9 13.0 %collective-permute-start.5 = (bf16[192,640]{1,0:T(8,128)(2,1)S(1)}, bf16[192,640]{1,0:T(8,128)(2,1)S(1)}, u32[]{:S(2)}, u32[]{:S(2)}) collective-permute-start(bf16[192,640]{1,0:T(8,128)(2,1)S(1)} %spatial_a1.1.x1.x0), channel_id=1, source_target_pairs={{0,32},{16,48},{32,64},{48,80},{64,96},{80,112},{96,128},{112,144}... | collective-permute-start | bytes 737288 | tf_op jit(solution)/shard_map/ppermute | solution.py:400
  24.5 14.4 %collective-permute-start.4 = (bf16[192,640]{1,0:T(8,128)(2,1)S(1)}, bf16[192,640]{1,0:T(8,128)(2,1)S(1)}, u32[]{:S(2)}, u32[]{:S(2)}) collective-permute-start(bf16[192,640]{1,0:T(8,128)(2,1)S(1)} %temporal.2.own), channel_id=1, source_target_pairs={{0,16},{16,0},{32,48},{48,32},{64,80},{80,64},{96,112},{112,96},{1... | collective-permute-start | bytes 737288 | tf_op jit(solution)/shard_map/ppermute | solution.py:394
  31.9 7.5 %collective-permute-start.3 = (bf16[192,640]{1,0:T(8,128)(2,1)S(1)}, bf16[192,640]{1,0:T(8,128)(2,1)S(1)}, u32[]{:S(2)}, u32[]{:S(2)}) collective-permute-start(bf16[192,640]{1,0:T(8,128)(2,1)S(1)} %temporal.2.own), channel_id=1, source_target_pairs={{1,16},{2,17},{3,18},{4,19},{5,20},{6,21},{7,22},{8,23},{9,24},{10... | collective-permute-start | bytes 737288 | tf_op jit(solution)/shard_map/ppermute | solution.py:397
  34.2 10.0 %collective-permute-start.7 = (bf16[192,640]{1,0:T(8,128)(2,1)S(1)}, bf16[192,640]{1,0:T(8,128)(2,1)S(1)}, u32[]{:S(2)}, u32[]{:S(2)}) collective-permute-start(bf16[192,640]{1,0:T(8,128)(2,1)S(1)} %temporal.3.own), channel_id=1, source_target_pairs={{0,16},{16,0},{32,48},{48,32},{64,80},{80,64},{96,112},{112,96},{1... | collective-permute-start | bytes 737288 | tf_op jit(solution)/shard_map/ppermute | solution.py:394
  36.8 7.5 %collective-permute-start.6 = (bf16[192,640]{1,0:T(8,128)(2,1)S(1)}, bf16[192,640]{1,0:T(8,128)(2,1)S(1)}, u32[]{:S(2)}, u32[]{:S(2)}) collective-permute-start(bf16[192,640]{1,0:T(8,128)(2,1)S(1)} %temporal.3.own), channel_id=1, source_target_pairs={{1,16},{2,17},{3,18},{4,19},{5,20},{6,21},{7,22},{8,23},{9,24},{10... | collective-permute-start | bytes 737288 | tf_op jit(solution)/shard_map/ppermute | solution.py:397
  42.0 9.1 %collective-permute-start.8 = (bf16[192,640]{1,0:T(8,128)(2,1)S(1)}, bf16[192,640]{1,0:T(8,128)(2,1)S(1)}, u32[]{:S(2)}, u32[]{:S(2)}) collective-permute-start(bf16[192,640]{1,0:T(8,128)(2,1)S(1)} %spatial_b.1.x0), channel_id=1, source_target_pairs={{0,32},{16,48},{32,64},{48,80},{64,96},{80,112},{96,128},{112,144}... | collective-permute-start | bytes 737288 | tf_op jit(solution)/shard_map/ppermute | solution.py:400
  46.9 11.5 %collective-permute-start.9 = (bf16[192,640]{1,0:T(8,128)(2,1)S(1)}, bf16[192,640]{1,0:T(8,128)(2,1)S(1)}, u32[]{:S(2)}, u32[]{:S(2)}) collective-permute-start(bf16[192,640]{1,0:T(8,128)(2,1)S(1)} %spatial_a.1.x1.y0), channel_id=1, source_target_pairs={{0,32},{16,48},{32,64},{48,80},{64,96},{80,112},{96,128},{112,144}... | collective-permute-start | bytes 737288 | tf_op jit(solution)/shard_map/ppermute | solution.py:400
  51.6 9.8 %collective-permute-start.11 = (bf16[192,640]{1,0:T(8,128)(2,1)S(1)}, bf16[192,640]{1,0:T(8,128)(2,1)S(1)}, u32[]{:S(2)}, u32[]{:S(2)}) collective-permute-start(bf16[192,640]{1,0:T(8,128)(2,1)S(1)} %get-tuple-element.40.mine), channel_id=1, source_target_pairs={{0,16},{16,0},{32,48},{48,32},{64,80},{80,64},{96,112},{112,96},{1... | collective-permute-start | bytes 737288 | tf_op jit(solution)/shard_map/ppermute | solution.py:394
  58.6 4.5 %collective-permute-start.10 = (bf16[192,640]{1,0:T(8,128)(2,1)S(1)}, bf16[192,640]{1,0:T(8,128)(2,1)S(1)}, u32[]{:S(2)}, u32[]{:S(2)}) collective-permute-start(bf16[192,640]{1,0:T(8,128)(2,1)S(1)} %temporal_last.1.x), channel_id=1, source_target_pairs={{0,16},{16,0},{32,48},{48,32},{64,80},{80,64},{96,112},{112,96},{1... | collective-permute-start | bytes 737288 | tf_op jit(solution)/shard_map/ppermute | solution.py:394

commit v8 on v7

--- a/solution.py
+++ b/solution.py
@@ -138,8 +138,14 @@
 def store_later_kernel(mine, other, out, rows, sems):
     @pl.when(core_index() == 1)
     def _():
-        unpack_rows(mine, out, rows, sems, 1)
-        unpack_rows(other, out, rows, sems, 0)
+        copies = []
+        for i, (x, at) in enumerate(((mine, 0), (mine, W), (other, 0), (other, W))):
+            rows[i] = x[:, at : at + W]
+            copy = pltpu.make_async_copy(rows.at[i], out.at[(2, 3, 0, 1)[i]], sems.at[i])
+            copy.start()
+            copies.append(copy)
+        for copy in copies:
+            copy.wait()
 
 
 def store_earlier_kernel(pair, x, part, out, rows, sems):
@@ -156,7 +162,7 @@
         jax.ShapeDtypeStruct((4, C, W), BF16),
         len(arrays) + len(part),
         "store",
-        scratch=[pltpu.VMEM((2, C, W), BF16), pltpu.SemaphoreType.DMA((2,))],
+        scratch=[pltpu.VMEM((4, C, W), BF16), pltpu.SemaphoreType.DMA((4,))],
         moved=500000,
         in_specs=[VMEM] * len(arrays) + [ANY] * len(part),
         out_specs=ANY,

time: 63.6 us -> 63.5 us (level)
  Pallas kernels: 20.8 us -> 20.1 us
    pallas_call x3, Pallas kernels: 1.65 us -> 1 us  [store(): call(kernel, jax.ShapeDtypeStruct((4, C, W), BF16), len(arrays) + len(par...]
  transfers between devices with their start and end apart: 12 -> 12, of which waited for: 5 -> 6; matrix products, arithmetic and copies ran while one was open for 0% -> 0% of each run, Pallas kernels for 30% -> 29%
where the time goes in v8:
time: 63.5 us; the launch traced here: 62.8 us
  starting transfers between devices  39.3 us (62%)
  Pallas kernels  20.1 us (32%)
  waiting for transfers between devices  3.04 us (5%)
    ppermute x5, starting transfers between devices, swap(): return lax.ppermute(x, 'frames', swaps)  20.2 us
    ppermute x4, starting transfers between devices, onward(): return lax.ppermute(x, 'frames', later)  11.3 us
    ppermute x3, starting transfers between devices, halo(): return lax.ppermute(x, ('frames', 'rows'), across)  7.8 us
    pallas_call x1, Pallas kernels, prepare(): call(weights_kernel, [shape((3 * C, 3 * C), BF16)] * 6 + [shape((C, LANES...  4.17 us
    pallas_call x1, Pallas kernels, on_device(): spatial(functools.partial(spatial_pick_kernel, 0), 8, 'spatial_a1')  2.7 us
    pallas_call x1, Pallas kernels, on_device(): inner_b = spatial(spatial_kernel, 7, 'spatial_b')(z_b, own_b, sib_b, *both)  2.58 us
    pallas_call x1, Pallas kernels, on_device(): inner_a = spatial(spatial_kernel, 7, 'spatial_a')(z_a, own_a, sib_a, *both)  2.58 us
    pallas_call x1, Pallas kernels, near(): call(functools.partial(near_pick_kernel, pick), [jax.ShapeDtypeStruct((C,...  2.3 us
  transfers between devices with their start and end apart: 12, of which 6 were waited for; matrix products, arithmetic and copies ran while one was open for 0% of the time, Pallas kernels for 29%

profile of v8, /device:TPU:25, one launch (start us, length us, event | category | flops | bytes accessed | tf_op | source)
XLA Modules:
  0.0 62.8 jit_solution(3401329952120937054)
XLA Ops:
  0.0 0.7 %collective-permute-start = (bf16[4,192,320]{2,1,0:T(8,128)(2,1)}, bf16[4,192,320]{2,1,0:T(8,128)(2,1)S(1)}, u32[]{:S(2)}, u32[]{:S(2)}) collective-permute-start(bf16[4,192,320]{2,1,0:T(8,128)(2,1)} %bitcast.6), channel_id=1, source_target_pairs={{0,16},{16,0},{32,48},{48,32},{64,80},{80,64},{96,112},{112,96},{1... | collective-permute-start | bytes 1474568 | tf_op jit(solution)/shard_map/ppermute | solution.py:400
  0.7 1.3 %pack.1.mine = bf16[2,192,640]{2,1,0:T(8,128)(2,1)S(1)} custom-call(bf16[4,192,320]{2,1,0:T(8,128)(2,1)} %bitcast.7), custom_call_target="tpu_custom_call" | custom-call | bytes 1000000 | tf_op jit(solution)/shard_map/pack/pallas_call | solution.py:410
  2.0 0.6 collective-permute-done.other
  2.5 0.2 join.1
  2.7 3.8 %collective-permute-start.1 = (bf16[2,192,640]{2,1,0:T(8,128)(2,1)S(1)}, bf16[2,192,640]{2,1,0:T(8,128)(2,1)S(1)}, u32[]{:S(2)}, u32[]{:S(2)}) collective-permute-start(bf16[2,192,640]{2,1,0:T(8,128)(2,1)S(1)} %get-tuple-element.25.owned), channel_id=1, source_target_pairs={{1,16},{2,17},{3,18},{4,19},{5,20},{6,21},{7,22},{8,23},{9,24},{10... | collective-permute-start | bytes 1474568 | tf_op jit(solution)/shard_map/ppermute | solution.py:403
  6.5 4.2 %weights.1 = (bf16[576,576]{1,0:T(8,128)(2,1)S(1)}, bf16[576,576]{1,0:T(8,128)(2,1)S(1)}, bf16[576,576]{1,0:T(8,128)(2,1)S(1)}, bf16[576,576]{1,0:T(8,128)(2,1)S...) custom-call(bf16[4,3,3,192,192]{4,3,2,1,0:T(8,128)(2,1)} %sw.1, ...), custom_call_target="tpu_custom_call" | custom-call | bytes 6000000 | tf_op jit(solution)/shard_map/weights/pallas_call | solution.py:87
  10.7 2.3 %near.1 = (f32[192,640]{1,0:T(8,128)S(1)}, f32[192,640]{1,0:T(8,128)S(1)}) custom-call(bf16[2,192,640]{2,1,0:T(8,128)(2,1)S(1)} %pack.1.mine, bf16[2,192,640]{2,1,0:T(8,128)(2,1)S(1)} %get-tuple-element.25.owned, bf16[192,640]{1,0:T(8,128)(2,1)S(1)} %get-tuple-element.26.sib_o, bf16[576,576]{1,0:T(8,128)(2,1)S(1)} %get-tuple-element.27.w1, ...), custom_call_target="tpu_custom_call" | custom-call | flops 424673280 | bytes 2000000 | tf_op jit(solution)/shard_map/near/pallas_call | solution.py:264
  13.0 0.3 collective-permute-done.1.z
  13.3 1.7 %far.1.x0 = bf16[192,640]{1,0:T(8,128)(2,1)S(1)} custom-call(bf16[2,192,640]{2,1,0:T(8,128)(2,1)S(1)} %collective-permute-done.1.z, f32[192,640]{1,0:T(8,128)S(1)} %get-tuple-element.31.part1, f32[192,640]{1,0:T(8,128)S(1)} %get-tuple-element.32.part2, bf16[576,576]{1,0:T(8,128)(2,1)S(1)} %get-tuple-element.27.w1, ...), custom_call_target="tpu_custom_call" | custom-call | flops 849346560 | bytes 4000000 | tf_op jit(solution)/shard_map/far/pallas_call | solution.py:293
  15.0 3.1 %collective-permute-start.2 = (bf16[192,640]{1,0:T(8,128)(2,1)S(1)}, bf16[192,640]{1,0:T(8,128)(2,1)S(1)}, u32[]{:S(2)}, u32[]{:S(2)}) collective-permute-start(bf16[192,640]{1,0:T(8,128)(2,1)S(1)} %far.1.x0), channel_id=1, source_target_pairs={{0,32},{16,48},{32,64},{48,80},{64,96},{80,112},{96,128},{112,144}... | collective-permute-start | bytes 737288 | tf_op jit(solution)/shard_map/ppermute | solution.py:406
  18.2 2.7 %spatial_a1.1.x1.x0 = bf16[192,640]{1,0:T(8,128)(2,1)S(1)} custom-call(bf16[2,192,640]{2,1,0:T(8,128)(2,1)S(1)} %collective-permute-done.1.z, bf16[2,192,640]{2,1,0:T(8,128)(2,1)S(1)} %pack.1.mine, bf16[2,192,640]{2,1,0:T(8,128)(2,1)S(1)} %get-tuple-element.25.owned, bf16[192,640]{1,0:T(8,128)(2,1)S(1)} %get-tuple-element.26.sib_o, ...), custom_call_target="tpu_custom_call" | custom-call | flops 1274019840 | bytes 4000000 | tf_op jit(solution)/shard_map/spatial_a1/pallas_call | solution.py:431
  20.9 3.1 %collective-permute-start.5 = (bf16[192,640]{1,0:T(8,128)(2,1)S(1)}, bf16[192,640]{1,0:T(8,128)(2,1)S(1)}, u32[]{:S(2)}, u32[]{:S(2)}) collective-permute-start(bf16[192,640]{1,0:T(8,128)(2,1)S(1)} %spatial_a1.1.x1.x0), channel_id=1, source_target_pairs={{0,32},{16,48},{32,64},{48,80},{64,96},{80,112},{96,128},{112,144}... | collective-permute-start | bytes 737288 | tf_op jit(solution)/shard_map/ppermute | solution.py:406
  24.0 0.1 collective-permute-done.2.x2.x1
  24.1 0.4 temporal.2.own
  24.5 7.4 %collective-permute-start.4 = (bf16[192,640]{1,0:T(8,128)(2,1)S(1)}, bf16[192,640]{1,0:T(8,128)(2,1)S(1)}, u32[]{:S(2)}, u32[]{:S(2)}) collective-permute-start(bf16[192,640]{1,0:T(8,128)(2,1)S(1)} %temporal.2.own), channel_id=1, source_target_pairs={{0,16},{16,0},{32,48},{48,32},{64,80},{80,64},{96,112},{112,96},{1... | collective-permute-start | bytes 737288 | tf_op jit(solution)/shard_map/ppermute | solution.py:400
  31.9 1.9 %collective-permute-start.3 = (bf16[192,640]{1,0:T(8,128)(2,1)S(1)}, bf16[192,640]{1,0:T(8,128)(2,1)S(1)}, u32[]{:S(2)}, u32[]{:S(2)}) collective-permute-start(bf16[192,640]{1,0:T(8,128)(2,1)S(1)} %temporal.2.own), channel_id=1, source_target_pairs={{1,16},{2,17},{3,18},{4,19},{5,20},{6,21},{7,22},{8,23},{9,24},{10... | collective-permute-start | bytes 737288 | tf_op jit(solution)/shard_map/ppermute | solution.py:403
  33.8 0.0 collective-permute-done.5.x2
  33.8 0.4 temporal.3.own
  34.2 2.6 %collective-permute-start.7 = (bf16[192,640]{1,0:T(8,128)(2,1)S(1)}, bf16[192,640]{1,0:T(8,128)(2,1)S(1)}, u32[]{:S(2)}, u32[]{:S(2)}) collective-permute-start(bf16[192,640]{1,0:T(8,128)(2,1)S(1)} %temporal.3.own), channel_id=1, source_target_pairs={{0,16},{16,0},{32,48},{48,32},{64,80},{80,64},{96,112},{112,96},{1... | collective-permute-start | bytes 737288 | tf_op jit(solution)/shard_map/ppermute | solution.py:400
  36.8 2.1 %collective-permute-start.6 = (bf16[192,640]{1,0:T(8,128)(2,1)S(1)}, bf16[192,640]{1,0:T(8,128)(2,1)S(1)}, u32[]{:S(2)}, u32[]{:S(2)}) collective-permute-start(bf16[192,640]{1,0:T(8,128)(2,1)S(1)} %temporal.3.own), channel_id=1, source_target_pairs={{1,16},{2,17},{3,18},{4,19},{5,20},{6,21},{7,22},{8,23},{9,24},{10... | collective-permute-start | bytes 737288 | tf_op jit(solution)/shard_map/ppermute | solution.py:403
  38.9 0.0 collective-permute-done.4.sib
  38.9 0.5 collective-permute-done.3.z
  39.4 2.6 %spatial_b.1.x0 = bf16[192,640]{1,0:T(8,128)(2,1)S(1)} custom-call(bf16[192,640]{1,0:T(8,128)(2,1)S(1)} %collective-permute-done.3.z, bf16[192,640]{1,0:T(8,128)(2,1)S(1)} %temporal.2.own, bf16[192,640]{1,0:T(8,128)(2,1)S(1)} %collective-permute-done.4.sib, bf16[576,576]{1,0:T(8,128)(2,1)S(1)} %get-tuple-element.35.rest_0_, ...), custom_call_target="tpu_custom_call" | custom-call | flops 1274019840 | bytes 4000000 | tf_op jit(solution)/shard_map/spatial_b/pallas_call | solution.py:439
  42.0 2.3 %collective-permute-start.8 = (bf16[192,640]{1,0:T(8,128)(2,1)S(1)}, bf16[192,640]{1,0:T(8,128)(2,1)S(1)}, u32[]{:S(2)}, u32[]{:S(2)}) collective-permute-start(bf16[192,640]{1,0:T(8,128)(2,1)S(1)} %spatial_b.1.x0), channel_id=1, source_target_pairs={{0,32},{16,48},{32,64},{48,80},{64,96},{80,112},{96,128},{112,144}... | collective-permute-start | bytes 737288 | tf_op jit(solution)/shard_map/ppermute | solution.py:406
  44.3 0.0 collective-permute-done.7.sib
  44.3 0.0 collective-permute-done.6.z
  44.3 2.6 %spatial_a.1.x1.y0 = bf16[192,640]{1,0:T(8,128)(2,1)S(1)} custom-call(bf16[192,640]{1,0:T(8,128)(2,1)S(1)} %collective-permute-done.6.z, bf16[192,640]{1,0:T(8,128)(2,1)S(1)} %temporal.3.own, bf16[192,640]{1,0:T(8,128)(2,1)S(1)} %collective-permute-done.7.sib, bf16[576,576]{1,0:T(8,128)(2,1)S(1)} %get-tuple-element.35.rest_0_, ...), custom_call_target="tpu_custom_call" | custom-call | flops 1274019840 | bytes 4000000 | tf_op jit(solution)/shard_map/spatial_a/pallas_call | solution.py:441
  46.9 2.7 %collective-permute-start.9 = (bf16[192,640]{1,0:T(8,128)(2,1)S(1)}, bf16[192,640]{1,0:T(8,128)(2,1)S(1)}, u32[]{:S(2)}, u32[]{:S(2)}) collective-permute-start(bf16[192,640]{1,0:T(8,128)(2,1)S(1)} %spatial_a.1.x1.y0), channel_id=1, source_target_pairs={{0,32},{16,48},{32,64},{48,80},{64,96},{80,112},{96,128},{112,144}... | collective-permute-start | bytes 737288 | tf_op jit(solution)/shard_map/ppermute | solution.py:406
  49.7 1.4 %collective-permute-done.8.x2 = bf16[192,640]{1,0:T(8,128)(2,1)S(1)} collective-permute-done((bf16[192,640]{1,0:T(8,128)(2,1)S(1)}, bf16[192,640]{1,0:T(8,128)(2,1)S(1)}, u32[]{:S(2)}, u32[]{:S(2)}) %collective-permute-start.8) | collective-permute-done | bytes 245792 | tf_op jit(solution)/shard_map/ppermute | solution.py:406
  51.0 0.6 temporal_late.1
  51.6 6.7 %collective-permute-start.11 = (bf16[192,640]{1,0:T(8,128)(2,1)S(1)}, bf16[192,640]{1,0:T(8,128)(2,1)S(1)}, u32[]{:S(2)}, u32[]{:S(2)}) collective-permute-start(bf16[192,640]{1,0:T(8,128)(2,1)S(1)} %get-tuple-element.40.mine), channel_id=1, source_target_pairs={{0,16},{16,0},{32,48},{48,32},{64,80},{80,64},{96,112},{112,96},{1... | collective-permute-start | bytes 737288 | tf_op jit(solution)/shard_map/ppermute | solution.py:400
  58.4 0.0 collective-permute-done.9.y2
  58.4 0.2 temporal_last.1.x
  58.6 2.8 %collective-permute-start.10 = (bf16[192,640]{1,0:T(8,128)(2,1)S(1)}, bf16[192,640]{1,0:T(8,128)(2,1)S(1)}, u32[]{:S(2)}, u32[]{:S(2)}) collective-permute-start(bf16[192,640]{1,0:T(8,128)(2,1)S(1)} %temporal_last.1.x), channel_id=1, source_target_pairs={{0,16},{16,0},{32,48},{48,32},{64,80},{80,64},{96,112},{112,96},{1... | collective-permute-start | bytes 737288 | tf_op jit(solution)/shard_map/ppermute | solution.py:400
  61.4 0.0 collective-permute-done.11.other
  61.4 0.9 %store.3.part = bf16[4,192,320]{2,1,0:T(8,128)(2,1)} custom-call(bf16[192,640]{1,0:T(8,128)(2,1)S(1)} %get-tuple-element.40.mine, bf16[192,640]{1,0:T(8,128)(2,1)S(1)} %collective-permute-done.11.other), custom_call_target="tpu_custom_call" | custom-call | bytes 500000 | tf_op jit(solution)/shard_map/store/pallas_call | solution.py:160
  62.4 0.1 store.4.part
  62.4 0.2 collective-permute-done.10.x
  (1 shorter events, 0.0 us)
Async XLA Ops:
  0.0 2.5 %collective-permute-start = (bf16[4,192,320]{2,1,0:T(8,128)(2,1)}, bf16[4,192,320]{2,1,0:T(8,128)(2,1)S(1)}, u32[]{:S(2)}, u32[]{:S(2)}) collective-permute-start(bf16[4,192,320]{2,1,0:T(8,128)(2,1)} %bitcast.6), channel_id=1, source_target_pairs={{0,16},{16,0},{32,48},{48,32},{64,80},{80,64},{96,112},{112,96},{1... | collective-permute-start | bytes 1474568 | tf_op jit(solution)/shard_map/ppermute | solution.py:400
  2.7 10.6 %collective-permute-start.1 = (bf16[2,192,640]{2,1,0:T(8,128)(2,1)S(1)}, bf16[2,192,640]{2,1,0:T(8,128)(2,1)S(1)}, u32[]{:S(2)}, u32[]{:S(2)}) collective-permute-start(bf16[2,192,640]{2,1,0:T(8,128)(2,1)S(1)} %get-tuple-element.25.owned), channel_id=1, source_target_pairs={{1,16},{2,17},{3,18},{4,19},{5,20},{6,21},{7,22},{8,23},{9,24},{10... | collective-permute-start | bytes 1474568 | tf_op jit(solution)/shard_map/ppermute | solution.py:403
  15.0 9.1 %collective-permute-start.2 = (bf16[192,640]{1,0:T(8,128)(2,1)S(1)}, bf16[192,640]{1,0:T(8,128)(2,1)S(1)}, u32[]{:S(2)}, u32[]{:S(2)}) collective-permute-start(bf16[192,640]{1,0:T(8,128)(2,1)S(1)} %far.1.x0), channel_id=1, source_target_pairs={{0,32},{16,48},{32,64},{48,80},{64,96},{80,112},{96,128},{112,144}... | collective-permute-start | bytes 737288 | tf_op jit(solution)/shard_map/ppermute | solution.py:406
  20.9 13.0 %collective-permute-start.5 = (bf16[192,640]{1,0:T(8,128)(2,1)S(1)}, bf16[192,640]{1,0:T(8,128)(2,1)S(1)}, u32[]{:S(2)}, u32[]{:S(2)}) collective-permute-start(bf16[192,640]{1,0:T(8,128)(2,1)S(1)} %spatial_a1.1.x1.x0), channel_id=1, source_target_pairs={{0,32},{16,48},{32,64},{48,80},{64,96},{80,112},{96,128},{112,144}... | collective-permute-start | bytes 737288 | tf_op jit(solution)/shard_map/ppermute | solution.py:406
  24.5 14.4 %collective-permute-start.4 = (bf16[192,640]{1,0:T(8,128)(2,1)S(1)}, bf16[192,640]{1,0:T(8,128)(2,1)S(1)}, u32[]{:S(2)}, u32[]{:S(2)}) collective-permute-start(bf16[192,640]{1,0:T(8,128)(2,1)S(1)} %temporal.2.own), channel_id=1, source_target_pairs={{0,16},{16,0},{32,48},{48,32},{64,80},{80,64},{96,112},{112,96},{1... | collective-permute-start | bytes 737288 | tf_op jit(solution)/shard_map/ppermute | solution.py:400
  31.9 7.5 %collective-permute-start.3 = (bf16[192,640]{1,0:T(8,128)(2,1)S(1)}, bf16[192,640]{1,0:T(8,128)(2,1)S(1)}, u32[]{:S(2)}, u32[]{:S(2)}) collective-permute-start(bf16[192,640]{1,0:T(8,128)(2,1)S(1)} %temporal.2.own), channel_id=1, source_target_pairs={{1,16},{2,17},{3,18},{4,19},{5,20},{6,21},{7,22},{8,23},{9,24},{10... | collective-permute-start | bytes 737288 | tf_op jit(solution)/shard_map/ppermute | solution.py:403
  34.2 10.0 %collective-permute-start.7 = (bf16[192,640]{1,0:T(8,128)(2,1)S(1)}, bf16[192,640]{1,0:T(8,128)(2,1)S(1)}, u32[]{:S(2)}, u32[]{:S(2)}) collective-permute-start(bf16[192,640]{1,0:T(8,128)(2,1)S(1)} %temporal.3.own), channel_id=1, source_target_pairs={{0,16},{16,0},{32,48},{48,32},{64,80},{80,64},{96,112},{112,96},{1... | collective-permute-start | bytes 737288 | tf_op jit(solution)/shard_map/ppermute | solution.py:400
  36.8 7.5 %collective-permute-start.6 = (bf16[192,640]{1,0:T(8,128)(2,1)S(1)}, bf16[192,640]{1,0:T(8,128)(2,1)S(1)}, u32[]{:S(2)}, u32[]{:S(2)}) collective-permute-start(bf16[192,640]{1,0:T(8,128)(2,1)S(1)} %temporal.3.own), channel_id=1, source_target_pairs={{1,16},{2,17},{3,18},{4,19},{5,20},{6,21},{7,22},{8,23},{9,24},{10... | collective-permute-start | bytes 737288 | tf_op jit(solution)/shard_map/ppermute | solution.py:403
  42.0 9.1 %collective-permute-start.8 = (bf16[192,640]{1,0:T(8,128)(2,1)S(1)}, bf16[192,640]{1,0:T(8,128)(2,1)S(1)}, u32[]{:S(2)}, u32[]{:S(2)}) collective-permute-start(bf16[192,640]{1,0:T(8,128)(2,1)S(1)} %spatial_b.1.x0), channel_id=1, source_target_pairs={{0,32},{16,48},{32,64},{48,80},{64,96},{80,112},{96,128},{112,144}... | collective-permute-start | bytes 737288 | tf_op jit(solution)/shard_map/ppermute | solution.py:406
  46.9 11.5 %collective-permute-start.9 = (bf16[192,640]{1,0:T(8,128)(2,1)S(1)}, bf16[192,640]{1,0:T(8,128)(2,1)S(1)}, u32[]{:S(2)}, u32[]{:S(2)}) collective-permute-start(bf16[192,640]{1,0:T(8,128)(2,1)S(1)} %spatial_a.1.x1.y0), channel_id=1, source_target_pairs={{0,32},{16,48},{32,64},{48,80},{64,96},{80,112},{96,128},{112,144}... | collective-permute-start | bytes 737288 | tf_op jit(solution)/shard_map/ppermute | solution.py:406
  51.6 9.8 %collective-permute-start.11 = (bf16[192,640]{1,0:T(8,128)(2,1)S(1)}, bf16[192,640]{1,0:T(8,128)(2,1)S(1)}, u32[]{:S(2)}, u32[]{:S(2)}) collective-permute-start(bf16[192,640]{1,0:T(8,128)(2,1)S(1)} %get-tuple-element.40.mine), channel_id=1, source_target_pairs={{0,16},{16,0},{32,48},{48,32},{64,80},{80,64},{96,112},{112,96},{1... | collective-permute-start | bytes 737288 | tf_op jit(solution)/shard_map/ppermute | solution.py:400
  58.6 4.0 %collective-permute-start.10 = (bf16[192,640]{1,0:T(8,128)(2,1)S(1)}, bf16[192,640]{1,0:T(8,128)(2,1)S(1)}, u32[]{:S(2)}, u32[]{:S(2)}) collective-permute-start(bf16[192,640]{1,0:T(8,128)(2,1)S(1)} %temporal_last.1.x), channel_id=1, source_target_pairs={{0,16},{16,0},{32,48},{48,32},{64,80},{80,64},{96,112},{112,96},{1... | collective-permute-start | bytes 737288 | tf_op jit(solution)/shard_map/ppermute | solution.py:400
